TPU v7x, 512 devices: a whole 4x4x16 slice. The times are simulated.
512 devices in a mesh: dp: 16 (over z_hi, x, core), seq: 32 (over z_lo, y).
Axes of the slice: x: 4, y: 4, z: 16 (z_hi: 2, z_lo: 8; z = z_hi * 8 + z_lo), core: 2. Of those that a mesh axis runs over, the one named last changes fastest.
Arguments:
- grad_out: bfloat16 [16, 64, 32768], P('dp', None, 'seq'), may hold values from -6 to 6
- gate: bfloat16 [16, 64, 32768], P('dp', None, 'seq'), may hold values from -6 to 6
- input_spectrum: float32 [16, 2, 64, 32768], P('dp', None, None, 'seq'), may hold values from -6 to 6
- filter_spectrum: float32 [2, 64, 32768], P(None, 'dp', 'seq'), may hold values from -6 to 6
Outputs:
- grad_input: bfloat16 [16, 64, 32768], P('dp', None, 'seq')
- grad_gate: bfloat16 [16, 64, 32768], P('dp', None, 'seq')
- grad_filter: float32 [2, 64, 32768], P(None, 'dp', 'seq')
All inputs are finite; a program needn't handle non-finite values.
Results may differ from a plain program's by a relative error of at most 0.002.
Values sent between devices are 32-bit elements; how exact they have to be, the bound alone decides.
No kernel may reach another device: no remote copies, remote signals or barrier semaphores. Data moves between devices by JAX's collectives and lax.ppermute only.
A program may use at most 64 MiB of HBM per device.

v0:
```python
import functools
import math

import jax
import jax.numpy as jnp
import numpy as np
from jax import lax
from jax.experimental import pallas as pl
from jax.experimental.pallas import tpu as pltpu
from jax.sharding import Mesh, PartitionSpec as P


f32 = jnp.float32
bf16 = jnp.bfloat16
SEQ = ("zlo", "y")
DP = ("zhi", "x", "core")
MIB = 1024 * 1024


def unit_roots(rows, columns, period):
    product = np.outer(np.arange(rows, dtype=np.int64), np.arange(columns, dtype=np.int64))
    angle = (product % period).astype(np.float64) * (2.0 * np.pi / period)
    return np.cos(angle).astype(np.float32), np.sin(angle).astype(np.float32)


def halves(values):
    high = values.astype(bf16)
    return high, (values - high.astype(f32)).astype(bf16)


def three_terms(values, axis):
    high, low = halves(values)
    return jnp.concatenate([high, low, high], axis=axis)


def small_table(points, inverse):
    cosine, sine = unit_roots(points, points, points)
    whole = np.concatenate([cosine, -sine], axis=1 if inverse else 0)
    high = whole.astype(bf16)
    low = (whole - high.astype(np.float32)).astype(bf16)
    return jnp.asarray(np.concatenate([high, high, low], axis=1))


def dot16(left, right):
    return jnp.dot(left, right, preferred_element_type=f32)


def tables_kernel(coarse_ref, fine_ref, cos_hi, cos_lo, sin_hi, sin_lo):
    steps = fine_ref.shape[1]

    @pl.loop(0, coarse_ref.shape[1])
    def _(a):
        at = pl.ds(pl.multiple_of(a * steps, steps), steps)
        coarse_cos, coarse_sin = coarse_ref[0, pl.ds(a, 1), :], coarse_ref[1, pl.ds(a, 1), :]
        fine_cos, fine_sin = fine_ref[0], fine_ref[1]
        cosine = coarse_cos * fine_cos - coarse_sin * fine_sin
        sine = coarse_sin * fine_cos + coarse_cos * fine_sin
        cos_hi[at, :], cos_lo[at, :] = halves(cosine)
        sin_hi[at, :], sin_lo[at, :] = halves(sine)


def root_tables(points):
    steps, columns = 32, points // 4
    coarse = jnp.asarray(np.stack(unit_roots(points // steps, columns, points // steps)))
    fine = jnp.asarray(np.stack(unit_roots(steps, columns, points)))
    return pl.pallas_call(
        tables_kernel,
        out_shape=[jax.ShapeDtypeStruct((points, columns), bf16)] * 4,
        name="root_tables",
        compiler_params=pltpu.CompilerParams(vmem_limit_bytes=16 * MIB),
        cost_estimate=pl.CostEstimate(
            flops=20 * points * columns, bytes_accessed=8 * points * columns, transcendentals=0
        ),
    )(coarse, fine)


def keep_quarters(rows_ref, place, count, real, imag, conjugate):
    rows, points = real.shape
    lane = lax.broadcasted_iota(jnp.int32, (1, points), 1)
    odd = lane % 2 == 1
    alternate = jnp.where(odd, -1.0, 1.0)
    early = jnp.where(lane % 4 < 2, 1.0, -1.0)
    outer = jnp.where((lane + 1) % 4 < 2, 1.0, -1.0)
    swap_real, swap_imag = jnp.where(odd, imag, real), jnp.where(odd, real, imag)
    turned = [
        (real, imag),
        (swap_real * outer, swap_imag * early),
        (real * alternate, imag * alternate),
        (swap_real * early, swap_imag * outer),
    ]
    if conjugate:
        turned[1], turned[3] = turned[3], turned[1]
    for m in range(4):
        for part, values in enumerate(turned[m]):
            high, low = halves(values)
            first = (part * count + place) * rows
            rows_ref[m, first : first + rows, :] = high
            rows_ref[m, 2 * count * rows + first : 2 * count * rows + first + rows, :] = low


def root_product(high_low, hi_ref, lo_ref):
    rows = high_low.shape[0] // 2
    both = dot16(high_low, hi_ref[...])
    return both[:rows] + both[rows:] + dot16(high_low[:rows], lo_ref[...])


def forward_kernel(
    moved_ref, small_ref, twiddle_ref, cos_hi, cos_lo, sin_hi, sin_lo, spec_ref, terms_ref, rows_ref
):
    classes = moved_ref.shape[0]
    points = cos_hi.shape[0]
    scale = 1.0 / math.sqrt(classes * points)
    tw_cos, tw_sin = twiddle_ref[0] * scale, twiddle_ref[1] * scale
    for channel in range(2):
        delta = moved_ref[:, (4 + channel) * points : (5 + channel) * points]
        part = dot16(small_ref[...], three_terms(delta, 0))
        part_real, part_imag = part[:classes], part[classes:]
        turned_real = part_real * tw_cos + part_imag * tw_sin
        turned_imag = part_imag * tw_cos - part_real * tw_sin
        keep_quarters(rows_ref, channel, 2, turned_real, turned_imag, True)
    half = 2 * classes
    width = points // 4
    for tile in range(4):
        at = slice(tile * width, (tile + 1) * width)
        by_cos = root_product(rows_ref[tile], cos_hi, cos_lo)
        by_sin = root_product(rows_ref[tile], sin_hi, sin_lo)
        real = by_cos[:half] + by_sin[half:]
        imag = by_cos[half:] - by_sin[:half]
        for channel in range(2):
            mine = slice(channel * classes, (channel + 1) * classes)
            put_real = slice(channel * points + at.start, channel * points + at.stop)
            put_imag = slice((2 + channel) * points + at.start, (2 + channel) * points + at.stop)
            in_real, in_imag = moved_ref[:, put_real], moved_ref[:, put_imag]
            spec_ref[:, put_real] = real[mine]
            spec_ref[:, put_imag] = imag[mine]
            terms_ref[:, put_real] = in_real * real[mine] + in_imag * imag[mine]
            terms_ref[:, put_imag] = in_real * imag[mine] - in_imag * real[mine]


def inverse_kernel(
    sign, first_ref, filt_ref, small_ref, twiddle_ref, cos_hi, cos_lo, sin_hi, sin_lo, out_ref,
    rows_ref,
):
    classes = first_ref.shape[0]
    points = cos_hi.shape[0]

    for channel in range(2):
        real_at = slice(channel * points, (channel + 1) * points)
        imag_at = slice((2 + channel) * points, (3 + channel) * points)
        filt_real, filt_imag = filt_ref[:, real_at], filt_ref[:, imag_at] * sign
        first_real, first_imag = first_ref[:, real_at], first_ref[:, imag_at]
        keep_quarters(
            rows_ref,
            channel,
            2,
            first_real * filt_real - first_imag * filt_imag,
            first_real * filt_imag + first_imag * filt_real,
            False,
        )
    half = 2 * classes
    width = points // 4
    for tile in range(4):
        at = slice(tile * width, (tile + 1) * width)
        by_cos = root_product(rows_ref[tile], cos_hi, cos_lo)
        by_sin = root_product(rows_ref[tile], sin_hi, sin_lo)
        real = by_cos[:half] - by_sin[half:]
        imag = by_cos[half:] + by_sin[:half]
        tw_cos, tw_sin = twiddle_ref[0, :, at], twiddle_ref[1, :, at]
        for channel in range(2):
            mine = slice(channel * classes, (channel + 1) * classes)
            turned = jnp.concatenate(
                [
                    real[mine] * tw_cos - imag[mine] * tw_sin,
                    imag[mine] * tw_cos + real[mine] * tw_sin,
                ],
                axis=0,
            )
            out_ref[:, channel * points + at.start : channel * points + at.stop] = dot16(
                small_ref[...], three_terms(turned, 0)
            )


def staging_pairs(x_count, core_count, seq_count):
    per_core, per_x = seq_count // core_count, seq_count // (core_count * x_count)
    pairs = []
    for number in range(2):
        found = []
        for d in range(2 * x_count * core_count):
            for s in range(seq_count):
                core, x, zhi = s // per_core, s % per_core // per_x, s % per_x // 2
                row = (zhi * x_count + x) * core_count + core
                found.append((d * seq_count + s, row * seq_count + 2 * d + ((s % 2) ^ number)))
        pairs.append(found)
    return pairs


def halving(values, upper, axis, pairs):
    rows = values.shape[0] // 2
    kept = jnp.where(upper, values[rows:], values[:rows])
    away = jnp.where(upper, values[:rows], values[rows:])
    return kept + lax.ppermute(away, axis, pairs)


def step(grad_out, gate, input_spectrum, filter_spectrum):
    _, channels, positions = grad_out.shape
    seq_count = lax.axis_size(SEQ)
    x_count = lax.axis_size("x")
    everyone = DP + SEQ
    odd = lax.axis_index(SEQ) % 2 == 1
    upper_zhi = lax.axis_index("zhi") == 1
    upper_core = lax.axis_index("core") == 1
    x_index = lax.axis_index("x")
    pairs = staging_pairs(x_count, 2, seq_count)
    per_seq = channels // seq_count

    upstream = grad_out.astype(f32)
    delta = (upstream * gate.astype(f32)).reshape(seq_count, per_seq * positions)
    spectrum = (
        input_spectrum.reshape(2, seq_count, per_seq, positions)
        .transpose(1, 0, 2, 3)
        .reshape(seq_count, 2 * per_seq * positions)
    )
    moved = lax.all_to_all(
        jnp.concatenate([spectrum, delta], axis=1), SEQ, split_axis=0, concat_axis=0, tiled=True
    )

    low_half, high_half = filter_spectrum[:, :2], filter_spectrum[:, 2:]
    sent = [jnp.where(odd, high_half, low_half), jnp.where(odd, low_half, high_half)]
    got = [
        lax.ppermute(sent[number], everyone, pairs[number]).reshape(1, 4 * positions)
        for number in range(2)
    ]
    pair = jnp.concatenate(
        [jnp.where(odd, got[1], got[0]), jnp.where(odd, got[0], got[1])], axis=0
    )
    other = lax.ppermute(pair, "zhi", [(0, 1), (1, 0)])
    four = jnp.concatenate(
        [jnp.where(upper_zhi, other, pair), jnp.where(upper_zhi, pair, other)], axis=0
    )
    filters = lax.all_gather(four, ("core", "x"), axis=0, tiled=True)

    tables = root_tables(positions)
    small_out = small_table(seq_count, False)
    small_back = small_table(seq_count, True)
    twiddle = jnp.asarray(np.stack(unit_roots(seq_count, positions, seq_count * positions)))

    wide = jax.ShapeDtypeStruct((seq_count, 4 * positions), f32)
    signal = jax.ShapeDtypeStruct((seq_count, 2 * positions), f32)
    rows = [pltpu.VMEM((4, 8 * seq_count, positions), bf16)]
    params = pltpu.CompilerParams(vmem_limit_bytes=16 * MIB)
    cost = pl.CostEstimate(flops=2 * 10**9, bytes_accessed=10**7, transcendentals=0)
    spec, terms = pl.pallas_call(
        forward_kernel,
        out_shape=[wide, wide],
        scratch_shapes=rows,
        name="forward",
        compiler_params=params,
        cost_estimate=cost,
    )(moved, small_out, twiddle, *tables)

    def inverse(sign, first):
        return pl.pallas_call(
            functools.partial(inverse_kernel, sign),
            out_shape=signal,
            scratch_shapes=rows,
            name="inverse",
            compiler_params=params,
            cost_estimate=cost,
        )(first, filters, small_back, twiddle, *tables)

    total = halving(terms, upper_core, "core", [(0, 1), (1, 0)])
    total = halving(total, x_index >= 2, "x", [(x, x ^ 2) for x in range(x_count)])
    total = halving(total, x_index % 2 == 1, "x", [(x, x ^ 1) for x in range(x_count)])
    total = halving(total, upper_zhi, "zhi", [(0, 1), (1, 0)])

    conv = inverse(1.0, moved)
    back = inverse(-1.0, spec)
    returned = lax.all_to_all(
        jnp.concatenate([conv, back], axis=1), SEQ, split_axis=0, concat_axis=0, tiled=True
    )

    pieces = [total[0], total[1]]
    pieces = [jnp.where(odd, pieces[1 - n], pieces[n]) for n in range(2)]
    ends = [
        lax.ppermute(pieces[number], everyone, [(b, a) for a, b in pairs[number]]).reshape(
            2, per_seq, positions
        )
        for number in range(2)
    ]
    grad_filter = jnp.concatenate(
        [jnp.where(odd, ends[1], ends[0]), jnp.where(odd, ends[0], ends[1])], axis=1
    )

    scale = 1.0 / math.sqrt(seq_count * positions)
    conv = returned[:, : per_seq * positions].reshape(1, channels, positions) * scale
    backward = returned[:, per_seq * positions :].reshape(1, channels, positions) * scale
    grad_gate = (upstream * conv).astype(bf16)
    return (backward.astype(bf16), grad_gate, grad_filter)


def solution(mesh):
    split = Mesh(mesh.devices.reshape(2, 4, 2, 8, 4), DP + SEQ)
    return jax.shard_map(
        step,
        mesh=split,
        in_specs=(P(DP, None, SEQ), P(DP, None, SEQ), P(DP, None, None, SEQ), P(None, DP, SEQ)),
        out_specs=(P(DP, None, SEQ), P(DP, None, SEQ), P(None, DP, SEQ)),
        check_vma=False,
    )
```

profile of v0, /device:TPU:30, one launch (start us, length us, event | category | flops | bytes accessed | tf_op | source)
XLA Modules:
  0.0 180.6 jit_solution(16466985008160290630)
XLA Ops:
  0.6 1.3 reshape.110
  2.0 0.1 copy.22
  2.0 0.0 copy-start.10
  2.1 0.0 copy-start.11
  2.1 0.5 reshape.111
  2.5 0.4 copy-done.10
  3.0 0.1 copy-done.11
  3.1 0.1 reshape.112
  3.1 0.1 pad_maximum_fusion
  3.2 1.5 all_to_all.15
  4.7 15.6 %all-to-all-start = ((f32[32,1,6144]{2,1,0:T(1,128)}), f32[32,1,6144]{2,1,0:T(1,128)}, u32[]{:S(2)}, u32[]{:S(2)}) async-start(f32[32,1,6144]{2,1,0:T(1,128)} %all_to_all.15), calls=%async_computation | async-start | bytes 1572864 | tf_op jit(solution)/shard_map/all_to_all | solution.py:223
  20.3 0.0 copy-start.14
  20.3 0.7 copy-done.14
  21.0 8.1 %collective-permute-start = (f32[2,2,1024]{2,1,0:T(2,128)S(1)}, f32[2,2,1024]{2,1,0:T(2,128)S(1)}, u32[]{:S(2)}, u32[]{:S(2)}) collective-permute-start(f32[2,2,1024]{2,1,0:T(2,128)S(1)} %get-tuple-element.25), channel_id=1, source_target_pairs={{0,1},{1,0},{2,257},{3,256},{4,65},{5,64},{6,321},{7,320},{8,129},... | collective-permute-start | bytes 49160 | tf_op jit(solution)/shard_map/ppermute | solution.py:230
  29.2 9.4 %collective-permute-start.1 = (f32[2,2,1024]{2,1,0:T(2,128)S(1)}, f32[2,2,1024]{2,1,0:T(2,128)S(1)}, u32[]{:S(2)}, u32[]{:S(2)}) collective-permute-start(f32[2,2,1024]{2,1,0:T(2,128)S(1)} %get-tuple-element.26), channel_id=1, source_target_pairs={{0,0},{1,1},{2,256},{3,257},{4,64},{5,65},{6,320},{7,321},{8,128},... | collective-permute-start | bytes 49160 | tf_op jit(solution)/shard_map/ppermute | solution.py:230
  38.6 1.1 collective-permute-done
  39.7 1.5 collective-permute-done.1
  41.3 0.0 copy-start
  41.3 0.0 copy-start.1
  41.4 28.8 %collective-permute-start.2 = (f32[2,4096]{1,0:T(2,128)S(1)}, f32[2,4096]{1,0:T(2,128)S(1)}, u32[]{:S(2)}, u32[]{:S(2)}) collective-permute-start(f32[2,4096]{1,0:T(2,128)S(1)} %pad_maximum_fusion.1), channel_id=1, source_target_pairs={{0,256},{256,0},{1,257},{257,1},{2,258},{258,2},{3,259},{259,3},{4... | collective-permute-start | bytes 98312 | tf_op jit(solution)/shard_map/ppermute | solution.py:236
  70.2 0.0 copy-done
  70.2 0.0 copy-done.1
  70.2 0.6 root_tables.1
  70.9 0.0 copy-start.2
  70.9 1.2 collective-permute-done.2
  72.1 0.7 broadcast_select_fusion.4
  72.8 0.0 all-to-all-done
  72.8 1.4 copy.20
  74.2 0.0 copy-done.2
  74.2 0.0 copy-done.7
  74.2 0.0 copy-done.4
  74.2 2.0 %forward.1 = (f32[32,4096]{1,0:T(8,128)S(1)}, f32[32,4096]{1,0:T(8,128)S(1)}) custom-call(f32[32,6144]{1,0:T(8,128)S(1)} %bitcast.17, bf16[64,96]{1,0:T(8,128)(2,1)S(1)} %copy-done.7, f32[2,32,1024]{2,1,0:T(8,128)S(1)} %copy-done.4, bf16[1024,256]{1,0:T(8,128)(2,1)S(1)} %get-tuple-element.9.cos_hi, bf16[1024,256]{1,0:T(8,128)(2,1)S(1)} %get-tuple-element.10.cos_lo, ...), custom_call_target="tpu_custom_call" | custom-call | flops 2000000000 | bytes 10000000 | tf_op jit(solution)/shard_map/forward/pallas_call | solution.py:252
  76.2 0.0 copy-start.8
  76.3 0.0 copy-start.12
  76.3 0.0 copy-start.13
  76.3 0.7 slice_select_fusion
  77.0 1.9 %collective-permute-start.3 = (f32[16,4096]{1,0:T(8,128)}, f32[16,4096]{1,0:T(8,128)}, u32[]{:S(2)}, u32[]{:S(2)}) collective-permute-start(f32[16,4096]{1,0:T(8,128)} %slice_select_fusion), channel_id=1, source_target_pairs={{0,32},{32,0},{1,33},{33,1},{2,34},{34,2},{3,35},{35,3},{4,36},{36... | collective-permute-start | bytes 786440 | tf_op jit(solution)/shard_map/ppermute | solution.py:201
  78.9 0.0 copy-done.12
  79.0 29.2 %all-gather = f32[8,4,4096]{2,1,0:T(4,128)} all-gather(f32[1,4,4096]{2,1,0:T(4,128)S(1)} %maximum_bitcast_fusion.1), channel_id=1, replica_groups=mesh['zhi'=2,'x'=4,'core'=2,'zlo'=8,'y'=4] {'core','x'}, dimensions={0}, use_global_device_ids=true | all-gather | bytes 589824 | tf_op jit(solution)/shard_map/all_gather | solution.py:240
  108.2 1.2 reshape.114.filt_ref
  109.4 0.0 collective-permute-done.3
  109.4 1.0 select_add_fusion
  110.5 0.0 copy-start.5
  110.5 0.0 copy-start.6
  110.5 3.7 %collective-permute-start.4 = (f32[8,4096]{1,0:T(8,128)S(1)}, f32[8,4096]{1,0:T(8,128)S(1)}, u32[]{:S(2)}, u32[]{:S(2)}) collective-permute-start(f32[8,4096]{1,0:T(8,128)S(1)} %slice_select_fusion.1), channel_id=1, source_target_pairs={{0,128},{64,192},{128,0},{192,64},{1,129},{65,193},{129,1},{193,65... | collective-permute-start | bytes 393224 | tf_op jit(solution)/shard_map/ppermute | solution.py:201
  114.3 3.9 %inverse.2 = f32[32,2048]{1,0:T(8,128)S(1)} custom-call(f32[32,6144]{1,0:T(8,128)S(1)} %bitcast.18, f32[32,4096]{1,0:T(8,128)S(1)} %reshape.114.filt_ref, bf16[32,192]{1,0:T(8,128)(2,1)S(1)} %copy-done.6, f32[2,32,1024]{2,1,0:T(8,128)S(1)} %copy-done.5, bf16[1024,256]{1,0:T(8,128)(2,1)S(1)} %get-tuple-element.9.cos_hi, ...), custom_call_target="tpu_custom_call" | custom-call | flops 2000000000 | bytes 10000000 | tf_op jit(solution)/shard_map/inverse/pallas_call | solution.py:262
  118.2 1.3 collective-permute-done.4
  119.6 1.9 %collective-permute-start.5 = (f32[4,4096]{1,0:T(4,128)S(1)}, f32[4,4096]{1,0:T(4,128)S(1)}, u32[]{:S(2)}, u32[]{:S(2)}) collective-permute-start(f32[4,4096]{1,0:T(4,128)S(1)} %slice_select_fusion.2), channel_id=1, source_target_pairs={{0,64},{64,0},{128,192},{192,128},{1,65},{65,1},{129,193},{193,129... | collective-permute-start | bytes 196616 | tf_op jit(solution)/shard_map/ppermute | solution.py:201
  121.5 0.0 copy-done.9
  121.6 3.9 %inverse.3 = f32[32,2048]{1,0:T(8,128)S(1)} custom-call(f32[32,4096]{1,0:T(8,128)S(1)} %copy-done.9, f32[32,4096]{1,0:T(8,128)S(1)} %reshape.114.filt_ref, bf16[32,192]{1,0:T(8,128)(2,1)S(1)} %copy-done.6, f32[2,32,1024]{2,1,0:T(8,128)S(1)} %copy-done.5, bf16[1024,256]{1,0:T(8,128)(2,1)S(1)} %get-tuple-element.9.cos_hi, ...), custom_call_target="tpu_custom_call" | custom-call | flops 2000000000 | bytes 10000000 | tf_op jit(solution)/shard_map/inverse/pallas_call | solution.py:262
  125.5 0.3 collective-permute-done.5
  125.8 8.8 %collective-permute-start.6 = (f32[2,4096]{1,0:T(2,128)S(1)}, f32[2,4096]{1,0:T(2,128)S(1)}, u32[]{:S(2)}, u32[]{:S(2)}) collective-permute-start(f32[2,4096]{1,0:T(2,128)S(1)} %broadcast_select_fusion.2), channel_id=1, source_target_pairs={{0,256},{256,0},{1,257},{257,1},{2,258},{258,2},{3,259},{259,3},{4... | collective-permute-start | bytes 98312 | tf_op jit(solution)/shard_map/ppermute | solution.py:201
  134.7 1.3 copy.14
  136.0 9.0 %all-to-all-start.1 = ((f32[32,1,4096]{2,1,0:T(1,128)}), f32[32,1,4096]{2,1,0:T(1,128)S(1)}, u32[]{:S(2)}, u32[]{:S(2)}) async-start(f32[32,1,4096]{2,1,0:T(1,128)} %copy.14), calls=%async_computation.1 | async-start | bytes 1048576 | tf_op jit(solution)/shard_map/all_to_all | solution.py:278
  145.1 0.0 collective-permute-done.6
  145.1 3.9 %collective-permute-start.7 = (f32[4096]{0:T(1024)S(1)}, f32[4096]{0:T(1024)S(1)}, u32[]{:S(2)}, u32[]{:S(2)}) collective-permute-start(f32[4096]{0:T(1024)S(1)} %bitcast.22), channel_id=1, source_target_pairs={{1,0},{0,1},{257,2},{256,3},{65,4},{64,5},{321,6},{320,7},{129,8},... | collective-permute-start | bytes 49160 | tf_op jit(solution)/shard_map/ppermute | solution.py:285
  149.1 8.6 %collective-permute-start.8 = (f32[4096]{0:T(1024)S(1)}, f32[4096]{0:T(1024)S(1)}, u32[]{:S(2)}, u32[]{:S(2)}) collective-permute-start(f32[4096]{0:T(1024)S(1)} %bitcast.21), channel_id=1, source_target_pairs={{0,0},{1,1},{256,2},{257,3},{64,4},{65,5},{320,6},{321,7},{128,8},... | collective-permute-start | bytes 49160 | tf_op jit(solution)/shard_map/ppermute | solution.py:285
  157.6 19.2 %collective-permute-done.7 = f32[4096]{0:T(1024)S(1)} collective-permute-done((f32[4096]{0:T(1024)S(1)}, f32[4096]{0:T(1024)S(1)}, u32[]{:S(2)}, u32[]{:S(2)}) %collective-permute-start.7) | collective-permute-done | bytes 16416 | tf_op jit(solution)/shard_map/ppermute | solution.py:285
  176.8 1.2 collective-permute-done.8
  178.1 0.6 pad_maximum_fusion.2
  178.8 0.0 all-to-all-done.1
  178.8 0.3 copy.21
  179.2 0.7 fusion
  179.9 0.7 convert_element_type.26
  (29 shorter events, 0.5 us)
Async XLA Ops:
  2.0 0.9 copy-start.10
  2.1 1.0 copy-start.11
  4.7 68.1 %all-to-all-start = ((f32[32,1,6144]{2,1,0:T(1,128)}), f32[32,1,6144]{2,1,0:T(1,128)}, u32[]{:S(2)}, u32[]{:S(2)}) async-start(f32[32,1,6144]{2,1,0:T(1,128)} %all_to_all.15), calls=%async_computation | async-start | bytes 1572864 | tf_op jit(solution)/shard_map/all_to_all | solution.py:223
  20.3 0.8 copy-start.14
  21.0 18.7 %collective-permute-start = (f32[2,2,1024]{2,1,0:T(2,128)S(1)}, f32[2,2,1024]{2,1,0:T(2,128)S(1)}, u32[]{:S(2)}, u32[]{:S(2)}) collective-permute-start(f32[2,2,1024]{2,1,0:T(2,128)S(1)} %get-tuple-element.25), channel_id=1, source_target_pairs={{0,1},{1,0},{2,257},{3,256},{4,65},{5,64},{6,321},{7,320},{8,129},... | collective-permute-start | bytes 49160 | tf_op jit(solution)/shard_map/ppermute | solution.py:230
  29.2 12.1 %collective-permute-start.1 = (f32[2,2,1024]{2,1,0:T(2,128)S(1)}, f32[2,2,1024]{2,1,0:T(2,128)S(1)}, u32[]{:S(2)}, u32[]{:S(2)}) collective-permute-start(f32[2,2,1024]{2,1,0:T(2,128)S(1)} %get-tuple-element.26), channel_id=1, source_target_pairs={{0,0},{1,1},{2,256},{3,257},{4,64},{5,65},{6,320},{7,321},{8,128},... | collective-permute-start | bytes 49160 | tf_op jit(solution)/shard_map/ppermute | solution.py:230
  41.3 28.9 %copy-start = (f32[2,32,256]{2,1,0:T(8,128)S(1)}, f32[2,32,256]{2,1,0:T(8,128)}, u32[]{:S(2)}) copy-start(f32[2,32,256]{2,1,0:T(8,128)} %constant.55.clone.coarse_ref) | copy-start | bytes 196612
  41.3 28.9 %copy-start.1 = (f32[2,32,256]{2,1,0:T(8,128)S(1)}, f32[2,32,256]{2,1,0:T(8,128)}, u32[]{:S(2)}) copy-start(f32[2,32,256]{2,1,0:T(8,128)} %constant.56.clone.fine_ref) | copy-start | bytes 196612
  41.4 30.7 %collective-permute-start.2 = (f32[2,4096]{1,0:T(2,128)S(1)}, f32[2,4096]{1,0:T(2,128)S(1)}, u32[]{:S(2)}, u32[]{:S(2)}) collective-permute-start(f32[2,4096]{1,0:T(2,128)S(1)} %pad_maximum_fusion.1), channel_id=1, source_target_pairs={{0,256},{256,0},{1,257},{257,1},{2,258},{258,2},{3,259},{259,3},{4... | collective-permute-start | bytes 98312 | tf_op jit(solution)/shard_map/ppermute | solution.py:236
  70.9 3.3 %copy-start.2 = (bf16[1024,256]{1,0:T(8,128)(2,1)}, bf16[1024,256]{1,0:T(8,128)(2,1)S(1)}, u32[]{:S(2)}) copy-start(bf16[1024,256]{1,0:T(8,128)(2,1)S(1)} %get-tuple-element.12.sin_lo) | copy-start | bytes 1572868
  72.8 1.4 copy-start.7
  72.8 1.4 copy-start.4
  76.2 2.8 %copy-start.8 = (f32[32,4096]{1,0:T(8,128)}, f32[32,4096]{1,0:T(8,128)S(1)}, u32[]{:S(2)}) copy-start(f32[32,4096]{1,0:T(8,128)S(1)} %get-tuple-element.13.first_ref) | copy-start | bytes 1572868
  76.3 2.7 %copy-start.12 = (f32[2,4096]{1,0:T(2,128)S(1)}, f32[2,4096]{1,0:T(2,128)}, u32[]{:S(2)}) copy-start(f32[2,4096]{1,0:T(2,128)} %get-tuple-element.17) | copy-start | bytes 98308
  76.3 2.7 %copy-start.13 = (f32[2,4096]{1,0:T(2,128)S(1)}, f32[2,4096]{1,0:T(2,128)}, u32[]{:S(2)}) copy-start(f32[2,4096]{1,0:T(2,128)} %get-tuple-element.18) | copy-start | bytes 98308
  77.0 32.4 %collective-permute-start.3 = (f32[16,4096]{1,0:T(8,128)}, f32[16,4096]{1,0:T(8,128)}, u32[]{:S(2)}, u32[]{:S(2)}) collective-permute-start(f32[16,4096]{1,0:T(8,128)} %slice_select_fusion), channel_id=1, source_target_pairs={{0,32},{32,0},{1,33},{33,1},{2,34},{34,2},{3,35},{35,3},{4,36},{36... | collective-permute-start | bytes 786440 | tf_op jit(solution)/shard_map/ppermute | solution.py:201
  109.4 4.9 %copy-start.3 = (bf16[1024,256]{1,0:T(8,128)(2,1)S(1)}, bf16[1024,256]{1,0:T(8,128)(2,1)}, u32[]{:S(2)}) copy-start(bf16[1024,256]{1,0:T(8,128)(2,1)} %copy-done.2) | copy-start | bytes 1572868
  110.5 3.8 %copy-start.5 = (f32[2,32,1024]{2,1,0:T(8,128)S(1)}, f32[2,32,1024]{2,1,0:T(8,128)}, u32[]{:S(2)}) copy-start(f32[2,32,1024]{2,1,0:T(8,128)} %constant.59.clone.twiddle_ref) | copy-start | bytes 786436
  110.5 3.8 %copy-start.6 = (bf16[32,192]{1,0:T(8,128)(2,1)S(1)}, bf16[32,192]{1,0:T(8,128)(2,1)}, u32[]{:S(2)}) copy-start(bf16[32,192]{1,0:T(8,128)(2,1)} %constant.58.clone.small_ref) | copy-start | bytes 36868
  110.5 9.1 %collective-permute-start.4 = (f32[8,4096]{1,0:T(8,128)S(1)}, f32[8,4096]{1,0:T(8,128)S(1)}, u32[]{:S(2)}, u32[]{:S(2)}) collective-permute-start(f32[8,4096]{1,0:T(8,128)S(1)} %slice_select_fusion.1), channel_id=1, source_target_pairs={{0,128},{64,192},{128,0},{192,64},{1,129},{65,193},{129,1},{193,65... | collective-permute-start | bytes 393224 | tf_op jit(solution)/shard_map/ppermute | solution.py:201
  118.2 3.3 %copy-start.9 = (f32[32,4096]{1,0:T(8,128)S(1)}, f32[32,4096]{1,0:T(8,128)}, u32[]{:S(2)}) copy-start(f32[32,4096]{1,0:T(8,128)} %copy-done.8) | copy-start | bytes 1572868
  119.6 6.2 %collective-permute-start.5 = (f32[4,4096]{1,0:T(4,128)S(1)}, f32[4,4096]{1,0:T(4,128)S(1)}, u32[]{:S(2)}, u32[]{:S(2)}) collective-permute-start(f32[4,4096]{1,0:T(4,128)S(1)} %slice_select_fusion.2), channel_id=1, source_target_pairs={{0,64},{64,0},{128,192},{192,128},{1,65},{65,1},{129,193},{193,129... | collective-permute-start | bytes 196616 | tf_op jit(solution)/shard_map/ppermute | solution.py:201
  125.8 19.2 %collective-permute-start.6 = (f32[2,4096]{1,0:T(2,128)S(1)}, f32[2,4096]{1,0:T(2,128)S(1)}, u32[]{:S(2)}, u32[]{:S(2)}) collective-permute-start(f32[2,4096]{1,0:T(2,128)S(1)} %broadcast_select_fusion.2), channel_id=1, source_target_pairs={{0,256},{256,0},{1,257},{257,1},{2,258},{258,2},{3,259},{259,3},{4... | collective-permute-start | bytes 98312 | tf_op jit(solution)/shard_map/ppermute | solution.py:201
  136.0 42.7 %all-to-all-start.1 = ((f32[32,1,4096]{2,1,0:T(1,128)}), f32[32,1,4096]{2,1,0:T(1,128)S(1)}, u32[]{:S(2)}, u32[]{:S(2)}) async-start(f32[32,1,4096]{2,1,0:T(1,128)} %copy.14), calls=%async_computation.1 | async-start | bytes 1048576 | tf_op jit(solution)/shard_map/all_to_all | solution.py:278
  145.1 31.7 %collective-permute-start.7 = (f32[4096]{0:T(1024)S(1)}, f32[4096]{0:T(1024)S(1)}, u32[]{:S(2)}, u32[]{:S(2)}) collective-permute-start(f32[4096]{0:T(1024)S(1)} %bitcast.22), channel_id=1, source_target_pairs={{1,0},{0,1},{257,2},{256,3},{65,4},{64,5},{321,6},{320,7},{129,8},... | collective-permute-start | bytes 49160 | tf_op jit(solution)/shard_map/ppermute | solution.py:285
  149.1 29.0 %collective-permute-start.8 = (f32[4096]{0:T(1024)S(1)}, f32[4096]{0:T(1024)S(1)}, u32[]{:S(2)}, u32[]{:S(2)}) collective-permute-start(f32[4096]{0:T(1024)S(1)} %bitcast.21), channel_id=1, source_target_pairs={{0,0},{1,1},{256,2},{257,3},{64,4},{65,5},{320,6},{321,7},{128,8},... | collective-permute-start | bytes 49160 | tf_op jit(solution)/shard_map/ppermute | solution.py:285
where the time goes:
time: 181 us
  starting transfers between devices  99.9 us (55%)
  blocking collectives  29.2 us (16%)
  waiting for transfers between devices  25.9 us (14%)
  Pallas kernels  10.5 us (6%)
  local copies, waits for them, and re-layouts  9.8 us (5%)
  other arithmetic  4.19 us (2%)
    all_gather x1, blocking collectives, step(): filters = lax.all_gather(four, ('core', 'x'), axis=0, tiled=True)  29.2 us
    ppermute x1, starting transfers between devices, step(): other = lax.ppermute(pair, 'zhi', [(0, 1), (1, 0)])  28.8 us
    ppermute x2, waiting for transfers between devices, step(): lax.ppermute(pieces[number], everyone, [(b, a) for a, b in pairs[number]])  20.4 us
    ppermute x2, starting transfers between devices, step(): lax.ppermute(sent[number], everyone, pairs[number])  17.6 us
    ppermute x4, starting transfers between devices, halving(): return kept + lax.ppermute(away, axis, pairs)  16.4 us
    all_to_all x1, starting transfers between devices, step(): lax.all_to_all(jnp.concatenate([spectrum, delta], axis=1), SEQ, split_axi...  15.6 us
    ppermute x2, starting transfers between devices, step(): lax.ppermute(pieces[number], everyone, [(b, a) for a, b in pairs[number]])  12.5 us
    all_to_all x1, starting transfers between devices, step(): lax.all_to_all(jnp.concatenate([conv, back], axis=1), SEQ, split_axis=0,...  9.02 us
  transfers between devices with their start and end apart: 11, of which 7 were waited for; matrix products, arithmetic and copies ran while one was open for 2% of the time, Pallas kernels for 5%

commit v1 on v0

--- a/solution.py
+++ b/solution.py
@@ -139,7 +139,7 @@
 
 def inverse_kernel(
     sign, first_ref, filt_ref, small_ref, twiddle_ref, cos_hi, cos_lo, sin_hi, sin_lo, out_ref,
-    rows_ref,
+    rows_ref, turned_ref,
 ):
     classes = first_ref.shape[0]
     points = cos_hi.shape[0]
@@ -168,16 +168,15 @@
         tw_cos, tw_sin = twiddle_ref[0, :, at], twiddle_ref[1, :, at]
         for channel in range(2):
             mine = slice(channel * classes, (channel + 1) * classes)
-            turned = jnp.concatenate(
-                [
-                    real[mine] * tw_cos - imag[mine] * tw_sin,
-                    imag[mine] * tw_cos + real[mine] * tw_sin,
-                ],
-                axis=0,
-            )
-            out_ref[:, channel * points + at.start : channel * points + at.stop] = dot16(
-                small_ref[...], three_terms(turned, 0)
-            )
+            put = slice(channel * points + at.start, channel * points + at.stop)
+            for part, turned in (
+                (0, real[mine] * tw_cos - imag[mine] * tw_sin),
+                (1, imag[mine] * tw_cos + real[mine] * tw_sin),
+            ):
+                high, low = halves(turned)
+                for place, values in ((part, high), (2 + part, low), (4 + part, high)):
+                    turned_ref[place * classes : (place + 1) * classes, put] = values
+    out_ref[...] = dot16(small_ref[...], turned_ref[...])
 
 
 def staging_pairs(x_count, core_count, seq_count):
@@ -187,9 +186,9 @@
         found = []
         for d in range(2 * x_count * core_count):
             for s in range(seq_count):
-                core, x, zhi = s // per_core, s % per_core // per_x, s % per_x // 2
+                core, x, zhi = s // per_core, s % per_core // per_x, (s % per_x // 2) ^ number
                 row = (zhi * x_count + x) * core_count + core
-                found.append((d * seq_count + s, row * seq_count + 2 * d + ((s % 2) ^ number)))
+                found.append((d * seq_count + s, row * seq_count + 2 * d + s % 2))
         pairs.append(found)
     return pairs
 
@@ -199,6 +198,13 @@
     kept = jnp.where(upper, values[rows:], values[:rows])
     away = jnp.where(upper, values[:rows], values[rows:])
     return kept + lax.ppermute(away, axis, pairs)
+
+
+def doubling(values, upper, axis, pairs):
+    other = lax.ppermute(values, axis, pairs)
+    return jnp.concatenate(
+        [jnp.where(upper, other, values), jnp.where(upper, values, other)], axis=0
+    )
 
 
 def step(grad_out, gate, input_spectrum, filter_spectrum):
@@ -224,20 +230,23 @@
         jnp.concatenate([spectrum, delta], axis=1), SEQ, split_axis=0, concat_axis=0, tiled=True
     )
 
-    low_half, high_half = filter_spectrum[:, :2], filter_spectrum[:, 2:]
-    sent = [jnp.where(odd, high_half, low_half), jnp.where(odd, low_half, high_half)]
-    got = [
-        lax.ppermute(sent[number], everyone, pairs[number]).reshape(1, 4 * positions)
-        for number in range(2)
-    ]
-    pair = jnp.concatenate(
-        [jnp.where(odd, got[1], got[0]), jnp.where(odd, got[0], got[1])], axis=0
-    )
-    other = lax.ppermute(pair, "zhi", [(0, 1), (1, 0)])
-    four = jnp.concatenate(
-        [jnp.where(upper_zhi, other, pair), jnp.where(upper_zhi, pair, other)], axis=0
-    )
-    filters = lax.all_gather(four, ("core", "x"), axis=0, tiled=True)
+    near_x = [(x, x ^ 1) for x in range(x_count)]
+    far_x = [(x, x ^ 2) for x in range(x_count)]
+    near_y = [(y, y ^ 1) for y in range(lax.axis_size("y"))]
+    cores = [(0, 1), (1, 0)]
+    wide_row = 4 * positions
+    halves_of = filter_spectrum.reshape(2, 2, per_seq, positions).transpose(1, 0, 2, 3)
+    sent = halves_of.reshape(2, wide_row)
+    got = [lax.ppermute(sent, everyone, pairs[number]) for number in range(2)]
+    first, second = jnp.where(upper_zhi, got[1], got[0]), jnp.where(upper_zhi, got[0], got[1])
+    mine = jnp.stack([jnp.where(odd, v[1], v[0]) for v in (first, second)])
+    away = jnp.stack([jnp.where(odd, v[0], v[1]) for v in (first, second)])
+    other = lax.ppermute(away, "y", near_y)
+    low, high = jnp.where(odd, other, mine), jnp.where(odd, mine, other)
+    four = jnp.stack([low[0], high[0], low[1], high[1]])
+    filters = doubling(four, x_index % 2 == 1, "x", near_x)
+    filters = doubling(filters, x_index >= 2, "x", far_x)
+    filters = doubling(filters, upper_core, "core", cores)
 
     tables = root_tables(positions)
     small_out = small_table(seq_count, False)
@@ -262,16 +271,19 @@
         return pl.pallas_call(
             functools.partial(inverse_kernel, sign),
             out_shape=signal,
-            scratch_shapes=rows,
+            scratch_shapes=rows + [pltpu.VMEM((6 * seq_count, 2 * positions), bf16)],
             name="inverse",
             compiler_params=params,
             cost_estimate=cost,
         )(first, filters, small_back, twiddle, *tables)
 
-    total = halving(terms, upper_core, "core", [(0, 1), (1, 0)])
-    total = halving(total, x_index >= 2, "x", [(x, x ^ 2) for x in range(x_count)])
-    total = halving(total, x_index % 2 == 1, "x", [(x, x ^ 1) for x in range(x_count)])
-    total = halving(total, upper_zhi, "zhi", [(0, 1), (1, 0)])
+    total = halving(terms, upper_core, "core", cores)
+    total = halving(total, x_index >= 2, "x", far_x)
+    total = halving(total, x_index % 2 == 1, "x", near_x)
+    mine = jnp.stack([jnp.where(odd, total[2 * n + 1], total[2 * n]) for n in range(2)])
+    away = jnp.stack([jnp.where(odd, total[2 * n], total[2 * n + 1]) for n in range(2)])
+    other = lax.ppermute(away, "y", near_y)
+    low, high = jnp.where(odd, other, mine), jnp.where(odd, mine, other)
 
     conv = inverse(1.0, moved)
     back = inverse(-1.0, spec)
@@ -279,16 +291,17 @@
         jnp.concatenate([conv, back], axis=1), SEQ, split_axis=0, concat_axis=0, tiled=True
     )
 
-    pieces = [total[0], total[1]]
-    pieces = [jnp.where(odd, pieces[1 - n], pieces[n]) for n in range(2)]
+    rows_out = [jnp.stack([low[n], high[n]]) for n in range(2)]
+    rows_out = [jnp.where(upper_zhi, rows_out[1 - n], rows_out[n]) for n in range(2)]
     ends = [
-        lax.ppermute(pieces[number], everyone, [(b, a) for a, b in pairs[number]]).reshape(
-            2, per_seq, positions
-        )
+        lax.ppermute(rows_out[number], everyone, [(b, a) for a, b in pairs[number]])
         for number in range(2)
     ]
-    grad_filter = jnp.concatenate(
-        [jnp.where(odd, ends[1], ends[0]), jnp.where(odd, ends[0], ends[1])], axis=1
+    grad_filter = (
+        (ends[0] + ends[1])
+        .reshape(2, 2, per_seq, positions)
+        .transpose(1, 0, 2, 3)
+        .reshape(2, 2 * per_seq, positions)
     )
 
     scale = 1.0 / math.sqrt(seq_count * positions)

time: 181 us -> 159 us (0.88)
  the two profiles are of different devices: /device:TPU:30 before, /device:TPU:7 now
where the time goes in v1:
time: 159 us; the launch traced here: 158 us
  starting transfers between devices  73 us (46%)
  waiting for transfers between devices  66.4 us (42%)
  local copies, waits for them, and re-layouts  7.54 us (5%)
  Pallas kernels  6.74 us (4%)
  other arithmetic  3.32 us (2%)
    all_to_all x1, waiting for transfers between devices, step(): lax.all_to_all(jnp.concatenate([spectrum, delta], axis=1), SEQ, split_axi...  25.6 us
    ppermute x2, starting transfers between devices, step(): got = [lax.ppermute(sent, everyone, pairs[number]) for number in range(2)]  19.3 us
    ppermute x2, waiting for transfers between devices, step(): lax.ppermute(rows_out[number], everyone, [(b, a) for a, b in pairs[number]])  18.8 us
    ppermute x2, starting transfers between devices, step(): lax.ppermute(rows_out[number], everyone, [(b, a) for a, b in pairs[number]])  17.7 us
    ppermute x2, waiting for transfers between devices, step(): got = [lax.ppermute(sent, everyone, pairs[number]) for number in range(2)]  12.2 us
    ppermute x3, starting transfers between devices, halving(): return kept + lax.ppermute(away, axis, pairs)  10.5 us
    ppermute x3, starting transfers between devices, doubling(): other = lax.ppermute(values, axis, pairs)  8.86 us
    all_to_all x1, starting transfers between devices, step(): lax.all_to_all(jnp.concatenate([conv, back], axis=1), SEQ, split_axis=0,...  6.76 us
  transfers between devices with their start and end apart: 14, of which 10 were waited for; matrix products, arithmetic and copies ran while one was open for 3% of the time, Pallas kernels for 3%

profile of v1, /device:TPU:7, one launch (start us, length us, event | category | flops | bytes accessed | tf_op | source)
XLA Modules:
  0.0 158.2 jit_solution(10862146171661470030)
XLA Ops:
  0.6 0.0 copy-start.7
  0.6 0.0 copy-start.9
  0.7 0.8 reshape.69
  1.5 0.0 copy-start.6
  1.6 17.3 %collective-permute-start = (f32[2,4096]{1,0:T(2,128)S(1)}, f32[2,4096]{1,0:T(2,128)S(1)}, u32[]{:S(2)}, u32[]{:S(2)}) collective-permute-start(f32[2,4096]{1,0:T(2,128)S(1)} %reshape.70), channel_id=1, source_target_pairs={{0,256},{1,257},{2,0},{3,1},{4,320},{5,321},{6,64},{7,65},{8,384},... | collective-permute-start | bytes 98312 | tf_op jit(solution)/shard_map/ppermute | solution.py:240
  18.9 1.9 %collective-permute-start.1 = (f32[2,4096]{1,0:T(2,128)S(1)}, f32[2,4096]{1,0:T(2,128)S(1)}, u32[]{:S(2)}, u32[]{:S(2)}) collective-permute-start(f32[2,4096]{1,0:T(2,128)S(1)} %reshape.70), channel_id=1, source_target_pairs={{0,0},{1,1},{2,256},{3,257},{4,64},{5,65},{6,320},{7,321},{8,128},... | collective-permute-start | bytes 98312 | tf_op jit(solution)/shard_map/ppermute | solution.py:240
  20.9 0.0 collective-permute-done
  20.9 12.2 %collective-permute-done.1 = f32[2,4096]{1,0:T(2,128)S(1)} collective-permute-done((f32[2,4096]{1,0:T(2,128)S(1)}, f32[2,4096]{1,0:T(2,128)S(1)}, u32[]{:S(2)}, u32[]{:S(2)}) %collective-permute-start.1) | collective-permute-done | bytes 32800 | tf_op jit(solution)/shard_map/ppermute | solution.py:240
  33.2 2.1 %collective-permute-start.2 = (f32[2,4096]{1,0:T(2,128)S(1)}, f32[2,4096]{1,0:T(2,128)S(1)}, u32[]{:S(2)}, u32[]{:S(2)}) collective-permute-start(f32[2,4096]{1,0:T(2,128)S(1)} %pad_maximum_fusion.5), channel_id=1, source_target_pairs={{0,1},{1,0},{2,3},{3,2},{4,5},{5,4},{6,7},{7,6},{8,9},{9,8},{10,11... | collective-permute-start | bytes 98312 | tf_op jit(solution)/shard_map/ppermute | solution.py:244
  35.3 0.0 copy-done.7
  35.4 0.0 copy-done.9
  35.4 0.0 copy-done.6
  35.4 0.3 reshape.66
  35.7 0.1 copy.27
  35.8 0.5 reshape.67
  36.3 0.1 reshape.68
  36.4 1.5 collective-permute-done.2
  38.0 0.1 pad_maximum_fusion.4
  38.0 2.8 %collective-permute-start.3 = (f32[4,4096]{1,0:T(4,128)S(1)}, f32[4,4096]{1,0:T(4,128)S(1)}, u32[]{:S(2)}, u32[]{:S(2)}) collective-permute-start(f32[4,4096]{1,0:T(4,128)S(1)} %pad_maximum_fusion.4), channel_id=1, source_target_pairs={{0,64},{64,0},{128,192},{192,128},{1,65},{65,1},{129,193},{193,129... | collective-permute-start | bytes 196616 | tf_op jit(solution)/shard_map/ppermute | solution.py:204
  40.8 0.1 pad_maximum_fusion
  40.9 1.4 all_to_all.15
  42.3 4.7 %all-to-all-start = ((f32[32,1,6144]{2,1,0:T(1,128)}), f32[32,1,6144]{2,1,0:T(1,128)S(1)}, u32[]{:S(2)}, u32[]{:S(2)}) async-start(f32[32,1,6144]{2,1,0:T(1,128)} %all_to_all.15), calls=%async_computation | async-start | bytes 1572864 | tf_op jit(solution)/shard_map/all_to_all | solution.py:229
  47.0 0.0 collective-permute-done.3
  47.0 0.1 broadcast_select_fusion.21
  47.1 3.7 %collective-permute-start.4 = (f32[8,4096]{1,0:T(8,128)S(1)}, f32[8,4096]{1,0:T(8,128)S(1)}, u32[]{:S(2)}, u32[]{:S(2)}) collective-permute-start(f32[8,4096]{1,0:T(8,128)S(1)} %pad_maximum_fusion.3), channel_id=1, source_target_pairs={{0,128},{64,192},{128,0},{192,64},{1,129},{65,193},{129,1},{193,65... | collective-permute-start | bytes 393224 | tf_op jit(solution)/shard_map/ppermute | solution.py:204
  50.9 5.1 %collective-permute-done.4 = f32[8,4096]{1,0:T(8,128)S(1)} collective-permute-done((f32[8,4096]{1,0:T(8,128)S(1)}, f32[8,4096]{1,0:T(8,128)S(1)}, u32[]{:S(2)}, u32[]{:S(2)}) %collective-permute-start.4) | collective-permute-done | bytes 131104 | tf_op jit(solution)/shard_map/ppermute | solution.py:204
  56.0 0.0 copy-start
  56.0 0.0 copy-start.1
  56.1 2.4 %collective-permute-start.5 = (f32[16,4096]{1,0:T(8,128)S(1)}, f32[16,4096]{1,0:T(8,128)}, u32[]{:S(2)}, u32[]{:S(2)}) collective-permute-start(f32[16,4096]{1,0:T(8,128)S(1)} %pad_maximum_fusion.2), channel_id=1, source_target_pairs={{0,32},{32,0},{1,33},{33,1},{2,34},{34,2},{3,35},{35,3},{4,36},{36... | collective-permute-start | bytes 786440 | tf_op jit(solution)/shard_map/ppermute | solution.py:204
  58.5 0.0 copy-done
  58.5 0.0 copy-done.1
  58.5 0.6 root_tables.1
  59.1 0.7 collective-permute-done.5
  59.8 1.7 %broadcast_select_fusion.1 = (f32[16,4096]{1,0:T(8,128)S(1)}, f32[16,4096]{1,0:T(8,128)}) fusion(f32[16,4096]{1,0:T(8,128)} %collective-permute-done.5, pred[]{:T(512)S(6)} %eq.17, f32[8,4096]{1,0:T(8,128)S(1)} %get-tuple-element.20, f32[8,4096]{1,0:T(8,128)S(1)} %get-tuple-element.19), kind=kLoop, calls=%fused_computation.18 | loop fusion | flops 196608 | bytes 1048577 | tf_op jit(solution)/shard_map/jit(_where)/select_n | solution.py:206
  61.5 25.6 %all-to-all-done = f32[32,1,6144]{2,1,0:T(1,128)S(1)} async-done(((f32[32,1,6144]{2,1,0:T(1,128)}), f32[32,1,6144]{2,1,0:T(1,128)S(1)}, u32[]{:S(2)}, u32[]{:S(2)}) %all-to-all-start) | async-done | bytes 786464 | tf_op jit(solution)/shard_map/all_to_all | solution.py:229
  87.0 0.2 copy.25
  87.3 2.0 %forward.1 = (f32[32,4096]{1,0:T(8,128)S(1)}, f32[32,4096]{1,0:T(8,128)S(1)}) custom-call(f32[32,6144]{1,0:T(8,128)S(1)} %bitcast.17, bf16[64,96]{1,0:T(8,128)(2,1)S(1)} %copy-done.4, f32[2,32,1024]{2,1,0:T(8,128)S(1)} %copy-done.2, bf16[1024,256]{1,0:T(8,128)(2,1)S(1)} %get-tuple-element.9.cos_hi, bf16[1024,256]{1,0:T(8,128)(2,1)S(1)} %get-tuple-element.10.cos_lo, ...), custom_call_target="tpu_custom_call" | custom-call | flops 2000000000 | bytes 10000000 | tf_op jit(solution)/shard_map/forward/pallas_call | solution.py:261
  89.4 2.4 %collective-permute-start.6 = (f32[16,4096]{1,0:T(8,128)S(1)}, f32[16,4096]{1,0:T(8,128)S(1)}, u32[]{:S(2)}, u32[]{:S(2)}) collective-permute-start(f32[16,4096]{1,0:T(8,128)S(1)} %slice_select_fusion), channel_id=1, source_target_pairs={{0,32},{32,0},{1,33},{33,1},{2,34},{34,2},{3,35},{35,3},{4,36},{36... | collective-permute-start | bytes 786440 | tf_op jit(solution)/shard_map/ppermute | solution.py:200
  91.9 1.1 collective-permute-done.6
  93.0 0.0 copy-start.3
  93.0 5.2 %collective-permute-start.7 = (f32[8,4096]{1,0:T(8,128)S(1)}, f32[8,4096]{1,0:T(8,128)S(1)}, u32[]{:S(2)}, u32[]{:S(2)}) collective-permute-start(f32[8,4096]{1,0:T(8,128)S(1)} %slice_select_fusion.1), channel_id=1, source_target_pairs={{0,128},{64,192},{128,0},{192,64},{1,129},{65,193},{129,1},{193,65... | collective-permute-start | bytes 393224 | tf_op jit(solution)/shard_map/ppermute | solution.py:200
  98.3 2.0 %inverse.2 = f32[32,2048]{1,0:T(8,128)S(1)} custom-call(f32[32,6144]{1,0:T(8,128)S(1)} %bitcast.18, f32[32,4096]{1,0:T(8,128)S(1)} %pad_maximum_fusion.1.filt_ref, bf16[32,192]{1,0:T(8,128)(2,1)S(1)} %copy-done.3, f32[2,32,1024]{2,1,0:T(8,128)S(1)} %copy-done.2, bf16[1024,256]{1,0:T(8,128)(2,1)S(1)} %get-tuple-element.9.cos_hi, ...), custom_call_target="tpu_custom_call" | custom-call | flops 2000000000 | bytes 10000000 | tf_op jit(solution)/shard_map/inverse/pallas_call | solution.py:271
  100.3 1.4 collective-permute-done.7
  101.8 2.9 %collective-permute-start.8 = (f32[4,4096]{1,0:T(4,128)S(1)}, f32[4,4096]{1,0:T(4,128)S(1)}, u32[]{:S(2)}, u32[]{:S(2)}) collective-permute-start(f32[4,4096]{1,0:T(4,128)S(1)} %slice_select_fusion.2), channel_id=1, source_target_pairs={{0,64},{64,0},{128,192},{192,128},{1,65},{65,1},{129,193},{193,129... | collective-permute-start | bytes 196616 | tf_op jit(solution)/shard_map/ppermute | solution.py:200
  104.7 2.0 %inverse.3 = f32[32,2048]{1,0:T(8,128)S(1)} custom-call(f32[32,4096]{1,0:T(8,128)S(1)} %get-tuple-element.13.first_ref, f32[32,4096]{1,0:T(8,128)S(1)} %pad_maximum_fusion.1.filt_ref, bf16[32,192]{1,0:T(8,128)(2,1)S(1)} %copy-done.3, f32[2,32,1024]{2,1,0:T(8,128)S(1)} %copy-done.2, bf16[1024,256]{1,0:T(8,128)(2,1)S(1)} %get-tuple-element.9.cos_hi, ...), custom_call_target="tpu_custom_call" | custom-call | flops 2000000000 | bytes 10000000 | tf_op jit(solution)/shard_map/inverse/pallas_call | solution.py:271
  106.7 0.1 collective-permute-done.8
  106.8 0.1 broadcast_select_fusion.9
  106.9 3.0 %collective-permute-start.9 = (f32[2,4096]{1,0:T(2,128)S(1)}, f32[2,4096]{1,0:T(2,128)S(1)}, u32[]{:S(2)}, u32[]{:S(2)}) collective-permute-start(f32[2,4096]{1,0:T(2,128)S(1)} %pad_maximum_fusion.7), channel_id=1, source_target_pairs={{0,1},{1,0},{2,3},{3,2},{4,5},{5,4},{6,7},{7,6},{8,9},{9,8},{10,11... | collective-permute-start | bytes 98312 | tf_op jit(solution)/shard_map/ppermute | solution.py:285
  110.0 1.3 copy.17
  111.4 6.8 %all-to-all-start.1 = ((f32[32,1,4096]{2,1,0:T(1,128)}), f32[32,1,4096]{2,1,0:T(1,128)S(1)}, u32[]{:S(2)}, u32[]{:S(2)}) async-start(f32[32,1,4096]{2,1,0:T(1,128)} %copy.17), calls=%async_computation.1 | async-start | bytes 1048576 | tf_op jit(solution)/shard_map/all_to_all | solution.py:290
  118.1 0.0 collective-permute-done.9
  118.2 0.1 fusion.2
  118.3 0.1 broadcast_select_fusion.4
  118.3 13.4 %collective-permute-start.10 = (f32[2,4096]{1,0:T(2,128)S(1)}, f32[2,4096]{1,0:T(2,128)S(1)}, u32[]{:S(2)}, u32[]{:S(2)}) collective-permute-start(f32[2,4096]{1,0:T(2,128)S(1)} %get-tuple-element.24), channel_id=1, source_target_pairs={{0,0},{1,1},{256,2},{257,3},{64,4},{65,5},{320,6},{321,7},{128,8},... | collective-permute-start | bytes 98312 | tf_op jit(solution)/shard_map/ppermute | solution.py:297
  131.7 4.3 %collective-permute-start.11 = (f32[2,4096]{1,0:T(2,128)S(1)}, f32[2,4096]{1,0:T(2,128)S(1)}, u32[]{:S(2)}, u32[]{:S(2)}) collective-permute-start(f32[2,4096]{1,0:T(2,128)S(1)} %get-tuple-element.23), channel_id=1, source_target_pairs={{256,0},{257,1},{0,2},{1,3},{320,4},{321,5},{64,6},{65,7},{384,8},... | collective-permute-start | bytes 98312 | tf_op jit(solution)/shard_map/ppermute | solution.py:297
  136.1 1.7 %collective-permute-done.10 = f32[2,4096]{1,0:T(2,128)S(1)} collective-permute-done((f32[2,4096]{1,0:T(2,128)S(1)}, f32[2,4096]{1,0:T(2,128)S(1)}, u32[]{:S(2)}, u32[]{:S(2)}) %collective-permute-start.10) | collective-permute-done | bytes 32800 | tf_op jit(solution)/shard_map/ppermute | solution.py:297
  137.8 17.1 %collective-permute-done.11 = f32[2,4096]{1,0:T(2,128)S(1)} collective-permute-done((f32[2,4096]{1,0:T(2,128)S(1)}, f32[2,4096]{1,0:T(2,128)S(1)}, u32[]{:S(2)}, u32[]{:S(2)}) %collective-permute-start.11) | collective-permute-done | bytes 32800 | tf_op jit(solution)/shard_map/ppermute | solution.py:297
  154.9 0.6 reshape.72
  155.6 0.0 all-to-all-done.1
  155.6 0.3 copy.26
  155.9 0.0 copy-start.8
  156.0 0.8 copy-done.8
  156.8 0.7 fusion
  157.5 0.7 convert_element_type.26
  (34 shorter events, 0.8 us)
Async XLA Ops:
  0.6 34.7 %copy-start.7 = (bf16[1,64,1024]{2,1,0:T(8,128)(2,1)S(1)}, bf16[1,64,1024]{2,1,0:T(8,128)(2,1)}, u32[]{:S(2)}) copy-start(bf16[1,64,1024]{2,1,0:T(8,128)(2,1)} %param.9) | copy-start | bytes 393220
  0.6 34.7 %copy-start.9 = (bf16[1,64,1024]{2,1,0:T(8,128)(2,1)S(1)}, bf16[1,64,1024]{2,1,0:T(8,128)(2,1)}, u32[]{:S(2)}) copy-start(bf16[1,64,1024]{2,1,0:T(8,128)(2,1)} %param.10) | copy-start | bytes 393220
  1.5 33.9 %copy-start.6 = (f32[1,2,64,1024]{3,2,1,0:T(8,128)S(1)}, f32[1,2,64,1024]{3,2,1,0:T(8,128)}, u32[]{:S(2)}) copy-start(f32[1,2,64,1024]{3,2,1,0:T(8,128)} %param.11) | copy-start | bytes 1572868
  1.6 19.3 %collective-permute-start = (f32[2,4096]{1,0:T(2,128)S(1)}, f32[2,4096]{1,0:T(2,128)S(1)}, u32[]{:S(2)}, u32[]{:S(2)}) collective-permute-start(f32[2,4096]{1,0:T(2,128)S(1)} %reshape.70), channel_id=1, source_target_pairs={{0,256},{1,257},{2,0},{3,1},{4,320},{5,321},{6,64},{7,65},{8,384},... | collective-permute-start | bytes 98312 | tf_op jit(solution)/shard_map/ppermute | solution.py:240
  18.9 14.2 %collective-permute-start.1 = (f32[2,4096]{1,0:T(2,128)S(1)}, f32[2,4096]{1,0:T(2,128)S(1)}, u32[]{:S(2)}, u32[]{:S(2)}) collective-permute-start(f32[2,4096]{1,0:T(2,128)S(1)} %reshape.70), channel_id=1, source_target_pairs={{0,0},{1,1},{2,256},{3,257},{4,64},{5,65},{6,320},{7,321},{8,128},... | collective-permute-start | bytes 98312 | tf_op jit(solution)/shard_map/ppermute | solution.py:240
  33.2 4.7 %collective-permute-start.2 = (f32[2,4096]{1,0:T(2,128)S(1)}, f32[2,4096]{1,0:T(2,128)S(1)}, u32[]{:S(2)}, u32[]{:S(2)}) collective-permute-start(f32[2,4096]{1,0:T(2,128)S(1)} %pad_maximum_fusion.5), channel_id=1, source_target_pairs={{0,1},{1,0},{2,3},{3,2},{4,5},{5,4},{6,7},{7,6},{8,9},{9,8},{10,11... | collective-permute-start | bytes 98312 | tf_op jit(solution)/shard_map/ppermute | solution.py:244
  38.0 9.0 %collective-permute-start.3 = (f32[4,4096]{1,0:T(4,128)S(1)}, f32[4,4096]{1,0:T(4,128)S(1)}, u32[]{:S(2)}, u32[]{:S(2)}) collective-permute-start(f32[4,4096]{1,0:T(4,128)S(1)} %pad_maximum_fusion.4), channel_id=1, source_target_pairs={{0,64},{64,0},{128,192},{192,128},{1,65},{65,1},{129,193},{193,129... | collective-permute-start | bytes 196616 | tf_op jit(solution)/shard_map/ppermute | solution.py:204
  42.3 44.7 %all-to-all-start = ((f32[32,1,6144]{2,1,0:T(1,128)}), f32[32,1,6144]{2,1,0:T(1,128)S(1)}, u32[]{:S(2)}, u32[]{:S(2)}) async-start(f32[32,1,6144]{2,1,0:T(1,128)} %all_to_all.15), calls=%async_computation | async-start | bytes 1572864 | tf_op jit(solution)/shard_map/all_to_all | solution.py:229
  47.1 8.8 %collective-permute-start.4 = (f32[8,4096]{1,0:T(8,128)S(1)}, f32[8,4096]{1,0:T(8,128)S(1)}, u32[]{:S(2)}, u32[]{:S(2)}) collective-permute-start(f32[8,4096]{1,0:T(8,128)S(1)} %pad_maximum_fusion.3), channel_id=1, source_target_pairs={{0,128},{64,192},{128,0},{192,64},{1,129},{65,193},{129,1},{193,65... | collective-permute-start | bytes 393224 | tf_op jit(solution)/shard_map/ppermute | solution.py:204
  56.0 2.4 %copy-start = (f32[2,32,256]{2,1,0:T(8,128)S(1)}, f32[2,32,256]{2,1,0:T(8,128)}, u32[]{:S(2)}) copy-start(f32[2,32,256]{2,1,0:T(8,128)} %constant.57.clone.coarse_ref) | copy-start | bytes 196612
  56.0 2.4 %copy-start.1 = (f32[2,32,256]{2,1,0:T(8,128)S(1)}, f32[2,32,256]{2,1,0:T(8,128)}, u32[]{:S(2)}) copy-start(f32[2,32,256]{2,1,0:T(8,128)} %constant.58.clone.fine_ref) | copy-start | bytes 196612
  56.1 3.7 %collective-permute-start.5 = (f32[16,4096]{1,0:T(8,128)S(1)}, f32[16,4096]{1,0:T(8,128)}, u32[]{:S(2)}, u32[]{:S(2)}) collective-permute-start(f32[16,4096]{1,0:T(8,128)S(1)} %pad_maximum_fusion.2), channel_id=1, source_target_pairs={{0,32},{32,0},{1,33},{33,1},{2,34},{34,2},{3,35},{35,3},{4,36},{36... | collective-permute-start | bytes 786440 | tf_op jit(solution)/shard_map/ppermute | solution.py:204
  61.5 25.8 %copy-start.2 = (f32[2,32,1024]{2,1,0:T(8,128)S(1)}, f32[2,32,1024]{2,1,0:T(8,128)}, u32[]{:S(2)}) copy-start(f32[2,32,1024]{2,1,0:T(8,128)} %constant.61.clone.twiddle_ref) | copy-start | bytes 786436
  61.5 25.8 %copy-start.4 = (bf16[64,96]{1,0:T(8,128)(2,1)S(1)}, bf16[64,96]{1,0:T(8,128)(2,1)}, u32[]{:S(2)}) copy-start(bf16[64,96]{1,0:T(8,128)(2,1)} %constant.59.clone.small_ref) | copy-start | bytes 36868
  89.3 2.5 %copy-start.5 = (f32[16,4096]{1,0:T(8,128)S(1)}, f32[16,4096]{1,0:T(8,128)}, u32[]{:S(2)}) copy-start(f32[16,4096]{1,0:T(8,128)} %get-tuple-element.18) | copy-start | bytes 786436
  89.4 3.6 %collective-permute-start.6 = (f32[16,4096]{1,0:T(8,128)S(1)}, f32[16,4096]{1,0:T(8,128)S(1)}, u32[]{:S(2)}, u32[]{:S(2)}) collective-permute-start(f32[16,4096]{1,0:T(8,128)S(1)} %slice_select_fusion), channel_id=1, source_target_pairs={{0,32},{32,0},{1,33},{33,1},{2,34},{34,2},{3,35},{35,3},{4,36},{36... | collective-permute-start | bytes 786440 | tf_op jit(solution)/shard_map/ppermute | solution.py:200
  93.0 5.3 %copy-start.3 = (bf16[32,192]{1,0:T(8,128)(2,1)S(1)}, bf16[32,192]{1,0:T(8,128)(2,1)}, u32[]{:S(2)}) copy-start(bf16[32,192]{1,0:T(8,128)(2,1)} %constant.60.clone.small_ref) | copy-start | bytes 36868
  93.0 8.7 %collective-permute-start.7 = (f32[8,4096]{1,0:T(8,128)S(1)}, f32[8,4096]{1,0:T(8,128)S(1)}, u32[]{:S(2)}, u32[]{:S(2)}) collective-permute-start(f32[8,4096]{1,0:T(8,128)S(1)} %slice_select_fusion.1), channel_id=1, source_target_pairs={{0,128},{64,192},{128,0},{192,64},{1,129},{65,193},{129,1},{193,65... | collective-permute-start | bytes 393224 | tf_op jit(solution)/shard_map/ppermute | solution.py:200
  101.8 5.0 %collective-permute-start.8 = (f32[4,4096]{1,0:T(4,128)S(1)}, f32[4,4096]{1,0:T(4,128)S(1)}, u32[]{:S(2)}, u32[]{:S(2)}) collective-permute-start(f32[4,4096]{1,0:T(4,128)S(1)} %slice_select_fusion.2), channel_id=1, source_target_pairs={{0,64},{64,0},{128,192},{192,128},{1,65},{65,1},{129,193},{193,129... | collective-permute-start | bytes 196616 | tf_op jit(solution)/shard_map/ppermute | solution.py:200
  106.9 11.2 %collective-permute-start.9 = (f32[2,4096]{1,0:T(2,128)S(1)}, f32[2,4096]{1,0:T(2,128)S(1)}, u32[]{:S(2)}, u32[]{:S(2)}) collective-permute-start(f32[2,4096]{1,0:T(2,128)S(1)} %pad_maximum_fusion.7), channel_id=1, source_target_pairs={{0,1},{1,0},{2,3},{3,2},{4,5},{5,4},{6,7},{7,6},{8,9},{9,8},{10,11... | collective-permute-start | bytes 98312 | tf_op jit(solution)/shard_map/ppermute | solution.py:285
  111.4 44.2 %all-to-all-start.1 = ((f32[32,1,4096]{2,1,0:T(1,128)}), f32[32,1,4096]{2,1,0:T(1,128)S(1)}, u32[]{:S(2)}, u32[]{:S(2)}) async-start(f32[32,1,4096]{2,1,0:T(1,128)} %copy.17), calls=%async_computation.1 | async-start | bytes 1048576 | tf_op jit(solution)/shard_map/all_to_all | solution.py:290
  118.3 19.4 %collective-permute-start.10 = (f32[2,4096]{1,0:T(2,128)S(1)}, f32[2,4096]{1,0:T(2,128)S(1)}, u32[]{:S(2)}, u32[]{:S(2)}) collective-permute-start(f32[2,4096]{1,0:T(2,128)S(1)} %get-tuple-element.24), channel_id=1, source_target_pairs={{0,0},{1,1},{256,2},{257,3},{64,4},{65,5},{320,6},{321,7},{128,8},... | collective-permute-start | bytes 98312 | tf_op jit(solution)/shard_map/ppermute | solution.py:297
  131.7 23.1 %collective-permute-start.11 = (f32[2,4096]{1,0:T(2,128)S(1)}, f32[2,4096]{1,0:T(2,128)S(1)}, u32[]{:S(2)}, u32[]{:S(2)}) collective-permute-start(f32[2,4096]{1,0:T(2,128)S(1)} %get-tuple-element.23), channel_id=1, source_target_pairs={{256,0},{257,1},{0,2},{1,3},{320,4},{321,5},{64,6},{65,7},{384,8},... | collective-permute-start | bytes 98312 | tf_op jit(solution)/shard_map/ppermute | solution.py:297
  155.9 0.9 copy-start.8

commit v2 on v1

--- a/solution.py
+++ b/solution.py
@@ -180,15 +180,14 @@
 
 
 def staging_pairs(x_count, core_count, seq_count):
-    per_core, per_x = seq_count // core_count, seq_count // (core_count * x_count)
     pairs = []
     for number in range(2):
         found = []
         for d in range(2 * x_count * core_count):
             for s in range(seq_count):
-                core, x, zhi = s // per_core, s % per_core // per_x, (s % per_x // 2) ^ number
-                row = (zhi * x_count + x) * core_count + core
-                found.append((d * seq_count + s, row * seq_count + 2 * d + s % 2))
+                e0, core, near, far, e1 = [s >> bit & 1 for bit in (4, 3, 2, 1, 0)]
+                row = ((e1 ^ number) * x_count + 2 * far + near) * core_count + core
+                found.append((d * seq_count + s, row * seq_count + 2 * d + e0))
         pairs.append(found)
     return pairs
 
@@ -234,19 +233,23 @@
     far_x = [(x, x ^ 2) for x in range(x_count)]
     near_y = [(y, y ^ 1) for y in range(lax.axis_size("y"))]
     cores = [(0, 1), (1, 0)]
-    wide_row = 4 * positions
-    halves_of = filter_spectrum.reshape(2, 2, per_seq, positions).transpose(1, 0, 2, 3)
-    sent = halves_of.reshape(2, wide_row)
+    half_row = 4 * positions
+    sent = (
+        filter_spectrum.reshape(2, 2, per_seq, positions)
+        .transpose(1, 0, 2, 3)
+        .reshape(1, 2 * half_row)
+    )
     got = [lax.ppermute(sent, everyone, pairs[number]) for number in range(2)]
-    first, second = jnp.where(upper_zhi, got[1], got[0]), jnp.where(upper_zhi, got[0], got[1])
-    mine = jnp.stack([jnp.where(odd, v[1], v[0]) for v in (first, second)])
-    away = jnp.stack([jnp.where(odd, v[0], v[1]) for v in (first, second)])
+    filters = jnp.concatenate(
+        [jnp.where(upper_zhi, got[1], got[0]), jnp.where(upper_zhi, got[0], got[1])], axis=0
+    )
+    filters = doubling(filters, x_index >= 2, "x", far_x)
+    filters = doubling(filters, x_index % 2 == 1, "x", near_x)
+    filters = doubling(filters, upper_core, "core", cores)
+    mine = jnp.where(odd, filters[:, half_row:], filters[:, :half_row])
+    away = jnp.where(odd, filters[:, :half_row], filters[:, half_row:])
     other = lax.ppermute(away, "y", near_y)
-    low, high = jnp.where(odd, other, mine), jnp.where(odd, mine, other)
-    four = jnp.stack([low[0], high[0], low[1], high[1]])
-    filters = doubling(four, x_index % 2 == 1, "x", near_x)
-    filters = doubling(filters, x_index >= 2, "x", far_x)
-    filters = doubling(filters, upper_core, "core", cores)
+    filters = jnp.concatenate([jnp.where(odd, other, mine), jnp.where(odd, mine, other)], axis=0)
 
     tables = root_tables(positions)
     small_out = small_table(seq_count, False)
@@ -277,13 +280,16 @@
             cost_estimate=cost,
         )(first, filters, small_back, twiddle, *tables)
 
-    total = halving(terms, upper_core, "core", cores)
+    half = seq_count // 2
+    mine = jnp.where(odd, terms[half:], terms[:half])
+    away = jnp.where(odd, terms[:half], terms[half:])
+    other = lax.ppermute(away, "y", near_y)
+    total = jnp.concatenate(
+        [jnp.where(odd, other, mine), jnp.where(odd, mine, other)], axis=1
+    )
+    total = halving(total, upper_core, "core", cores)
+    total = halving(total, x_index % 2 == 1, "x", near_x)
     total = halving(total, x_index >= 2, "x", far_x)
-    total = halving(total, x_index % 2 == 1, "x", near_x)
-    mine = jnp.stack([jnp.where(odd, total[2 * n + 1], total[2 * n]) for n in range(2)])
-    away = jnp.stack([jnp.where(odd, total[2 * n], total[2 * n + 1]) for n in range(2)])
-    other = lax.ppermute(away, "y", near_y)
-    low, high = jnp.where(odd, other, mine), jnp.where(odd, mine, other)
 
     conv = inverse(1.0, moved)
     back = inverse(-1.0, spec)
@@ -291,8 +297,9 @@
         jnp.concatenate([conv, back], axis=1), SEQ, split_axis=0, concat_axis=0, tiled=True
     )
 
-    rows_out = [jnp.stack([low[n], high[n]]) for n in range(2)]
-    rows_out = [jnp.where(upper_zhi, rows_out[1 - n], rows_out[n]) for n in range(2)]
+    rows_out = [
+        jnp.where(upper_zhi, total[1 - n : 2 - n], total[n : n + 1]) for n in range(2)
+    ]
     ends = [
         lax.ppermute(rows_out[number], everyone, [(b, a) for a, b in pairs[number]])
         for number in range(2)

time: 159 us -> 166 us (1.044)
  starting transfers between devices: 73 us -> 84.5 us
  waiting for transfers between devices: 66.4 us -> 59.4 us
  local copies, waits for them, and re-layouts: 7.54 us -> 9.32 us
    all_to_all x1, starting transfers between devices: 4.68 us -> 14.8 us  [step(): lax.all_to_all(jnp.concatenate([spectrum, delta], axis=1), SEQ, split_axi...]
    ppermute x2, waiting for transfers between devices: 12.2 us -> 3.43 us  [step(): got = [lax.ppermute(sent, everyone, pairs[number]) for number in range(2)]]
    ppermute x2, starting transfers between devices: 17.7 us -> 12.3 us  [step(): lax.ppermute(rows_out[number], everyone, [(b, a) for a, b in pairs[number]])]
    ppermute x3, starting transfers between devices: 10.5 us -> 14.6 us  [halving(): return kept + lax.ppermute(away, axis, pairs)]
    ppermute x2, waiting for transfers between devices: 1.5 us -> 4 us  [step(): other = lax.ppermute(away, 'y', near_y)]
    unnamed x22 -> x28, local copies, waits for them, and re-layouts: 1.45 us -> 3.39 us
    ppermute x2, waiting for transfers between devices: 18.8 us -> 20.6 us  [step(): lax.ppermute(rows_out[number], everyone, [(b, a) for a, b in pairs[number]])]
  transfers between devices with their start and end apart: 14 -> 14, of which waited for: 10 -> 7; matrix products, arithmetic and copies ran while one was open for 3% -> 4% of each run, Pallas kernels for 3% -> 4%
where the time goes in v2:
time: 166 us
  starting transfers between devices  84.5 us (51%)
  waiting for transfers between devices  59.4 us (36%)
  local copies, waits for them, and re-layouts  9.32 us (6%)
  Pallas kernels  6.74 us (4%)
  other arithmetic  4.51 us (3%)
    all_to_all x1, waiting for transfers between devices, step(): lax.all_to_all(jnp.concatenate([spectrum, delta], axis=1), SEQ, split_axi...  25.6 us
    ppermute x2, waiting for transfers between devices, step(): lax.ppermute(rows_out[number], everyone, [(b, a) for a, b in pairs[number]])  20.6 us
    ppermute x2, starting transfers between devices, step(): got = [lax.ppermute(sent, everyone, pairs[number]) for number in range(2)]  20.6 us
    all_to_all x1, starting transfers between devices, step(): lax.all_to_all(jnp.concatenate([spectrum, delta], axis=1), SEQ, split_axi...  14.8 us
    ppermute x3, starting transfers between devices, halving(): return kept + lax.ppermute(away, axis, pairs)  14.6 us
    ppermute x2, starting transfers between devices, step(): lax.ppermute(rows_out[number], everyone, [(b, a) for a, b in pairs[number]])  12.3 us
    ppermute x3, starting transfers between devices, doubling(): other = lax.ppermute(values, axis, pairs)  9.33 us
    all_to_all x1, starting transfers between devices, step(): lax.all_to_all(jnp.concatenate([conv, back], axis=1), SEQ, split_axis=0,...  7.1 us
  transfers between devices with their start and end apart: 14, of which 7 were waited for; matrix products, arithmetic and copies ran while one was open for 4% of the time, Pallas kernels for 4%

profile of v2, /device:TPU:7, one launch (start us, length us, event | category | flops | bytes accessed | tf_op | source)
XLA Modules:
  0.0 165.7 jit_solution(12238606069696800620)
XLA Ops:
  0.6 0.8 reshape.69
  1.4 0.1 reshape.70
  1.5 9.4 %collective-permute-start.1 = (f32[1,8192]{1,0:T(1,128)S(1)}, f32[1,8192]{1,0:T(1,128)S(1)}, u32[]{:S(2)}, u32[]{:S(2)}) collective-permute-start(f32[1,8192]{1,0:T(1,128)S(1)} %reshape.70), channel_id=1, source_target_pairs={{0,0},{1,256},{2,128},{3,384},{4,64},{5,320},{6,192},{7,448},{8,32... | collective-permute-start | bytes 98312 | tf_op jit(solution)/shard_map/ppermute | solution.py:242
  10.9 11.2 %collective-permute-start = (f32[1,8192]{1,0:T(1,128)S(1)}, f32[1,8192]{1,0:T(1,128)S(1)}, u32[]{:S(2)}, u32[]{:S(2)}) collective-permute-start(f32[1,8192]{1,0:T(1,128)S(1)} %reshape.70), channel_id=1, source_target_pairs={{0,256},{1,0},{2,384},{3,128},{4,320},{5,64},{6,448},{7,192},{8,28... | collective-permute-start | bytes 98312 | tf_op jit(solution)/shard_map/ppermute | solution.py:242
  22.1 0.0 copy-start.10
  22.1 0.0 copy-start.12
  22.2 3.4 %collective-permute-done = f32[1,8192]{1,0:T(1,128)S(1)} collective-permute-done((f32[1,8192]{1,0:T(1,128)S(1)}, f32[1,8192]{1,0:T(1,128)S(1)}, u32[]{:S(2)}, u32[]{:S(2)}) %collective-permute-start) | collective-permute-done | bytes 32800 | tf_op jit(solution)/shard_map/ppermute | solution.py:242
  25.6 0.1 pad_maximum_fusion.6
  25.7 0.0 copy-start.9
  25.7 2.1 %collective-permute-start.2 = (f32[2,8192]{1,0:T(2,128)S(1)}, f32[2,8192]{1,0:T(2,128)S(1)}, u32[]{:S(2)}, u32[]{:S(2)}) collective-permute-start(f32[2,8192]{1,0:T(2,128)S(1)} %pad_maximum_fusion.6), channel_id=1, source_target_pairs={{0,128},{64,192},{128,0},{192,64},{1,129},{65,193},{129,1},{193,65... | collective-permute-start | bytes 196616 | tf_op jit(solution)/shard_map/ppermute | solution.py:203
  27.8 0.1 reshape.68
  27.9 0.3 reshape.66
  28.3 0.1 copy.27
  28.3 0.5 reshape.67
  28.8 3.6 %collective-permute-done.2 = f32[2,8192]{1,0:T(2,128)S(1)} collective-permute-done((f32[2,8192]{1,0:T(2,128)S(1)}, f32[2,8192]{1,0:T(2,128)S(1)}, u32[]{:S(2)}, u32[]{:S(2)}) %collective-permute-start.2) | collective-permute-done | bytes 65568 | tf_op jit(solution)/shard_map/ppermute | solution.py:203
  32.4 0.1 broadcast_select_fusion.15
  32.5 0.1 pad_maximum_fusion.5
  32.5 3.2 %collective-permute-start.3 = (f32[4,8192]{1,0:T(4,128)S(1)}, f32[4,8192]{1,0:T(4,128)S(1)}, u32[]{:S(2)}, u32[]{:S(2)}) collective-permute-start(f32[4,8192]{1,0:T(4,128)S(1)} %pad_maximum_fusion.5), channel_id=1, source_target_pairs={{0,64},{64,0},{128,192},{192,128},{1,65},{65,1},{129,193},{193,129... | collective-permute-start | bytes 393224 | tf_op jit(solution)/shard_map/ppermute | solution.py:203
  35.7 0.1 pad_maximum_fusion
  35.8 1.4 all_to_all.15
  37.2 14.8 %all-to-all-start = ((f32[32,1,6144]{2,1,0:T(1,128)}), f32[32,1,6144]{2,1,0:T(1,128)S(1)}, u32[]{:S(2)}, u32[]{:S(2)}) async-start(f32[32,1,6144]{2,1,0:T(1,128)} %all_to_all.15), calls=%async_computation | async-start | bytes 1572864 | tf_op jit(solution)/shard_map/all_to_all | solution.py:228
  52.0 0.1 broadcast_select_fusion.17
  52.1 0.0 copy-start.7
  52.1 0.0 copy-start
  52.2 0.0 copy-start.1
  52.2 0.1 pad_maximum_fusion.4
  52.2 0.6 copy-done.7
  52.8 4.1 %collective-permute-start.4 = (f32[8,8192]{1,0:T(8,128)S(1)}, f32[8,8192]{1,0:T(8,128)}, u32[]{:S(2)}, u32[]{:S(2)}) collective-permute-start(f32[8,8192]{1,0:T(8,128)S(1)} %pad_maximum_fusion.4), channel_id=1, source_target_pairs={{0,32},{32,0},{1,33},{33,1},{2,34},{34,2},{3,35},{35,3},{4,36},{36... | collective-permute-start | bytes 786440 | tf_op jit(solution)/shard_map/ppermute | solution.py:203
  56.9 0.0 copy-start.8
  56.9 0.6 root_tables.1
  57.5 0.6 collective-permute-done.4
  58.1 1.0 broadcast_select_fusion.2
  59.2 0.7 copy-done.5
  59.9 0.7 broadcast_select_fusion.8
  60.6 3.5 %collective-permute-start.5 = (f32[16,4096]{1,0:T(8,128)}, f32[16,4096]{1,0:T(8,128)}, u32[]{:S(2)}, u32[]{:S(2)}) collective-permute-start(f32[16,4096]{1,0:T(8,128)} %broadcast_select_fusion.8), channel_id=1, source_target_pairs={{0,1},{1,0},{2,3},{3,2},{4,5},{5,4},{6,7},{7,6},{8,9},{9,8},{10,11... | collective-permute-start | bytes 786440 | tf_op jit(solution)/shard_map/ppermute | solution.py:251
  64.2 25.6 %all-to-all-done = f32[32,1,6144]{2,1,0:T(1,128)S(1)} async-done(((f32[32,1,6144]{2,1,0:T(1,128)}), f32[32,1,6144]{2,1,0:T(1,128)S(1)}, u32[]{:S(2)}, u32[]{:S(2)}) %all-to-all-start) | async-done | bytes 786464 | tf_op jit(solution)/shard_map/all_to_all | solution.py:228
  89.8 0.2 copy.25
  90.1 2.0 %forward.1 = (f32[32,4096]{1,0:T(8,128)S(1)}, f32[32,4096]{1,0:T(8,128)S(1)}) custom-call(f32[32,6144]{1,0:T(8,128)S(1)} %bitcast.17, bf16[64,96]{1,0:T(8,128)(2,1)S(1)} %copy-done.4, f32[2,32,1024]{2,1,0:T(8,128)S(1)} %copy-done.2, bf16[1024,256]{1,0:T(8,128)(2,1)S(1)} %get-tuple-element.9.cos_hi, bf16[1024,256]{1,0:T(8,128)(2,1)S(1)} %get-tuple-element.10.cos_lo, ...), custom_call_target="tpu_custom_call" | custom-call | flops 2000000000 | bytes 10000000 | tf_op jit(solution)/shard_map/forward/pallas_call | solution.py:264
  92.1 2.2 %collective-permute-start.6 = (f32[16,4096]{1,0:T(8,128)S(1)}, f32[16,4096]{1,0:T(8,128)S(1)}, u32[]{:S(2)}, u32[]{:S(2)}) collective-permute-start(f32[16,4096]{1,0:T(8,128)S(1)} %slice_select_fusion.1), channel_id=1, source_target_pairs={{0,1},{1,0},{2,3},{3,2},{4,5},{5,4},{6,7},{7,6},{8,9},{9,8},{10,11... | collective-permute-start | bytes 786440 | tf_op jit(solution)/shard_map/ppermute | solution.py:286
  94.4 0.0 collective-permute-done.5
  94.4 1.0 broadcast_select_fusion.6
  95.4 4.0 %collective-permute-done.6 = f32[16,4096]{1,0:T(8,128)S(1)} collective-permute-done((f32[16,4096]{1,0:T(8,128)S(1)}, f32[16,4096]{1,0:T(8,128)S(1)}, u32[]{:S(2)}, u32[]{:S(2)}) %collective-permute-start.6) | collective-permute-done | bytes 262176 | tf_op jit(solution)/shard_map/ppermute | solution.py:286
  99.4 0.1 broadcast_select_fusion.4
  99.5 7.2 %collective-permute-start.7 = (f32[8,8192]{1,0:T(8,128)S(1)}, f32[8,8192]{1,0:T(8,128)S(1)}, u32[]{:S(2)}, u32[]{:S(2)}) collective-permute-start(f32[8,8192]{1,0:T(8,128)S(1)} %broadcast_select_fusion), channel_id=1, source_target_pairs={{0,32},{32,0},{1,33},{33,1},{2,34},{34,2},{3,35},{35,3},{4,36},{36... | collective-permute-start | bytes 786440 | tf_op jit(solution)/shard_map/ppermute | solution.py:199
  106.7 0.0 copy-start.3
  106.7 0.7 copy-done.3
  107.4 2.0 %inverse.2 = f32[32,2048]{1,0:T(8,128)S(1)} custom-call(f32[32,6144]{1,0:T(8,128)S(1)} %bitcast.18, f32[32,4096]{1,0:T(8,128)S(1)} %pad_maximum_fusion.1.filt_ref, bf16[32,192]{1,0:T(8,128)(2,1)S(1)} %copy-done.3, f32[2,32,1024]{2,1,0:T(8,128)S(1)} %copy-done.2, bf16[1024,256]{1,0:T(8,128)(2,1)S(1)} %get-tuple-element.9.cos_hi, ...), custom_call_target="tpu_custom_call" | custom-call | flops 2000000000 | bytes 10000000 | tf_op jit(solution)/shard_map/inverse/pallas_call | solution.py:274
  109.5 3.4 %collective-permute-start.8 = (f32[4,8192]{1,0:T(4,128)S(1)}, f32[4,8192]{1,0:T(4,128)S(1)}, u32[]{:S(2)}, u32[]{:S(2)}) collective-permute-start(f32[4,8192]{1,0:T(4,128)S(1)} %slice_select_fusion.2), channel_id=1, source_target_pairs={{0,64},{64,0},{128,192},{192,128},{1,65},{65,1},{129,193},{193,129... | collective-permute-start | bytes 393224 | tf_op jit(solution)/shard_map/ppermute | solution.py:199
  112.9 2.1 %inverse.3 = f32[32,2048]{1,0:T(8,128)S(1)} custom-call(f32[32,4096]{1,0:T(8,128)S(1)} %get-tuple-element.13.first_ref, f32[32,4096]{1,0:T(8,128)S(1)} %pad_maximum_fusion.1.filt_ref, bf16[32,192]{1,0:T(8,128)(2,1)S(1)} %copy-done.3, f32[2,32,1024]{2,1,0:T(8,128)S(1)} %copy-done.2, bf16[1024,256]{1,0:T(8,128)(2,1)S(1)} %get-tuple-element.9.cos_hi, ...), custom_call_target="tpu_custom_call" | custom-call | flops 2000000000 | bytes 10000000 | tf_op jit(solution)/shard_map/inverse/pallas_call | solution.py:274
  115.0 1.5 collective-permute-done.8
  116.6 4.1 %collective-permute-start.9 = (f32[2,8192]{1,0:T(2,128)S(1)}, f32[2,8192]{1,0:T(2,128)S(1)}, u32[]{:S(2)}, u32[]{:S(2)}) collective-permute-start(f32[2,8192]{1,0:T(2,128)S(1)} %broadcast_select_fusion.13), channel_id=1, source_target_pairs={{0,128},{64,192},{128,0},{192,64},{1,129},{65,193},{129,1},{193,65... | collective-permute-start | bytes 196616 | tf_op jit(solution)/shard_map/ppermute | solution.py:199
  120.7 1.3 copy.17
  122.1 7.1 %all-to-all-start.1 = ((f32[32,1,4096]{2,1,0:T(1,128)}), f32[32,1,4096]{2,1,0:T(1,128)S(1)}, u32[]{:S(2)}, u32[]{:S(2)}) async-start(f32[32,1,4096]{2,1,0:T(1,128)} %copy.17), calls=%async_computation.1 | async-start | bytes 1048576 | tf_op jit(solution)/shard_map/all_to_all | solution.py:296
  129.2 0.1 select_add_fusion.2
  129.3 10.0 %collective-permute-start.11 = (f32[1,8192]{1,0:T(1,128)S(1)}, f32[1,8192]{1,0:T(1,128)S(1)}, u32[]{:S(2)}, u32[]{:S(2)}) collective-permute-start(f32[1,8192]{1,0:T(1,128)S(1)} %get-tuple-element.27), channel_id=1, source_target_pairs={{256,0},{0,1},{384,2},{128,3},{320,4},{64,5},{448,6},{192,7},{288,... | collective-permute-start | bytes 98312 | tf_op jit(solution)/shard_map/ppermute | solution.py:304
  139.4 2.2 %collective-permute-start.10 = (f32[1,8192]{1,0:T(1,128)S(1)}, f32[1,8192]{1,0:T(1,128)S(1)}, u32[]{:S(2)}, u32[]{:S(2)}) collective-permute-start(f32[1,8192]{1,0:T(1,128)S(1)} %get-tuple-element.28), channel_id=1, source_target_pairs={{0,0},{256,1},{128,2},{384,3},{64,4},{320,5},{192,6},{448,7},{32,8... | collective-permute-start | bytes 98312 | tf_op jit(solution)/shard_map/ppermute | solution.py:304
  141.6 20.6 %collective-permute-done.11 = f32[1,8192]{1,0:T(1,128)S(1)} collective-permute-done((f32[1,8192]{1,0:T(1,128)S(1)}, f32[1,8192]{1,0:T(1,128)S(1)}, u32[]{:S(2)}, u32[]{:S(2)}) %collective-permute-start.11) | collective-permute-done | bytes 32800 | tf_op jit(solution)/shard_map/ppermute | solution.py:304
  162.2 0.1 add_reduce_fusion
  162.3 0.6 reshape.72
  163.0 0.3 copy.26
  163.4 0.0 copy-start.11
  163.4 0.8 copy-done.11
  164.3 0.7 fusion
  164.9 0.7 convert_element_type.26
  (35 shorter events, 0.6 us)
Async XLA Ops:
  1.5 20.7 %collective-permute-start.1 = (f32[1,8192]{1,0:T(1,128)S(1)}, f32[1,8192]{1,0:T(1,128)S(1)}, u32[]{:S(2)}, u32[]{:S(2)}) collective-permute-start(f32[1,8192]{1,0:T(1,128)S(1)} %reshape.70), channel_id=1, source_target_pairs={{0,0},{1,256},{2,128},{3,384},{4,64},{5,320},{6,192},{7,448},{8,32... | collective-permute-start | bytes 98312 | tf_op jit(solution)/shard_map/ppermute | solution.py:242
  10.9 14.7 %collective-permute-start = (f32[1,8192]{1,0:T(1,128)S(1)}, f32[1,8192]{1,0:T(1,128)S(1)}, u32[]{:S(2)}, u32[]{:S(2)}) collective-permute-start(f32[1,8192]{1,0:T(1,128)S(1)} %reshape.70), channel_id=1, source_target_pairs={{0,256},{1,0},{2,384},{3,128},{4,320},{5,64},{6,448},{7,192},{8,28... | collective-permute-start | bytes 98312 | tf_op jit(solution)/shard_map/ppermute | solution.py:242
  22.1 5.7 %copy-start.10 = (bf16[1,64,1024]{2,1,0:T(8,128)(2,1)S(1)}, bf16[1,64,1024]{2,1,0:T(8,128)(2,1)}, u32[]{:S(2)}) copy-start(bf16[1,64,1024]{2,1,0:T(8,128)(2,1)} %param.9) | copy-start | bytes 393220
  22.1 5.7 %copy-start.12 = (bf16[1,64,1024]{2,1,0:T(8,128)(2,1)S(1)}, bf16[1,64,1024]{2,1,0:T(8,128)(2,1)}, u32[]{:S(2)}) copy-start(bf16[1,64,1024]{2,1,0:T(8,128)(2,1)} %param.10) | copy-start | bytes 393220
  25.7 2.2 %copy-start.9 = (f32[1,2,64,1024]{3,2,1,0:T(8,128)S(1)}, f32[1,2,64,1024]{3,2,1,0:T(8,128)}, u32[]{:S(2)}) copy-start(f32[1,2,64,1024]{3,2,1,0:T(8,128)} %param.11) | copy-start | bytes 1572868
  25.7 6.6 %collective-permute-start.2 = (f32[2,8192]{1,0:T(2,128)S(1)}, f32[2,8192]{1,0:T(2,128)S(1)}, u32[]{:S(2)}, u32[]{:S(2)}) collective-permute-start(f32[2,8192]{1,0:T(2,128)S(1)} %pad_maximum_fusion.6), channel_id=1, source_target_pairs={{0,128},{64,192},{128,0},{192,64},{1,129},{65,193},{129,1},{193,65... | collective-permute-start | bytes 196616 | tf_op jit(solution)/shard_map/ppermute | solution.py:203
  32.5 19.5 %collective-permute-start.3 = (f32[4,8192]{1,0:T(4,128)S(1)}, f32[4,8192]{1,0:T(4,128)S(1)}, u32[]{:S(2)}, u32[]{:S(2)}) collective-permute-start(f32[4,8192]{1,0:T(4,128)S(1)} %pad_maximum_fusion.5), channel_id=1, source_target_pairs={{0,64},{64,0},{128,192},{192,128},{1,65},{65,1},{129,193},{193,129... | collective-permute-start | bytes 393224 | tf_op jit(solution)/shard_map/ppermute | solution.py:203
  37.2 52.6 %all-to-all-start = ((f32[32,1,6144]{2,1,0:T(1,128)}), f32[32,1,6144]{2,1,0:T(1,128)S(1)}, u32[]{:S(2)}, u32[]{:S(2)}) async-start(f32[32,1,6144]{2,1,0:T(1,128)} %all_to_all.15), calls=%async_computation | async-start | bytes 1572864 | tf_op jit(solution)/shard_map/all_to_all | solution.py:228
  52.1 0.7 copy-start.7
  52.1 4.7 %copy-start = (f32[2,32,256]{2,1,0:T(8,128)S(1)}, f32[2,32,256]{2,1,0:T(8,128)}, u32[]{:S(2)}) copy-start(f32[2,32,256]{2,1,0:T(8,128)} %constant.58.clone.fine_ref) | copy-start | bytes 196612
  52.2 4.7 %copy-start.1 = (f32[2,32,256]{2,1,0:T(8,128)S(1)}, f32[2,32,256]{2,1,0:T(8,128)}, u32[]{:S(2)}) copy-start(f32[2,32,256]{2,1,0:T(8,128)} %constant.57.clone.coarse_ref) | copy-start | bytes 196612
  52.8 5.4 %collective-permute-start.4 = (f32[8,8192]{1,0:T(8,128)S(1)}, f32[8,8192]{1,0:T(8,128)}, u32[]{:S(2)}, u32[]{:S(2)}) collective-permute-start(f32[8,8192]{1,0:T(8,128)S(1)} %pad_maximum_fusion.4), channel_id=1, source_target_pairs={{0,32},{32,0},{1,33},{33,1},{2,34},{34,2},{3,35},{35,3},{4,36},{36... | collective-permute-start | bytes 786440 | tf_op jit(solution)/shard_map/ppermute | solution.py:203
  56.9 1.2 copy-start.8
  59.2 0.7 copy-start.5
  60.6 29.4 %copy-start.2 = (f32[2,32,1024]{2,1,0:T(8,128)S(1)}, f32[2,32,1024]{2,1,0:T(8,128)}, u32[]{:S(2)}) copy-start(f32[2,32,1024]{2,1,0:T(8,128)} %constant.61.clone.twiddle_ref) | copy-start | bytes 786436
  60.6 29.4 %copy-start.4 = (bf16[64,96]{1,0:T(8,128)(2,1)S(1)}, bf16[64,96]{1,0:T(8,128)(2,1)}, u32[]{:S(2)}) copy-start(bf16[64,96]{1,0:T(8,128)(2,1)} %constant.59.clone.small_ref) | copy-start | bytes 36868
  60.6 33.7 %collective-permute-start.5 = (f32[16,4096]{1,0:T(8,128)}, f32[16,4096]{1,0:T(8,128)}, u32[]{:S(2)}, u32[]{:S(2)}) collective-permute-start(f32[16,4096]{1,0:T(8,128)} %broadcast_select_fusion.8), channel_id=1, source_target_pairs={{0,1},{1,0},{2,3},{3,2},{4,5},{5,4},{6,7},{7,6},{8,9},{9,8},{10,11... | collective-permute-start | bytes 786440 | tf_op jit(solution)/shard_map/ppermute | solution.py:251
  92.1 2.3 %copy-start.6 = (f32[8,8192]{1,0:T(8,128)S(1)}, f32[8,8192]{1,0:T(8,128)}, u32[]{:S(2)}) copy-start(f32[8,8192]{1,0:T(8,128)} %copy-done.5) | copy-start | bytes 786436
  92.1 7.2 %collective-permute-start.6 = (f32[16,4096]{1,0:T(8,128)S(1)}, f32[16,4096]{1,0:T(8,128)S(1)}, u32[]{:S(2)}, u32[]{:S(2)}) collective-permute-start(f32[16,4096]{1,0:T(8,128)S(1)} %slice_select_fusion.1), channel_id=1, source_target_pairs={{0,1},{1,0},{2,3},{3,2},{4,5},{5,4},{6,7},{7,6},{8,9},{9,8},{10,11... | collective-permute-start | bytes 786440 | tf_op jit(solution)/shard_map/ppermute | solution.py:286
  99.5 10.0 %collective-permute-start.7 = (f32[8,8192]{1,0:T(8,128)S(1)}, f32[8,8192]{1,0:T(8,128)S(1)}, u32[]{:S(2)}, u32[]{:S(2)}) collective-permute-start(f32[8,8192]{1,0:T(8,128)S(1)} %broadcast_select_fusion), channel_id=1, source_target_pairs={{0,32},{32,0},{1,33},{33,1},{2,34},{34,2},{3,35},{35,3},{4,36},{36... | collective-permute-start | bytes 786440 | tf_op jit(solution)/shard_map/ppermute | solution.py:199
  106.7 0.7 copy-start.3
  109.5 6.9 %collective-permute-start.8 = (f32[4,8192]{1,0:T(4,128)S(1)}, f32[4,8192]{1,0:T(4,128)S(1)}, u32[]{:S(2)}, u32[]{:S(2)}) collective-permute-start(f32[4,8192]{1,0:T(4,128)S(1)} %slice_select_fusion.2), channel_id=1, source_target_pairs={{0,64},{64,0},{128,192},{192,128},{1,65},{65,1},{129,193},{193,129... | collective-permute-start | bytes 393224 | tf_op jit(solution)/shard_map/ppermute | solution.py:199
  116.6 12.6 %collective-permute-start.9 = (f32[2,8192]{1,0:T(2,128)S(1)}, f32[2,8192]{1,0:T(2,128)S(1)}, u32[]{:S(2)}, u32[]{:S(2)}) collective-permute-start(f32[2,8192]{1,0:T(2,128)S(1)} %broadcast_select_fusion.13), channel_id=1, source_target_pairs={{0,128},{64,192},{128,0},{192,64},{1,129},{65,193},{129,1},{193,65... | collective-permute-start | bytes 196616 | tf_op jit(solution)/shard_map/ppermute | solution.py:199
  122.1 40.9 %all-to-all-start.1 = ((f32[32,1,4096]{2,1,0:T(1,128)}), f32[32,1,4096]{2,1,0:T(1,128)S(1)}, u32[]{:S(2)}, u32[]{:S(2)}) async-start(f32[32,1,4096]{2,1,0:T(1,128)} %copy.17), calls=%async_computation.1 | async-start | bytes 1048576 | tf_op jit(solution)/shard_map/all_to_all | solution.py:296
  129.3 32.9 %collective-permute-start.11 = (f32[1,8192]{1,0:T(1,128)S(1)}, f32[1,8192]{1,0:T(1,128)S(1)}, u32[]{:S(2)}, u32[]{:S(2)}) collective-permute-start(f32[1,8192]{1,0:T(1,128)S(1)} %get-tuple-element.27), channel_id=1, source_target_pairs={{256,0},{0,1},{384,2},{128,3},{320,4},{64,5},{448,6},{192,7},{288,... | collective-permute-start | bytes 98312 | tf_op jit(solution)/shard_map/ppermute | solution.py:304
  139.4 22.9 %collective-permute-start.10 = (f32[1,8192]{1,0:T(1,128)S(1)}, f32[1,8192]{1,0:T(1,128)S(1)}, u32[]{:S(2)}, u32[]{:S(2)}) collective-permute-start(f32[1,8192]{1,0:T(1,128)S(1)} %get-tuple-element.28), channel_id=1, source_target_pairs={{0,0},{256,1},{128,2},{384,3},{64,4},{320,5},{192,6},{448,7},{32,8... | collective-permute-start | bytes 98312 | tf_op jit(solution)/shard_map/ppermute | solution.py:304
  163.4 0.9 copy-start.11

commit v3 on v2

--- a/solution.py
+++ b/solution.py
@@ -1,4 +1,3 @@
-import functools
 import math
 
 import jax
@@ -104,12 +103,30 @@
     return both[:rows] + both[rows:] + dot16(high_low[:rows], lo_ref[...])
 
 
+def pack_kernel(out_ref, gate_ref, spec_ref, packed_ref, rows_ref):
+    points = out_ref.shape[2]
+    count = packed_ref.shape[0]
+    for source in range(3):
+        for start in range(0, points, 128):
+            cut = slice(start, start + 128)
+            slot = source * (points // 128) + start // 128
+            if source == 2:
+                rows_ref[slot] = out_ref[0, :, cut].astype(f32) * gate_ref[0, :, cut].astype(f32)
+            else:
+                rows_ref[slot] = spec_ref[0, source, :, cut]
+            for channel in range(2):
+                at = (2 * source + channel) * points + start
+                packed_ref[:, 0, at : at + 128] = rows_ref[slot, pl.ds(channel, count, stride=2), :]
+
+
 def forward_kernel(
-    moved_ref, small_ref, twiddle_ref, cos_hi, cos_lo, sin_hi, sin_lo, spec_ref, terms_ref, rows_ref
+    odd_ref, moved_ref, small_ref, twiddle_ref, cos_hi, cos_lo, sin_hi, sin_lo, spec_ref, mine_ref,
+    away_ref, rows_ref,
 ):
     classes = moved_ref.shape[0]
     points = cos_hi.shape[0]
     scale = 1.0 / math.sqrt(classes * points)
+    odd = odd_ref[0] == 1
     tw_cos, tw_sin = twiddle_ref[0] * scale, twiddle_ref[1] * scale
     for channel in range(2):
         delta = moved_ref[:, (4 + channel) * points : (5 + channel) * points]
@@ -133,21 +150,31 @@
             in_real, in_imag = moved_ref[:, put_real], moved_ref[:, put_imag]
             spec_ref[:, put_real] = real[mine]
             spec_ref[:, put_imag] = imag[mine]
-            terms_ref[:, put_real] = in_real * real[mine] + in_imag * imag[mine]
-            terms_ref[:, put_imag] = in_real * imag[mine] - in_imag * real[mine]
-
-
-def inverse_kernel(
-    sign, first_ref, filt_ref, small_ref, twiddle_ref, cos_hi, cos_lo, sin_hi, sin_lo, out_ref,
-    rows_ref, turned_ref,
+            term_real = in_real * real[mine] + in_imag * imag[mine]
+            term_imag = in_real * imag[mine] - in_imag * real[mine]
+            for put, term in ((put_real, term_real), (put_imag, term_imag)):
+                lower, upper = term[: classes // 2], term[classes // 2 :]
+                mine_ref[:, put] = jnp.where(odd, upper, lower)
+                away_ref[:, put] = jnp.where(odd, lower, upper)
+
+
+def inverse_rows(
+    sign, odd_ref, first_ref, mine_ref, other_ref, small_ref, twiddle_ref, tables, rows_ref,
+    turned_ref,
 ):
+    cos_hi, cos_lo, sin_hi, sin_lo = tables
     classes = first_ref.shape[0]
     points = cos_hi.shape[0]
+    odd = odd_ref[0] == 1
+
+    def filt(at):
+        mine, other = mine_ref[:, at], other_ref[:, at]
+        return jnp.concatenate([jnp.where(odd, other, mine), jnp.where(odd, mine, other)], axis=0)
 
     for channel in range(2):
         real_at = slice(channel * points, (channel + 1) * points)
         imag_at = slice((2 + channel) * points, (3 + channel) * points)
-        filt_real, filt_imag = filt_ref[:, real_at], filt_ref[:, imag_at] * sign
+        filt_real, filt_imag = filt(real_at), filt(imag_at) * sign
         first_real, first_imag = first_ref[:, real_at], first_ref[:, imag_at]
         keep_quarters(
             rows_ref,
@@ -176,7 +203,31 @@
                 high, low = halves(turned)
                 for place, values in ((part, high), (2 + part, low), (4 + part, high)):
                     turned_ref[place * classes : (place + 1) * classes, put] = values
-    out_ref[...] = dot16(small_ref[...], turned_ref[...])
+    return dot16(small_ref[...], turned_ref[...])
+
+
+def conv_kernel(
+    odd_ref, moved_ref, mine_ref, other_ref, small_ref, twiddle_ref, cos_hi, cos_lo, sin_hi, sin_lo,
+    conv_ref, rows_ref, turned_ref,
+):
+    tables = (cos_hi, cos_lo, sin_hi, sin_lo)
+    conv_ref[...] = inverse_rows(
+        1.0, odd_ref, moved_ref, mine_ref, other_ref, small_ref, twiddle_ref, tables, rows_ref,
+        turned_ref,
+    )
+
+
+def back_kernel(
+    odd_ref, conv_ref, spec_ref, mine_ref, other_ref, small_ref, twiddle_ref, cos_hi, cos_lo,
+    sin_hi, sin_lo, packed_ref, rows_ref, turned_ref,
+):
+    tables = (cos_hi, cos_lo, sin_hi, sin_lo)
+    width = conv_ref.shape[1]
+    packed_ref[:, 0, :width] = conv_ref[...]
+    packed_ref[:, 0, width:] = inverse_rows(
+        -1.0, odd_ref, spec_ref, mine_ref, other_ref, small_ref, twiddle_ref, tables, rows_ref,
+        turned_ref,
+    )
 
 
 def staging_pairs(x_count, core_count, seq_count):
@@ -192,10 +243,14 @@
     return pairs
 
 
+def kept_and_away(values, upper):
+    half = values.shape[1] // 2
+    lower, higher = values[:, :half], values[:, half:]
+    return jnp.where(upper, higher, lower), jnp.where(upper, lower, higher)
+
+
 def halving(values, upper, axis, pairs):
-    rows = values.shape[0] // 2
-    kept = jnp.where(upper, values[rows:], values[:rows])
-    away = jnp.where(upper, values[:rows], values[rows:])
+    kept, away = kept_and_away(values, upper)
     return kept + lax.ppermute(away, axis, pairs)
 
 
@@ -218,16 +273,17 @@
     pairs = staging_pairs(x_count, 2, seq_count)
     per_seq = channels // seq_count
 
-    upstream = grad_out.astype(f32)
-    delta = (upstream * gate.astype(f32)).reshape(seq_count, per_seq * positions)
-    spectrum = (
-        input_spectrum.reshape(2, seq_count, per_seq, positions)
-        .transpose(1, 0, 2, 3)
-        .reshape(seq_count, 2 * per_seq * positions)
-    )
-    moved = lax.all_to_all(
-        jnp.concatenate([spectrum, delta], axis=1), SEQ, split_axis=0, concat_axis=0, tiled=True
-    )
+    params = pltpu.CompilerParams(vmem_limit_bytes=16 * MIB)
+    packed = pl.pallas_call(
+        pack_kernel,
+        out_shape=jax.ShapeDtypeStruct((seq_count, 1, 3 * per_seq * positions), f32),
+        scratch_shapes=[pltpu.VMEM((3 * positions // 128, channels, 128), f32)],
+        name="pack",
+        compiler_params=params,
+        cost_estimate=pl.CostEstimate(flops=10**5, bytes_accessed=2 * 10**6, transcendentals=0),
+    )(grad_out, gate, input_spectrum)
+    moved = lax.all_to_all(packed, SEQ, split_axis=0, concat_axis=0, tiled=True)
+    moved = moved.reshape(seq_count, 3 * per_seq * positions)
 
     near_x = [(x, x ^ 1) for x in range(x_count)]
     far_x = [(x, x ^ 2) for x in range(x_count)]
@@ -248,58 +304,64 @@
     filters = doubling(filters, upper_core, "core", cores)
     mine = jnp.where(odd, filters[:, half_row:], filters[:, :half_row])
     away = jnp.where(odd, filters[:, :half_row], filters[:, half_row:])
-    other = lax.ppermute(away, "y", near_y)
-    filters = jnp.concatenate([jnp.where(odd, other, mine), jnp.where(odd, mine, other)], axis=0)
+    filters = (mine, lax.ppermute(away, "y", near_y))
 
     tables = root_tables(positions)
     small_out = small_table(seq_count, False)
     small_back = small_table(seq_count, True)
     twiddle = jnp.asarray(np.stack(unit_roots(seq_count, positions, seq_count * positions)))
 
-    wide = jax.ShapeDtypeStruct((seq_count, 4 * positions), f32)
-    signal = jax.ShapeDtypeStruct((seq_count, 2 * positions), f32)
+    half = seq_count // 2
+    parity = odd.astype(jnp.int32).reshape(1)
+    wide = jax.ShapeDtypeStruct((seq_count, half_row), f32)
+    narrow = jax.ShapeDtypeStruct((half, half_row), f32)
     rows = [pltpu.VMEM((4, 8 * seq_count, positions), bf16)]
-    params = pltpu.CompilerParams(vmem_limit_bytes=16 * MIB)
+    turned = [pltpu.VMEM((6 * seq_count, 2 * positions), bf16)]
     cost = pl.CostEstimate(flops=2 * 10**9, bytes_accessed=10**7, transcendentals=0)
-    spec, terms = pl.pallas_call(
+
+    def specs(count):
+        return [pl.BlockSpec(memory_space=pltpu.SMEM)] + [
+            pl.BlockSpec(memory_space=pltpu.VMEM) for _ in range(count)
+        ]
+
+    spec, mine, away = pl.pallas_call(
         forward_kernel,
-        out_shape=[wide, wide],
+        out_shape=[wide, narrow, narrow],
+        in_specs=specs(7),
         scratch_shapes=rows,
         name="forward",
         compiler_params=params,
         cost_estimate=cost,
-    )(moved, small_out, twiddle, *tables)
-
-    def inverse(sign, first):
-        return pl.pallas_call(
-            functools.partial(inverse_kernel, sign),
-            out_shape=signal,
-            scratch_shapes=rows + [pltpu.VMEM((6 * seq_count, 2 * positions), bf16)],
-            name="inverse",
-            compiler_params=params,
-            cost_estimate=cost,
-        )(first, filters, small_back, twiddle, *tables)
-
-    half = seq_count // 2
-    mine = jnp.where(odd, terms[half:], terms[:half])
-    away = jnp.where(odd, terms[:half], terms[half:])
+    )(parity, moved, small_out, twiddle, *tables)
+
     other = lax.ppermute(away, "y", near_y)
-    total = jnp.concatenate(
-        [jnp.where(odd, other, mine), jnp.where(odd, mine, other)], axis=1
-    )
-    total = halving(total, upper_core, "core", cores)
+    total = halving(jnp.stack([mine, other]), upper_core, "core", cores)
     total = halving(total, x_index % 2 == 1, "x", near_x)
     total = halving(total, x_index >= 2, "x", far_x)
 
-    conv = inverse(1.0, moved)
-    back = inverse(-1.0, spec)
-    returned = lax.all_to_all(
-        jnp.concatenate([conv, back], axis=1), SEQ, split_axis=0, concat_axis=0, tiled=True
-    )
-
-    rows_out = [
-        jnp.where(upper_zhi, total[1 - n : 2 - n], total[n : n + 1]) for n in range(2)
-    ]
+    conv = pl.pallas_call(
+        conv_kernel,
+        out_shape=jax.ShapeDtypeStruct((seq_count, 2 * positions), f32),
+        in_specs=specs(9),
+        scratch_shapes=rows + turned,
+        name="conv",
+        compiler_params=params,
+        cost_estimate=cost,
+    )(parity, moved, *filters, small_back, twiddle, *tables)
+    signals = pl.pallas_call(
+        back_kernel,
+        out_shape=jax.ShapeDtypeStruct((seq_count, 1, 4 * positions), f32),
+        in_specs=specs(10),
+        scratch_shapes=rows + turned,
+        name="back",
+        compiler_params=params,
+        cost_estimate=cost,
+    )(parity, conv, spec, *filters, small_back, twiddle, *tables)
+    returned = lax.all_to_all(signals, SEQ, split_axis=0, concat_axis=0, tiled=True)
+    returned = returned.reshape(seq_count, 4 * positions)
+
+    ordered = jnp.where(odd, total[::-1], total)
+    rows_out = [jnp.where(upper_zhi, ordered[:, 1 - n], ordered[:, n]) for n in range(2)]
     ends = [
         lax.ppermute(rows_out[number], everyone, [(b, a) for a, b in pairs[number]])
         for number in range(2)
@@ -314,7 +376,7 @@
     scale = 1.0 / math.sqrt(seq_count * positions)
     conv = returned[:, : per_seq * positions].reshape(1, channels, positions) * scale
     backward = returned[:, per_seq * positions :].reshape(1, channels, positions) * scale
-    grad_gate = (upstream * conv).astype(bf16)
+    grad_gate = (grad_out.astype(f32) * conv).astype(bf16)
     return (backward.astype(bf16), grad_gate, grad_filter)
 
 

time: 166 us -> 166 us (level)
  waiting for transfers between devices: 59.4 us -> 69.7 us
  starting transfers between devices: 84.5 us -> 77.7 us
  local copies, waits for them, and re-layouts: 9.32 us -> 3.95 us
  Pallas kernels: 6.74 us -> 9.05 us
    all_to_all x2, starting transfers between devices: 21.9 us -> 16.8 us  [the longest x1 9.5 us: step(): moved = lax.all_to_all(packed, SEQ, split_axis=0, concat_axis=0, tiled=True)]
    ppermute x0 -> x1, waiting for transfers between devices: none -> 5 us  [step(): filters = (mine, lax.ppermute(away, 'y', near_y))]
    ppermute x2, waiting for transfers between devices: 3.43 us -> 6.39 us  [step(): got = [lax.ppermute(sent, everyone, pairs[number]) for number in range(2)]]
    all_to_all x2 -> x0, local copies, waits for them, and re-layouts: 2.76 us -> none  [the longest x1 1.43 us: step(): lax.all_to_all(jnp.concatenate([spectrum, delta], axis=1), SEQ, split_axi...]
    ppermute x0 -> x1, starting transfers between devices: none -> 2.69 us  [step(): filters = (mine, lax.ppermute(away, 'y', near_y))]
    ppermute x2 -> x1, starting transfers between devices: 5.75 us -> 3.09 us  [step(): other = lax.ppermute(away, 'y', near_y)]
    ppermute x3, starting transfers between devices: 14.6 us -> 12.1 us  [halving(): return kept + lax.ppermute(away, axis, pairs)]
    ppermute x3, starting transfers between devices: 9.33 us -> 6.9 us  [doubling(): other = lax.ppermute(values, axis, pairs)]
  transfers between devices with their start and end apart: 14 -> 14, of which waited for: 7 -> 7; matrix products, arithmetic and copies ran while one was open for 4% -> 2% of each run, Pallas kernels for 4% -> 5%
where the time goes in v3:
time: 166 us; the launch traced here: 165 us
  starting transfers between devices  77.7 us (47%)
  waiting for transfers between devices  69.7 us (42%)
  Pallas kernels  9.05 us (5%)
  local copies, waits for them, and re-layouts  3.95 us (2%)
  other arithmetic  3.33 us (2%)
    all_to_all x1, waiting for transfers between devices, step(): moved = lax.all_to_all(packed, SEQ, split_axis=0, concat_axis=0, tiled=True)  27.6 us
    ppermute x2, waiting for transfers between devices, step(): lax.ppermute(rows_out[number], everyone, [(b, a) for a, b in pairs[number]])  22.8 us
    ppermute x2, starting transfers between devices, step(): got = [lax.ppermute(sent, everyone, pairs[number]) for number in range(2)]  22.4 us
    ppermute x2, starting transfers between devices, step(): lax.ppermute(rows_out[number], everyone, [(b, a) for a, b in pairs[number]])  13.7 us
    ppermute x3, starting transfers between devices, halving(): return kept + lax.ppermute(away, axis, pairs)  12.1 us
    all_to_all x1, starting transfers between devices, step(): moved = lax.all_to_all(packed, SEQ, split_axis=0, concat_axis=0, tiled=True)  9.5 us
    all_to_all x1, starting transfers between devices, step(): lax.all_to_all(signals, SEQ, split_axis=0, concat_axis=0, tiled=True)  7.31 us
    ppermute x3, starting transfers between devices, doubling(): other = lax.ppermute(values, axis, pairs)  6.9 us
  transfers between devices with their start and end apart: 14, of which 7 were waited for; matrix products, arithmetic and copies ran while one was open for 2% of the time, Pallas kernels for 5%

profile of v3, /device:TPU:7, one launch (start us, length us, event | category | flops | bytes accessed | tf_op | source)
XLA Modules:
  0.0 164.9 jit_solution(11484686275708327885)
XLA Ops:
  0.6 0.8 reshape.71
  1.4 0.1 reshape.72
  1.5 17.2 %collective-permute-start = (f32[1,8192]{1,0:T(1,128)S(1)}, f32[1,8192]{1,0:T(1,128)S(1)}, u32[]{:S(2)}, u32[]{:S(2)}) collective-permute-start(f32[1,8192]{1,0:T(1,128)S(1)} %reshape.72), channel_id=1, source_target_pairs={{0,256},{1,0},{2,384},{3,128},{4,320},{5,64},{6,448},{7,192},{8,28... | collective-permute-start | bytes 98312 | tf_op jit(solution)/shard_map/ppermute | solution.py:298
  18.7 5.2 %collective-permute-start.1 = (f32[1,8192]{1,0:T(1,128)S(1)}, f32[1,8192]{1,0:T(1,128)S(1)}, u32[]{:S(2)}, u32[]{:S(2)}) collective-permute-start(f32[1,8192]{1,0:T(1,128)S(1)} %reshape.72), channel_id=1, source_target_pairs={{0,0},{1,256},{2,128},{3,384},{4,64},{5,320},{6,192},{7,448},{8,32... | collective-permute-start | bytes 98312 | tf_op jit(solution)/shard_map/ppermute | solution.py:298
  23.9 0.0 copy-start.1
  24.0 0.0 copy-start.2
  24.0 0.0 collective-permute-done
  24.0 6.4 %collective-permute-done.1 = f32[1,8192]{1,0:T(1,128)S(1)} collective-permute-done((f32[1,8192]{1,0:T(1,128)S(1)}, f32[1,8192]{1,0:T(1,128)S(1)}, u32[]{:S(2)}, u32[]{:S(2)}) %collective-permute-start.1) | collective-permute-done | bytes 32800 | tf_op jit(solution)/shard_map/ppermute | solution.py:298
  30.4 0.1 pad_maximum_fusion.4
  30.5 1.9 %collective-permute-start.2 = (f32[2,8192]{1,0:T(2,128)S(1)}, f32[2,8192]{1,0:T(2,128)S(1)}, u32[]{:S(2)}, u32[]{:S(2)}) collective-permute-start(f32[2,8192]{1,0:T(2,128)S(1)} %pad_maximum_fusion.4), channel_id=1, source_target_pairs={{0,128},{64,192},{128,0},{192,64},{1,129},{65,193},{129,1},{193,65... | collective-permute-start | bytes 196616 | tf_op jit(solution)/shard_map/ppermute | solution.py:258
  32.4 0.0 copy-start
  32.4 1.0 copy-done
  33.5 1.4 pack.1
  34.9 9.5 %all-to-all-start = ((f32[32,1,6144]{2,1,0:T(1,128)}), f32[32,1,6144]{2,1,0:T(1,128)S(1)}, u32[]{:S(2)}, u32[]{:S(2)}) async-start(f32[32,1,6144]{2,1,0:T(1,128)} %pack.1), calls=%async_computation | async-start | bytes 1572864 | tf_op jit(solution)/shard_map/all_to_all | solution.py:285
  44.4 0.0 collective-permute-done.2
  44.4 0.1 broadcast_select_fusion.10
  44.5 0.1 pad_maximum_fusion.3
  44.6 1.9 %collective-permute-start.3 = (f32[4,8192]{1,0:T(4,128)S(1)}, f32[4,8192]{1,0:T(4,128)S(1)}, u32[]{:S(2)}, u32[]{:S(2)}) collective-permute-start(f32[4,8192]{1,0:T(4,128)S(1)} %pad_maximum_fusion.3), channel_id=1, source_target_pairs={{0,64},{64,0},{128,192},{192,128},{1,65},{65,1},{129,193},{193,129... | collective-permute-start | bytes 393224 | tf_op jit(solution)/shard_map/ppermute | solution.py:258
  46.5 4.7 %collective-permute-done.3 = f32[4,8192]{1,0:T(4,128)S(1)} collective-permute-done((f32[4,8192]{1,0:T(4,128)S(1)}, f32[4,8192]{1,0:T(4,128)S(1)}, u32[]{:S(2)}, u32[]{:S(2)}) %collective-permute-start.3) | collective-permute-done | bytes 131104 | tf_op jit(solution)/shard_map/ppermute | solution.py:258
  51.2 0.1 broadcast_select_fusion.12
  51.3 0.0 copy-start.8
  51.3 0.0 copy-start.3
  51.4 0.0 copy-start.4
  51.4 0.8 pad_maximum_fusion.2
  52.1 3.1 %collective-permute-start.4 = (f32[8,8192]{1,0:T(8,128)}, f32[8,8192]{1,0:T(8,128)}, u32[]{:S(2)}, u32[]{:S(2)}) collective-permute-start(f32[8,8192]{1,0:T(8,128)} %pad_maximum_fusion.2), channel_id=1, source_target_pairs={{0,32},{32,0},{1,33},{33,1},{2,34},{34,2},{3,35},{35,3},{4,36},{36... | collective-permute-start | bytes 786440 | tf_op jit(solution)/shard_map/ppermute | solution.py:258
  55.2 0.0 copy-done.3
  55.2 0.0 copy-done.4
  55.2 0.6 root_tables.1
  55.9 0.0 copy-start.5
  55.9 0.0 copy-start.7
  55.9 27.6 %all-to-all-done = f32[32,1,6144]{2,1,0:T(1,128)S(1)} async-done(((f32[32,1,6144]{2,1,0:T(1,128)}), f32[32,1,6144]{2,1,0:T(1,128)S(1)}, u32[]{:S(2)}, u32[]{:S(2)}) %all-to-all-start) | async-done | bytes 786464 | tf_op jit(solution)/shard_map/all_to_all | solution.py:285
  83.5 0.2 copy.37
  83.8 0.0 copy-done.5
  83.8 0.0 copy-start.9
  83.8 2.1 %forward.1 = (f32[32,4096]{1,0:T(8,128)S(1)}, f32[16,4096]{1,0:T(8,128)S(1)}, f32[16,4096]{1,0:T(8,128)S(1)}) custom-call(s32[1]{0:T(128)} %bitcast.odd_ref, f32[32,6144]{1,0:T(8,128)S(1)} %bitcast.20, bf16[64,96]{1,0:T(8,128)(2,1)S(1)} %copy-done.7, f32[2,32,1024]{2,1,0:T(8,128)S(1)} %copy-done.5, bf16[1024,256]{1,0:T(8,128)(2,1)S(1)} %get-tuple-element.10.cos_hi, ...), custom_call_target="tpu_custom_call" | custom-call | flops 2000000000 | bytes 10000000 | tf_op jit(solution)/shard_map/forward/pallas_call | solution.py:327
  85.9 3.1 %collective-permute-start.6 = (f32[16,4096]{1,0:T(8,128)S(1)}, f32[16,4096]{1,0:T(8,128)S(1)}, u32[]{:S(2)}, u32[]{:S(2)}) collective-permute-start(f32[16,4096]{1,0:T(8,128)S(1)} %get-tuple-element.16), channel_id=1, source_target_pairs={{0,1},{1,0},{2,3},{3,2},{4,5},{5,4},{6,7},{7,6},{8,9},{9,8},{10,11... | collective-permute-start | bytes 786440 | tf_op jit(solution)/shard_map/ppermute | solution.py:337
  89.0 0.0 collective-permute-done.4
  89.0 1.0 broadcast_select_fusion.2
  90.0 3.1 %collective-permute-done.6 = f32[16,4096]{1,0:T(8,128)S(1)} collective-permute-done((f32[16,4096]{1,0:T(8,128)S(1)}, f32[16,4096]{1,0:T(8,128)S(1)}, u32[]{:S(2)}, u32[]{:S(2)}) %collective-permute-start.6) | collective-permute-done | bytes 262176 | tf_op jit(solution)/shard_map/ppermute | solution.py:337
  93.2 5.6 %collective-permute-start.7 = (f32[2,8,4096]{2,1,0:T(8,128)S(1)}, f32[2,8,4096]{2,1,0:T(8,128)S(1)}, u32[]{:S(2)}, u32[]{:S(2)}) collective-permute-start(f32[2,8,4096]{2,1,0:T(8,128)S(1)} %broadcast_select_fusion), channel_id=1, source_target_pairs={{0,32},{32,0},{1,33},{33,1},{2,34},{34,2},{3,35},{35,3},{4,36},{36... | collective-permute-start | bytes 786440 | tf_op jit(solution)/shard_map/ppermute | solution.py:254
  98.9 0.1 broadcast_select_fusion.3
  98.9 2.7 %collective-permute-start.5 = (f32[16,4096]{1,0:T(8,128)S(1)}, f32[16,4096]{1,0:T(8,128)S(1)}, u32[]{:S(2)}, u32[]{:S(2)}) collective-permute-start(f32[16,4096]{1,0:T(8,128)S(1)} %get-tuple-element.19), channel_id=1, source_target_pairs={{0,1},{1,0},{2,3},{3,2},{4,5},{5,4},{6,7},{7,6},{8,9},{9,8},{10,11... | collective-permute-start | bytes 786440 | tf_op jit(solution)/shard_map/ppermute | solution.py:307
  101.6 0.0 collective-permute-done.7
  101.6 0.1 select_add_fusion
  101.7 0.0 copy-start.6
  101.7 1.9 %collective-permute-start.8 = (f32[2,4,4096]{2,1,0:T(4,128)S(1)}, f32[2,4,4096]{2,1,0:T(4,128)S(1)}, u32[]{:S(2)}, u32[]{:S(2)}) collective-permute-start(f32[2,4,4096]{2,1,0:T(4,128)S(1)} %slice_select_fusion), channel_id=1, source_target_pairs={{0,64},{64,0},{128,192},{192,128},{1,65},{65,1},{129,193},{193,129... | collective-permute-start | bytes 393224 | tf_op jit(solution)/shard_map/ppermute | solution.py:254
  103.7 5.0 %collective-permute-done.5.other_ref = f32[16,4096]{1,0:T(8,128)S(1)} collective-permute-done((f32[16,4096]{1,0:T(8,128)S(1)}, f32[16,4096]{1,0:T(8,128)S(1)}, u32[]{:S(2)}, u32[]{:S(2)}) %collective-permute-start.5) | collective-permute-done | bytes 262176 | tf_op jit(solution)/shard_map/ppermute | solution.py:307
  108.7 2.1 %conv.1.conv_ref = f32[32,2048]{1,0:T(8,128)S(1)} custom-call(s32[1]{0:T(128)} %bitcast.odd_ref, f32[32,6144]{1,0:T(8,128)S(1)} %bitcast.21, f32[16,4096]{1,0:T(8,128)S(1)} %get-tuple-element.20.mine_ref, f32[16,4096]{1,0:T(8,128)S(1)} %collective-permute-done.5.other_ref, bf16[32,192]{1,0:T(8,128)(2,1)S(1)} %copy-done.6, f32[2,32,1024]{2,1,0:T(8,128)S(1)} %copy-done.5, ...), custom_call_target="tpu_custom_call" | custom-call | flops 2000000000 | bytes 10000000 | tf_op jit(solution)/shard_map/conv/pallas_call | solution.py:342
  110.7 0.0 collective-permute-done.8
  110.8 4.5 %collective-permute-start.9 = (f32[2,2,4096]{2,1,0:T(2,128)S(1)}, f32[2,2,4096]{2,1,0:T(2,128)S(1)}, u32[]{:S(2)}, u32[]{:S(2)}) collective-permute-start(f32[2,2,4096]{2,1,0:T(2,128)S(1)} %broadcast_select_fusion.6), channel_id=1, source_target_pairs={{0,128},{64,192},{128,0},{192,64},{1,129},{65,193},{129,1},{193,65... | collective-permute-start | bytes 196616 | tf_op jit(solution)/shard_map/ppermute | solution.py:254
  115.4 2.9 %back.1 = f32[32,1,4096]{2,1,0:T(1,128)} custom-call(s32[1]{0:T(128)} %bitcast.odd_ref, f32[32,2048]{1,0:T(8,128)S(1)} %conv.1.conv_ref, f32[32,4096]{1,0:T(8,128)S(1)} %get-tuple-element.14.spec_ref, f32[16,4096]{1,0:T(8,128)S(1)} %get-tuple-element.20.mine_ref, f32[16,4096]{1,0:T(8,128)S(1)} %collective-permute-done.5.other_ref, ...), custom_call_target="tpu_custom_call" | custom-call | flops 2000000000 | bytes 10000000 | tf_op jit(solution)/shard_map/back/pallas_call | solution.py:351
  118.2 7.3 %all-to-all-start.1 = ((f32[32,1,4096]{2,1,0:T(1,128)}), f32[32,1,4096]{2,1,0:T(1,128)S(1)}, u32[]{:S(2)}, u32[]{:S(2)}) async-start(f32[32,1,4096]{2,1,0:T(1,128)} %back.1), calls=%async_computation.1 | async-start | bytes 1048576 | tf_op jit(solution)/shard_map/all_to_all | solution.py:360
  125.5 0.0 collective-permute-done.9
  125.6 0.1 select_add_fusion.2
  125.7 0.1 broadcast_select_fusion.5
  125.8 7.5 %collective-permute-start.10 = (f32[2,4096]{1,0:T(2,128)S(1)}, f32[2,4096]{1,0:T(2,128)S(1)}, u32[]{:S(2)}, u32[]{:S(2)}) collective-permute-start(f32[2,4096]{1,0:T(2,128)S(1)} %fusion.3), channel_id=1, source_target_pairs={{0,0},{256,1},{128,2},{384,3},{64,4},{320,5},{192,6},{448,7},{32,8... | collective-permute-start | bytes 98312 | tf_op jit(solution)/shard_map/ppermute | solution.py:366
  133.3 6.3 %collective-permute-start.11 = (f32[2,4096]{1,0:T(2,128)S(1)}, f32[2,4096]{1,0:T(2,128)S(1)}, u32[]{:S(2)}, u32[]{:S(2)}) collective-permute-start(f32[2,4096]{1,0:T(2,128)S(1)} %bitcast.27), channel_id=1, source_target_pairs={{256,0},{0,1},{384,2},{128,3},{320,4},{64,5},{448,6},{192,7},{288,... | collective-permute-start | bytes 98312 | tf_op jit(solution)/shard_map/ppermute | solution.py:366
  139.6 4.6 %collective-permute-done.10 = f32[2,4096]{1,0:T(2,128)S(1)} collective-permute-done((f32[2,4096]{1,0:T(2,128)S(1)}, f32[2,4096]{1,0:T(2,128)S(1)}, u32[]{:S(2)}, u32[]{:S(2)}) %collective-permute-start.10) | collective-permute-done | bytes 32800 | tf_op jit(solution)/shard_map/ppermute | solution.py:366
  144.2 18.2 %collective-permute-done.11 = f32[2,4096]{1,0:T(2,128)S(1)} collective-permute-done((f32[2,4096]{1,0:T(2,128)S(1)}, f32[2,4096]{1,0:T(2,128)S(1)}, u32[]{:S(2)}, u32[]{:S(2)}) %collective-permute-start.11) | collective-permute-done | bytes 32800 | tf_op jit(solution)/shard_map/ppermute | solution.py:366
  162.5 0.6 reshape.75
  163.1 0.0 all-to-all-done.1
  163.1 0.3 copy.38
  163.5 0.7 multiply_convert_fusion
  164.2 0.7 convert_element_type.22
  (20 shorter events, 0.5 us)
Async XLA Ops:
  1.5 22.5 %collective-permute-start = (f32[1,8192]{1,0:T(1,128)S(1)}, f32[1,8192]{1,0:T(1,128)S(1)}, u32[]{:S(2)}, u32[]{:S(2)}) collective-permute-start(f32[1,8192]{1,0:T(1,128)S(1)} %reshape.72), channel_id=1, source_target_pairs={{0,256},{1,0},{2,384},{3,128},{4,320},{5,64},{6,448},{7,192},{8,28... | collective-permute-start | bytes 98312 | tf_op jit(solution)/shard_map/ppermute | solution.py:298
  18.7 11.6 %collective-permute-start.1 = (f32[1,8192]{1,0:T(1,128)S(1)}, f32[1,8192]{1,0:T(1,128)S(1)}, u32[]{:S(2)}, u32[]{:S(2)}) collective-permute-start(f32[1,8192]{1,0:T(1,128)S(1)} %reshape.72), channel_id=1, source_target_pairs={{0,0},{1,256},{2,128},{3,384},{4,64},{5,320},{6,192},{7,448},{8,32... | collective-permute-start | bytes 98312 | tf_op jit(solution)/shard_map/ppermute | solution.py:298
  23.9 8.5 %copy-start.1 = (bf16[1,64,1024]{2,1,0:T(8,128)(2,1)S(1)}, bf16[1,64,1024]{2,1,0:T(8,128)(2,1)}, u32[]{:S(2)}) copy-start(bf16[1,64,1024]{2,1,0:T(8,128)(2,1)} %out_ref.1) | copy-start | bytes 393220
  24.0 8.5 %copy-start.2 = (bf16[1,64,1024]{2,1,0:T(8,128)(2,1)S(1)}, bf16[1,64,1024]{2,1,0:T(8,128)(2,1)}, u32[]{:S(2)}) copy-start(bf16[1,64,1024]{2,1,0:T(8,128)(2,1)} %gate_ref.1) | copy-start | bytes 393220
  30.5 13.9 %collective-permute-start.2 = (f32[2,8192]{1,0:T(2,128)S(1)}, f32[2,8192]{1,0:T(2,128)S(1)}, u32[]{:S(2)}, u32[]{:S(2)}) collective-permute-start(f32[2,8192]{1,0:T(2,128)S(1)} %pad_maximum_fusion.4), channel_id=1, source_target_pairs={{0,128},{64,192},{128,0},{192,64},{1,129},{65,193},{129,1},{193,65... | collective-permute-start | bytes 196616 | tf_op jit(solution)/shard_map/ppermute | solution.py:258
  32.4 1.0 copy-start
  34.9 48.6 %all-to-all-start = ((f32[32,1,6144]{2,1,0:T(1,128)}), f32[32,1,6144]{2,1,0:T(1,128)S(1)}, u32[]{:S(2)}, u32[]{:S(2)}) async-start(f32[32,1,6144]{2,1,0:T(1,128)} %pack.1), calls=%async_computation | async-start | bytes 1572864 | tf_op jit(solution)/shard_map/all_to_all | solution.py:285
  44.6 6.6 %collective-permute-start.3 = (f32[4,8192]{1,0:T(4,128)S(1)}, f32[4,8192]{1,0:T(4,128)S(1)}, u32[]{:S(2)}, u32[]{:S(2)}) collective-permute-start(f32[4,8192]{1,0:T(4,128)S(1)} %pad_maximum_fusion.3), channel_id=1, source_target_pairs={{0,64},{64,0},{128,192},{192,128},{1,65},{65,1},{129,193},{193,129... | collective-permute-start | bytes 393224 | tf_op jit(solution)/shard_map/ppermute | solution.py:258
  51.3 0.8 copy-start.8
  51.3 3.9 %copy-start.3 = (f32[2,32,256]{2,1,0:T(8,128)S(1)}, f32[2,32,256]{2,1,0:T(8,128)}, u32[]{:S(2)}) copy-start(f32[2,32,256]{2,1,0:T(8,128)} %constant.57.clone.coarse_ref) | copy-start | bytes 196612
  51.4 3.9 %copy-start.4 = (f32[2,32,256]{2,1,0:T(8,128)S(1)}, f32[2,32,256]{2,1,0:T(8,128)}, u32[]{:S(2)}) copy-start(f32[2,32,256]{2,1,0:T(8,128)} %constant.58.clone.fine_ref) | copy-start | bytes 196612
  52.1 36.8 %collective-permute-start.4 = (f32[8,8192]{1,0:T(8,128)}, f32[8,8192]{1,0:T(8,128)}, u32[]{:S(2)}, u32[]{:S(2)}) collective-permute-start(f32[8,8192]{1,0:T(8,128)} %pad_maximum_fusion.2), channel_id=1, source_target_pairs={{0,32},{32,0},{1,33},{33,1},{2,34},{34,2},{3,35},{35,3},{4,36},{36... | collective-permute-start | bytes 786440 | tf_op jit(solution)/shard_map/ppermute | solution.py:258
  55.9 27.9 %copy-start.5 = (f32[2,32,1024]{2,1,0:T(8,128)S(1)}, f32[2,32,1024]{2,1,0:T(8,128)}, u32[]{:S(2)}) copy-start(f32[2,32,1024]{2,1,0:T(8,128)} %constant.61.clone.twiddle_ref) | copy-start | bytes 786436
  55.9 27.9 %copy-start.7 = (bf16[64,96]{1,0:T(8,128)(2,1)S(1)}, bf16[64,96]{1,0:T(8,128)(2,1)}, u32[]{:S(2)}) copy-start(bf16[64,96]{1,0:T(8,128)(2,1)} %constant.59.clone.small_ref) | copy-start | bytes 36868
  83.8 5.2 %copy-start.9 = (f32[4,8192]{1,0:T(4,128)S(1)}, f32[4,8192]{1,0:T(4,128)}, u32[]{:S(2)}) copy-start(f32[4,8192]{1,0:T(4,128)} %copy-done.8) | copy-start | bytes 393220
  85.9 7.3 %collective-permute-start.6 = (f32[16,4096]{1,0:T(8,128)S(1)}, f32[16,4096]{1,0:T(8,128)S(1)}, u32[]{:S(2)}, u32[]{:S(2)}) collective-permute-start(f32[16,4096]{1,0:T(8,128)S(1)} %get-tuple-element.16), channel_id=1, source_target_pairs={{0,1},{1,0},{2,3},{3,2},{4,5},{5,4},{6,7},{7,6},{8,9},{9,8},{10,11... | collective-permute-start | bytes 786440 | tf_op jit(solution)/shard_map/ppermute | solution.py:337
  93.2 8.4 %collective-permute-start.7 = (f32[2,8,4096]{2,1,0:T(8,128)S(1)}, f32[2,8,4096]{2,1,0:T(8,128)S(1)}, u32[]{:S(2)}, u32[]{:S(2)}) collective-permute-start(f32[2,8,4096]{2,1,0:T(8,128)S(1)} %broadcast_select_fusion), channel_id=1, source_target_pairs={{0,32},{32,0},{1,33},{33,1},{2,34},{34,2},{3,35},{35,3},{4,36},{36... | collective-permute-start | bytes 786440 | tf_op jit(solution)/shard_map/ppermute | solution.py:254
  98.9 9.7 %collective-permute-start.5 = (f32[16,4096]{1,0:T(8,128)S(1)}, f32[16,4096]{1,0:T(8,128)S(1)}, u32[]{:S(2)}, u32[]{:S(2)}) collective-permute-start(f32[16,4096]{1,0:T(8,128)S(1)} %get-tuple-element.19), channel_id=1, source_target_pairs={{0,1},{1,0},{2,3},{3,2},{4,5},{5,4},{6,7},{7,6},{8,9},{9,8},{10,11... | collective-permute-start | bytes 786440 | tf_op jit(solution)/shard_map/ppermute | solution.py:307
  101.7 7.0 %copy-start.6 = (bf16[32,192]{1,0:T(8,128)(2,1)S(1)}, bf16[32,192]{1,0:T(8,128)(2,1)}, u32[]{:S(2)}) copy-start(bf16[32,192]{1,0:T(8,128)(2,1)} %constant.60.clone.small_ref) | copy-start | bytes 36868
  101.7 9.0 %collective-permute-start.8 = (f32[2,4,4096]{2,1,0:T(4,128)S(1)}, f32[2,4,4096]{2,1,0:T(4,128)S(1)}, u32[]{:S(2)}, u32[]{:S(2)}) collective-permute-start(f32[2,4,4096]{2,1,0:T(4,128)S(1)} %slice_select_fusion), channel_id=1, source_target_pairs={{0,64},{64,0},{128,192},{192,128},{1,65},{65,1},{129,193},{193,129... | collective-permute-start | bytes 393224 | tf_op jit(solution)/shard_map/ppermute | solution.py:254
  110.8 14.7 %collective-permute-start.9 = (f32[2,2,4096]{2,1,0:T(2,128)S(1)}, f32[2,2,4096]{2,1,0:T(2,128)S(1)}, u32[]{:S(2)}, u32[]{:S(2)}) collective-permute-start(f32[2,2,4096]{2,1,0:T(2,128)S(1)} %broadcast_select_fusion.6), channel_id=1, source_target_pairs={{0,128},{64,192},{128,0},{192,64},{1,129},{65,193},{129,1},{193,65... | collective-permute-start | bytes 196616 | tf_op jit(solution)/shard_map/ppermute | solution.py:254
  118.2 44.9 %all-to-all-start.1 = ((f32[32,1,4096]{2,1,0:T(1,128)}), f32[32,1,4096]{2,1,0:T(1,128)S(1)}, u32[]{:S(2)}, u32[]{:S(2)}) async-start(f32[32,1,4096]{2,1,0:T(1,128)} %back.1), calls=%async_computation.1 | async-start | bytes 1048576 | tf_op jit(solution)/shard_map/all_to_all | solution.py:360
  125.8 18.4 %collective-permute-start.10 = (f32[2,4096]{1,0:T(2,128)S(1)}, f32[2,4096]{1,0:T(2,128)S(1)}, u32[]{:S(2)}, u32[]{:S(2)}) collective-permute-start(f32[2,4096]{1,0:T(2,128)S(1)} %fusion.3), channel_id=1, source_target_pairs={{0,0},{256,1},{128,2},{384,3},{64,4},{320,5},{192,6},{448,7},{32,8... | collective-permute-start | bytes 98312 | tf_op jit(solution)/shard_map/ppermute | solution.py:366
  133.3 29.1 %collective-permute-start.11 = (f32[2,4096]{1,0:T(2,128)S(1)}, f32[2,4096]{1,0:T(2,128)S(1)}, u32[]{:S(2)}, u32[]{:S(2)}) collective-permute-start(f32[2,4096]{1,0:T(2,128)S(1)} %bitcast.27), channel_id=1, source_target_pairs={{256,0},{0,1},{384,2},{128,3},{320,4},{64,5},{448,6},{192,7},{288,... | collective-permute-start | bytes 98312 | tf_op jit(solution)/shard_map/ppermute | solution.py:366

commit v4 on v3

--- a/solution.py
+++ b/solution.py
@@ -120,13 +120,14 @@
 
 
 def forward_kernel(
-    odd_ref, moved_ref, small_ref, twiddle_ref, cos_hi, cos_lo, sin_hi, sin_lo, spec_ref, mine_ref,
+    core_ref, moved_ref, small_ref, twiddle_ref, cos_hi, cos_lo, sin_hi, sin_lo, spec_ref, kept_ref,
     away_ref, rows_ref,
 ):
     classes = moved_ref.shape[0]
     points = cos_hi.shape[0]
     scale = 1.0 / math.sqrt(classes * points)
-    odd = odd_ref[0] == 1
+    upper_core = core_ref[0] == 1
+    quarter = classes // 4
     tw_cos, tw_sin = twiddle_ref[0] * scale, twiddle_ref[1] * scale
     for channel in range(2):
         delta = moved_ref[:, (4 + channel) * points : (5 + channel) * points]
@@ -153,28 +154,23 @@
             term_real = in_real * real[mine] + in_imag * imag[mine]
             term_imag = in_real * imag[mine] - in_imag * real[mine]
             for put, term in ((put_real, term_real), (put_imag, term_imag)):
-                lower, upper = term[: classes // 2], term[classes // 2 :]
-                mine_ref[:, put] = jnp.where(odd, upper, lower)
-                away_ref[:, put] = jnp.where(odd, lower, upper)
+                for side in range(2):
+                    lower = term[2 * side * quarter : (2 * side + 1) * quarter]
+                    upper = term[(2 * side + 1) * quarter : (2 * side + 2) * quarter]
+                    kept_ref[side, :, put] = jnp.where(upper_core, upper, lower)
+                    away_ref[side, :, put] = jnp.where(upper_core, lower, upper)
 
 
 def inverse_rows(
-    sign, odd_ref, first_ref, mine_ref, other_ref, small_ref, twiddle_ref, tables, rows_ref,
-    turned_ref,
+    sign, first_ref, filt_ref, small_ref, twiddle_ref, tables, rows_ref, turned_ref
 ):
     cos_hi, cos_lo, sin_hi, sin_lo = tables
     classes = first_ref.shape[0]
     points = cos_hi.shape[0]
-    odd = odd_ref[0] == 1
-
-    def filt(at):
-        mine, other = mine_ref[:, at], other_ref[:, at]
-        return jnp.concatenate([jnp.where(odd, other, mine), jnp.where(odd, mine, other)], axis=0)
-
     for channel in range(2):
         real_at = slice(channel * points, (channel + 1) * points)
         imag_at = slice((2 + channel) * points, (3 + channel) * points)
-        filt_real, filt_imag = filt(real_at), filt(imag_at) * sign
+        filt_real, filt_imag = filt_ref[:, real_at], filt_ref[:, imag_at] * sign
         first_real, first_imag = first_ref[:, real_at], first_ref[:, imag_at]
         keep_quarters(
             rows_ref,
@@ -207,26 +203,24 @@
 
 
 def conv_kernel(
-    odd_ref, moved_ref, mine_ref, other_ref, small_ref, twiddle_ref, cos_hi, cos_lo, sin_hi, sin_lo,
-    conv_ref, rows_ref, turned_ref,
+    moved_ref, filt_ref, small_ref, twiddle_ref, cos_hi, cos_lo, sin_hi, sin_lo, conv_ref, rows_ref,
+    turned_ref,
 ):
     tables = (cos_hi, cos_lo, sin_hi, sin_lo)
     conv_ref[...] = inverse_rows(
-        1.0, odd_ref, moved_ref, mine_ref, other_ref, small_ref, twiddle_ref, tables, rows_ref,
-        turned_ref,
+        1.0, moved_ref, filt_ref, small_ref, twiddle_ref, tables, rows_ref, turned_ref
     )
 
 
 def back_kernel(
-    odd_ref, conv_ref, spec_ref, mine_ref, other_ref, small_ref, twiddle_ref, cos_hi, cos_lo,
-    sin_hi, sin_lo, packed_ref, rows_ref, turned_ref,
+    conv_ref, spec_ref, filt_ref, small_ref, twiddle_ref, cos_hi, cos_lo, sin_hi, sin_lo, packed_ref,
+    rows_ref, turned_ref,
 ):
     tables = (cos_hi, cos_lo, sin_hi, sin_lo)
     width = conv_ref.shape[1]
     packed_ref[:, 0, :width] = conv_ref[...]
     packed_ref[:, 0, width:] = inverse_rows(
-        -1.0, odd_ref, spec_ref, mine_ref, other_ref, small_ref, twiddle_ref, tables, rows_ref,
-        turned_ref,
+        -1.0, spec_ref, filt_ref, small_ref, twiddle_ref, tables, rows_ref, turned_ref
     )
 
 
@@ -257,7 +251,7 @@
 def doubling(values, upper, axis, pairs):
     other = lax.ppermute(values, axis, pairs)
     return jnp.concatenate(
-        [jnp.where(upper, other, values), jnp.where(upper, values, other)], axis=0
+        [jnp.where(upper, other, values), jnp.where(upper, values, other)], axis=1
     )
 
 
@@ -290,73 +284,63 @@
     near_y = [(y, y ^ 1) for y in range(lax.axis_size("y"))]
     cores = [(0, 1), (1, 0)]
     half_row = 4 * positions
-    sent = (
-        filter_spectrum.reshape(2, 2, per_seq, positions)
-        .transpose(1, 0, 2, 3)
-        .reshape(1, 2 * half_row)
-    )
-    got = [lax.ppermute(sent, everyone, pairs[number]) for number in range(2)]
-    filters = jnp.concatenate(
-        [jnp.where(upper_zhi, got[1], got[0]), jnp.where(upper_zhi, got[0], got[1])], axis=0
-    )
+    got = [lax.ppermute(filter_spectrum, everyone, pairs[number]) for number in range(2)]
+    ordered = [jnp.where(upper_zhi, got[1 - n], got[n]) for n in range(2)]
+    mine = jnp.stack([jnp.where(odd, v[:, per_seq:], v[:, :per_seq]) for v in ordered])
+    away = jnp.stack([jnp.where(odd, v[:, :per_seq], v[:, per_seq:]) for v in ordered])
+    other = lax.ppermute(away, "y", near_y)
+    mine, other = mine.reshape(2, half_row), other.reshape(2, half_row)
+    filters = jnp.stack([jnp.where(odd, other, mine), jnp.where(odd, mine, other)])
     filters = doubling(filters, x_index >= 2, "x", far_x)
     filters = doubling(filters, x_index % 2 == 1, "x", near_x)
-    filters = doubling(filters, upper_core, "core", cores)
-    mine = jnp.where(odd, filters[:, half_row:], filters[:, :half_row])
-    away = jnp.where(odd, filters[:, :half_row], filters[:, half_row:])
-    filters = (mine, lax.ppermute(away, "y", near_y))
+    filters = doubling(filters, upper_core, "core", cores).reshape(seq_count, half_row)
 
     tables = root_tables(positions)
     small_out = small_table(seq_count, False)
     small_back = small_table(seq_count, True)
     twiddle = jnp.asarray(np.stack(unit_roots(seq_count, positions, seq_count * positions)))
 
-    half = seq_count // 2
-    parity = odd.astype(jnp.int32).reshape(1)
+    core_flag = upper_core.astype(jnp.int32).reshape(1)
     wide = jax.ShapeDtypeStruct((seq_count, half_row), f32)
-    narrow = jax.ShapeDtypeStruct((half, half_row), f32)
+    part = jax.ShapeDtypeStruct((2, seq_count // 4, half_row), f32)
     rows = [pltpu.VMEM((4, 8 * seq_count, positions), bf16)]
     turned = [pltpu.VMEM((6 * seq_count, 2 * positions), bf16)]
     cost = pl.CostEstimate(flops=2 * 10**9, bytes_accessed=10**7, transcendentals=0)
 
-    def specs(count):
-        return [pl.BlockSpec(memory_space=pltpu.SMEM)] + [
-            pl.BlockSpec(memory_space=pltpu.VMEM) for _ in range(count)
-        ]
-
-    spec, mine, away = pl.pallas_call(
+    vmem = pl.BlockSpec(memory_space=pltpu.VMEM)
+    spec, kept, away = pl.pallas_call(
         forward_kernel,
-        out_shape=[wide, narrow, narrow],
-        in_specs=specs(7),
+        out_shape=[wide, part, part],
+        in_specs=[pl.BlockSpec(memory_space=pltpu.SMEM)] + [vmem] * 7,
         scratch_shapes=rows,
         name="forward",
         compiler_params=params,
         cost_estimate=cost,
-    )(parity, moved, small_out, twiddle, *tables)
-
-    other = lax.ppermute(away, "y", near_y)
-    total = halving(jnp.stack([mine, other]), upper_core, "core", cores)
+    )(core_flag, moved, small_out, twiddle, *tables)
+
+    total = kept + lax.ppermute(away, "core", cores)
+    mine = jnp.where(odd, total[1], total[0])
+    other = lax.ppermute(jnp.where(odd, total[0], total[1]), "y", near_y)
+    total = jnp.stack([mine, other])
     total = halving(total, x_index % 2 == 1, "x", near_x)
     total = halving(total, x_index >= 2, "x", far_x)
 
     conv = pl.pallas_call(
         conv_kernel,
         out_shape=jax.ShapeDtypeStruct((seq_count, 2 * positions), f32),
-        in_specs=specs(9),
         scratch_shapes=rows + turned,
         name="conv",
         compiler_params=params,
         cost_estimate=cost,
-    )(parity, moved, *filters, small_back, twiddle, *tables)
+    )(moved, filters, small_back, twiddle, *tables)
     signals = pl.pallas_call(
         back_kernel,
         out_shape=jax.ShapeDtypeStruct((seq_count, 1, 4 * positions), f32),
-        in_specs=specs(10),
         scratch_shapes=rows + turned,
         name="back",
         compiler_params=params,
         cost_estimate=cost,
-    )(parity, conv, spec, *filters, small_back, twiddle, *tables)
+    )(conv, spec, filters, small_back, twiddle, *tables)
     returned = lax.all_to_all(signals, SEQ, split_axis=0, concat_axis=0, tiled=True)
     returned = returned.reshape(seq_count, 4 * positions)
 

time: 166 us -> 154 us (0.928)
  starting transfers between devices: 77.7 us -> 69.1 us
  waiting for transfers between devices: 69.7 us -> 67.7 us
    ppermute x3 -> x2, starting transfers between devices: 12.1 us -> 3.84 us  [halving(): return kept + lax.ppermute(away, axis, pairs)]
    all_to_all x1, waiting for transfers between devices: 27.6 us -> 21.9 us  [step(): moved = lax.all_to_all(packed, SEQ, split_axis=0, concat_axis=0, tiled=True)]
    ppermute x3, waiting for transfers between devices: 4.71 us -> 10.2 us  [doubling(): other = lax.ppermute(values, axis, pairs)]
    ppermute x1, waiting for transfers between devices: 3.14 us -> 0.01 us  [step(): other = lax.ppermute(away, 'y', near_y)]
    ppermute x3 -> x2, waiting for transfers between devices: 0.01 us -> 1.73 us  [halving(): return kept + lax.ppermute(away, axis, pairs)]
    ppermute x3 -> x4, starting transfers between devices: 25.1 us -> 26.3 us  [the longest x2 22.4 us: step(): lax.ppermute(filter_spectrum, everyone, pairs[number])]
    ppermute x3 -> x4, waiting for transfers between devices: 11.4 us -> 11.9 us  [the longest x2 6.61 us: step(): lax.ppermute(filter_spectrum, everyone, pairs[number])]
  transfers between devices with their start and end apart: 14 -> 14, of which waited for: 7 -> 9; matrix products, arithmetic and copies ran while one was open for 2% -> 2% of each run, Pallas kernels for 5% -> 6%
where the time goes in v4:
time: 154 us; the launch traced here: 153 us
  starting transfers between devices  69.1 us (45%)
  waiting for transfers between devices  67.7 us (44%)
  Pallas kernels  9.03 us (6%)
  other arithmetic  3.26 us (2%)
  local copies, waits for them, and re-layouts  3.2 us (2%)
    ppermute x2, starting transfers between devices, step(): lax.ppermute(filter_spectrum, everyone, pairs[number])  22.4 us
    all_to_all x1, waiting for transfers between devices, step(): moved = lax.all_to_all(packed, SEQ, split_axis=0, concat_axis=0, tiled=True)  21.9 us
    ppermute x2, waiting for transfers between devices, step(): lax.ppermute(rows_out[number], everyone, [(b, a) for a, b in pairs[number]])  21.9 us
    ppermute x2, starting transfers between devices, step(): lax.ppermute(rows_out[number], everyone, [(b, a) for a, b in pairs[number]])  14.2 us
    all_to_all x1, starting transfers between devices, step(): moved = lax.all_to_all(packed, SEQ, split_axis=0, concat_axis=0, tiled=True)  10.8 us
    ppermute x3, waiting for transfers between devices, doubling(): other = lax.ppermute(values, axis, pairs)  10.2 us
    ppermute x2, waiting for transfers between devices, step(): lax.ppermute(filter_spectrum, everyone, pairs[number])  6.61 us
    ppermute x3, starting transfers between devices, doubling(): other = lax.ppermute(values, axis, pairs)  6.34 us
  transfers between devices with their start and end apart: 14, of which 9 were waited for; matrix products, arithmetic and copies ran while one was open for 2% of the time, Pallas kernels for 6%

profile of v4, /device:TPU:7, one launch (start us, length us, event | category | flops | bytes accessed | tf_op | source)
XLA Modules:
  0.0 153.4 jit_solution(6869004433119022995)
XLA Ops:
  0.6 17.2 %collective-permute-start = (f32[2,4,1024]{2,1,0:T(4,128)}, f32[2,4,1024]{2,1,0:T(4,128)S(1)}, u32[]{:S(2)}, u32[]{:S(2)}) collective-permute-start(f32[2,4,1024]{2,1,0:T(4,128)} %param.12), channel_id=1, source_target_pairs={{0,256},{1,0},{2,384},{3,128},{4,320},{5,64},{6,448},{7,192},{8,28... | collective-permute-start | bytes 98312 | tf_op jit(solution)/shard_map/ppermute | solution.py:287
  17.9 5.2 %collective-permute-start.1 = (f32[2,4,1024]{2,1,0:T(4,128)}, f32[2,4,1024]{2,1,0:T(4,128)S(1)}, u32[]{:S(2)}, u32[]{:S(2)}) collective-permute-start(f32[2,4,1024]{2,1,0:T(4,128)} %param.12), channel_id=1, source_target_pairs={{0,0},{1,256},{2,128},{3,384},{4,64},{5,320},{6,192},{7,448},{8,32... | collective-permute-start | bytes 98312 | tf_op jit(solution)/shard_map/ppermute | solution.py:287
  23.1 0.0 collective-permute-done
  23.1 6.6 %collective-permute-done.1 = f32[2,4,1024]{2,1,0:T(4,128)S(1)} collective-permute-done((f32[2,4,1024]{2,1,0:T(4,128)}, f32[2,4,1024]{2,1,0:T(4,128)S(1)}, u32[]{:S(2)}, u32[]{:S(2)}) %collective-permute-start.1) | collective-permute-done | bytes 32800 | tf_op jit(solution)/shard_map/ppermute | solution.py:287
  29.7 0.0 copy-start.2
  29.7 0.0 copy-start.1
  29.8 2.1 %collective-permute-start.2 = (f32[2,2,2,1024]{3,2,1,0:T(2,128)S(1)}, f32[2,2,2,1024]{3,2,1,0:T(2,128)S(1)}, u32[]{:S(2)}, u32[]{:S(2)}) collective-permute-start(f32[2,2,2,1024]{3,2,1,0:T(2,128)S(1)} %pad_maximum_fusion.5), channel_id=1, source_target_pairs={{0,1},{1,0},{2,3},{3,2},{4,5},{5,4},{6,7},{7,6},{8,9},{9,8},{10,11... | collective-permute-start | bytes 98312 | tf_op jit(solution)/shard_map/ppermute | solution.py:291
  31.9 0.0 copy-done.2
  31.9 0.0 copy-done.1
  31.9 0.0 copy-start
  31.9 1.0 copy-done
  32.9 1.4 pack.1
  34.3 10.8 %all-to-all-start = ((f32[32,1,6144]{2,1,0:T(1,128)}), f32[32,1,6144]{2,1,0:T(1,128)S(1)}, u32[]{:S(2)}, u32[]{:S(2)}) async-start(f32[32,1,6144]{2,1,0:T(1,128)} %pack.1), calls=%async_computation | async-start | bytes 1572864 | tf_op jit(solution)/shard_map/all_to_all | solution.py:279
  45.2 0.0 collective-permute-done.2
  45.3 1.9 %collective-permute-start.3 = (f32[2,2,4096]{2,1,0:T(2,128)S(1)}, f32[2,2,4096]{2,1,0:T(2,128)S(1)}, u32[]{:S(2)}, u32[]{:S(2)}) collective-permute-start(f32[2,2,4096]{2,1,0:T(2,128)S(1)} %pad_maximum_fusion.4), channel_id=1, source_target_pairs={{0,128},{64,192},{128,0},{192,64},{1,129},{65,193},{129,1},{193,65... | collective-permute-start | bytes 196616 | tf_op jit(solution)/shard_map/ppermute | solution.py:252
  47.3 4.9 %collective-permute-done.3 = f32[2,2,4096]{2,1,0:T(2,128)S(1)} collective-permute-done((f32[2,2,4096]{2,1,0:T(2,128)S(1)}, f32[2,2,4096]{2,1,0:T(2,128)S(1)}, u32[]{:S(2)}, u32[]{:S(2)}) %collective-permute-start.3) | collective-permute-done | bytes 65568 | tf_op jit(solution)/shard_map/ppermute | solution.py:252
  52.2 0.1 broadcast_select_fusion.5
  52.3 0.1 pad_maximum_fusion.3
  52.3 1.9 %collective-permute-start.4 = (f32[2,4,4096]{2,1,0:T(4,128)S(1)}, f32[2,4,4096]{2,1,0:T(4,128)S(1)}, u32[]{:S(2)}, u32[]{:S(2)}) collective-permute-start(f32[2,4,4096]{2,1,0:T(4,128)S(1)} %pad_maximum_fusion.3), channel_id=1, source_target_pairs={{0,64},{64,0},{128,192},{192,128},{1,65},{65,1},{129,193},{193,129... | collective-permute-start | bytes 393224 | tf_op jit(solution)/shard_map/ppermute | solution.py:252
  54.3 5.3 %collective-permute-done.4 = f32[2,4,4096]{2,1,0:T(4,128)S(1)} collective-permute-done((f32[2,4,4096]{2,1,0:T(4,128)S(1)}, f32[2,4,4096]{2,1,0:T(4,128)S(1)}, u32[]{:S(2)}, u32[]{:S(2)}) %collective-permute-start.4) | collective-permute-done | bytes 131104 | tf_op jit(solution)/shard_map/ppermute | solution.py:252
  59.5 0.1 broadcast_select_fusion.8
  59.6 0.0 copy-start.8
  59.6 0.0 copy-start.3
  59.6 0.0 copy-start.4
  59.7 0.8 pad_maximum_fusion.1
  60.4 0.0 copy-done.8
  60.4 2.5 %collective-permute-start.5 = (f32[2,8,4096]{2,1,0:T(8,128)}, f32[2,8,4096]{2,1,0:T(8,128)}, u32[]{:S(2)}, u32[]{:S(2)}) collective-permute-start(f32[2,8,4096]{2,1,0:T(8,128)} %pad_maximum_fusion.1), channel_id=1, source_target_pairs={{0,32},{32,0},{1,33},{33,1},{2,34},{34,2},{3,35},{35,3},{4,36},{36... | collective-permute-start | bytes 786440 | tf_op jit(solution)/shard_map/ppermute | solution.py:252
  63.0 0.0 copy-done.3
  63.0 0.0 copy-done.4
  63.0 0.6 root_tables.1
  63.6 0.0 copy-start.5
  63.6 0.0 copy-start.7
  63.6 21.9 %all-to-all-done = f32[32,1,6144]{2,1,0:T(1,128)S(1)} async-done(((f32[32,1,6144]{2,1,0:T(1,128)}), f32[32,1,6144]{2,1,0:T(1,128)S(1)}, u32[]{:S(2)}, u32[]{:S(2)}) %all-to-all-start) | async-done | bytes 786464 | tf_op jit(solution)/shard_map/all_to_all | solution.py:279
  85.5 0.2 copy.34
  85.8 0.0 copy-done.5
  85.8 0.0 copy-done.7
  85.8 0.0 copy-start.9
  85.8 2.0 %forward.1 = (f32[32,4096]{1,0:T(8,128)S(1)}, f32[2,8,4096]{2,1,0:T(8,128)S(1)}, f32[2,8,4096]{2,1,0:T(8,128)S(1)}) custom-call(s32[1]{0:T(128)} %bitcast.3.core_ref, f32[32,6144]{1,0:T(8,128)S(1)} %bitcast.25, bf16[64,96]{1,0:T(8,128)(2,1)S(1)} %copy-done.7, f32[2,32,1024]{2,1,0:T(8,128)S(1)} %copy-done.5, bf16[1024,256]{1,0:T(8,128)(2,1)S(1)} %get-tuple-element.10.cos_hi, ...), custom_call_target="tpu_custom_call" | custom-call | flops 2000000000 | bytes 10000000 | tf_op jit(solution)/shard_map/forward/pallas_call | solution.py:311
  87.9 1.9 %collective-permute-start.6 = (f32[2,8,4096]{2,1,0:T(8,128)S(1)}, f32[2,8,4096]{2,1,0:T(8,128)S(1)}, u32[]{:S(2)}, u32[]{:S(2)}) collective-permute-start(f32[2,8,4096]{2,1,0:T(8,128)S(1)} %get-tuple-element.16), channel_id=1, source_target_pairs={{0,32},{32,0},{1,33},{33,1},{2,34},{34,2},{3,35},{35,3},{4,36},{36... | collective-permute-start | bytes 786440 | tf_op jit(solution)/shard_map/ppermute | solution.py:321
  89.8 0.0 collective-permute-done.5
  89.8 0.0 copy-done.9
  89.8 1.0 broadcast_select_fusion.1
  90.8 0.5 collective-permute-done.6
  91.4 1.9 %collective-permute-start.7 = (f32[8,4096]{1,0:T(8,128)S(1)}, f32[8,4096]{1,0:T(8,128)S(1)}, u32[]{:S(2)}, u32[]{:S(2)}) collective-permute-start(f32[8,4096]{1,0:T(8,128)S(1)} %get-tuple-element.22), channel_id=1, source_target_pairs={{0,1},{1,0},{2,3},{3,2},{4,5},{5,4},{6,7},{7,6},{8,9},{9,8},{10,11... | collective-permute-start | bytes 393224 | tf_op jit(solution)/shard_map/ppermute | solution.py:323
  93.3 4.8 %collective-permute-done.7 = f32[8,4096]{1,0:T(8,128)S(1)} collective-permute-done((f32[8,4096]{1,0:T(8,128)S(1)}, f32[8,4096]{1,0:T(8,128)S(1)}, u32[]{:S(2)}, u32[]{:S(2)}) %collective-permute-start.7) | collective-permute-done | bytes 131104 | tf_op jit(solution)/shard_map/ppermute | solution.py:323
  98.2 1.9 %collective-permute-start.8 = (f32[2,4,4096]{2,1,0:T(4,128)S(1)}, f32[2,4,4096]{2,1,0:T(4,128)S(1)}, u32[]{:S(2)}, u32[]{:S(2)}) collective-permute-start(f32[2,4,4096]{2,1,0:T(4,128)S(1)} %broadcast_select_fusion.6), channel_id=1, source_target_pairs={{0,64},{64,0},{128,192},{192,128},{1,65},{65,1},{129,193},{193,129... | collective-permute-start | bytes 393224 | tf_op jit(solution)/shard_map/ppermute | solution.py:248
  100.1 0.0 copy-done.6
  100.2 2.0 %conv.1.conv_ref = f32[32,2048]{1,0:T(8,128)S(1)} custom-call(f32[32,6144]{1,0:T(8,128)S(1)} %bitcast.26, f32[32,4096]{1,0:T(8,128)S(1)} %bitcast.27, bf16[32,192]{1,0:T(8,128)(2,1)S(1)} %copy-done.6, f32[2,32,1024]{2,1,0:T(8,128)S(1)} %copy-done.5, bf16[1024,256]{1,0:T(8,128)(2,1)S(1)} %get-tuple-element.10.cos_hi, ...), custom_call_target="tpu_custom_call" | custom-call | flops 2000000000 | bytes 10000000 | tf_op jit(solution)/shard_map/conv/pallas_call | solution.py:328
  102.2 1.7 %collective-permute-done.8 = f32[2,4,4096]{2,1,0:T(4,128)S(1)} collective-permute-done((f32[2,4,4096]{2,1,0:T(4,128)S(1)}, f32[2,4,4096]{2,1,0:T(4,128)S(1)}, u32[]{:S(2)}, u32[]{:S(2)}) %collective-permute-start.8) | collective-permute-done | bytes 131104 | tf_op jit(solution)/shard_map/ppermute | solution.py:248
  104.0 1.9 %collective-permute-start.9 = (f32[2,2,4096]{2,1,0:T(2,128)S(1)}, f32[2,2,4096]{2,1,0:T(2,128)S(1)}, u32[]{:S(2)}, u32[]{:S(2)}) collective-permute-start(f32[2,2,4096]{2,1,0:T(2,128)S(1)} %broadcast_select_fusion.3), channel_id=1, source_target_pairs={{0,128},{64,192},{128,0},{192,64},{1,129},{65,193},{129,1},{193,65... | collective-permute-start | bytes 196616 | tf_op jit(solution)/shard_map/ppermute | solution.py:248
  105.9 2.9 %back.1 = f32[32,1,4096]{2,1,0:T(1,128)} custom-call(f32[32,2048]{1,0:T(8,128)S(1)} %conv.1.conv_ref, f32[32,4096]{1,0:T(8,128)S(1)} %get-tuple-element.14.spec_ref, f32[32,4096]{1,0:T(8,128)S(1)} %bitcast.28, bf16[32,192]{1,0:T(8,128)(2,1)S(1)} %copy-done.6, f32[2,32,1024]{2,1,0:T(8,128)S(1)} %copy-done.5, bf16[1024,256]{1,0:T(8,128)(2,1)S(1)} %get-tuple-element.10.cos_hi, ...), custom_call_target="tpu_custom_call" | custom-call | flops 2000000000 | bytes 10000000 | tf_op jit(solution)/shard_map/back/pallas_call | solution.py:336
  108.8 5.7 %all-to-all-start.1 = ((f32[32,1,4096]{2,1,0:T(1,128)}), f32[32,1,4096]{2,1,0:T(1,128)S(1)}, u32[]{:S(2)}, u32[]{:S(2)}) async-start(f32[32,1,4096]{2,1,0:T(1,128)} %back.1), calls=%async_computation.1 | async-start | bytes 1048576 | tf_op jit(solution)/shard_map/all_to_all | solution.py:344
  114.5 0.0 collective-permute-done.9
  114.5 0.1 select_add_fusion.1
  114.6 0.1 broadcast_select_fusion.2
  114.8 12.3 %collective-permute-start.10 = (f32[2,4096]{1,0:T(2,128)S(1)}, f32[2,4096]{1,0:T(2,128)S(1)}, u32[]{:S(2)}, u32[]{:S(2)}) collective-permute-start(f32[2,4096]{1,0:T(2,128)S(1)} %fusion.2), channel_id=1, source_target_pairs={{0,0},{256,1},{128,2},{384,3},{64,4},{320,5},{192,6},{448,7},{32,8... | collective-permute-start | bytes 98312 | tf_op jit(solution)/shard_map/ppermute | solution.py:350
  127.1 1.9 %collective-permute-start.11 = (f32[2,4096]{1,0:T(2,128)S(1)}, f32[2,4096]{1,0:T(2,128)S(1)}, u32[]{:S(2)}, u32[]{:S(2)}) collective-permute-start(f32[2,4096]{1,0:T(2,128)S(1)} %bitcast.35), channel_id=1, source_target_pairs={{256,0},{0,1},{384,2},{128,3},{320,4},{64,5},{448,6},{192,7},{288,... | collective-permute-start | bytes 98312 | tf_op jit(solution)/shard_map/ppermute | solution.py:350
  129.0 10.1 %collective-permute-done.10 = f32[2,4096]{1,0:T(2,128)S(1)} collective-permute-done((f32[2,4096]{1,0:T(2,128)S(1)}, f32[2,4096]{1,0:T(2,128)S(1)}, u32[]{:S(2)}, u32[]{:S(2)}) %collective-permute-start.10) | collective-permute-done | bytes 32800 | tf_op jit(solution)/shard_map/ppermute | solution.py:350
  139.1 11.8 %collective-permute-done.11 = f32[2,4096]{1,0:T(2,128)S(1)} collective-permute-done((f32[2,4096]{1,0:T(2,128)S(1)}, f32[2,4096]{1,0:T(2,128)S(1)}, u32[]{:S(2)}, u32[]{:S(2)}) %collective-permute-start.11) | collective-permute-done | bytes 32800 | tf_op jit(solution)/shard_map/ppermute | solution.py:350
  151.0 0.6 reshape.158
  151.6 0.0 all-to-all-done.1
  151.6 0.3 copy.35
  152.0 0.7 multiply_convert_fusion
  152.7 0.7 convert_element_type.22
  (23 shorter events, 0.7 us)
Async XLA Ops:
  0.6 22.5 %collective-permute-start = (f32[2,4,1024]{2,1,0:T(4,128)}, f32[2,4,1024]{2,1,0:T(4,128)S(1)}, u32[]{:S(2)}, u32[]{:S(2)}) collective-permute-start(f32[2,4,1024]{2,1,0:T(4,128)} %param.12), channel_id=1, source_target_pairs={{0,256},{1,0},{2,384},{3,128},{4,320},{5,64},{6,448},{7,192},{8,28... | collective-permute-start | bytes 98312 | tf_op jit(solution)/shard_map/ppermute | solution.py:287
  17.9 11.9 %collective-permute-start.1 = (f32[2,4,1024]{2,1,0:T(4,128)}, f32[2,4,1024]{2,1,0:T(4,128)S(1)}, u32[]{:S(2)}, u32[]{:S(2)}) collective-permute-start(f32[2,4,1024]{2,1,0:T(4,128)} %param.12), channel_id=1, source_target_pairs={{0,0},{1,256},{2,128},{3,384},{4,64},{5,320},{6,192},{7,448},{8,32... | collective-permute-start | bytes 98312 | tf_op jit(solution)/shard_map/ppermute | solution.py:287
  29.7 2.1 %copy-start.2 = (bf16[1,64,1024]{2,1,0:T(8,128)(2,1)S(1)}, bf16[1,64,1024]{2,1,0:T(8,128)(2,1)}, u32[]{:S(2)}) copy-start(bf16[1,64,1024]{2,1,0:T(8,128)(2,1)} %gate_ref.1) | copy-start | bytes 393220
  29.7 2.1 %copy-start.1 = (bf16[1,64,1024]{2,1,0:T(8,128)(2,1)S(1)}, bf16[1,64,1024]{2,1,0:T(8,128)(2,1)}, u32[]{:S(2)}) copy-start(bf16[1,64,1024]{2,1,0:T(8,128)(2,1)} %out_ref.1) | copy-start | bytes 393220
  29.8 15.4 %collective-permute-start.2 = (f32[2,2,2,1024]{3,2,1,0:T(2,128)S(1)}, f32[2,2,2,1024]{3,2,1,0:T(2,128)S(1)}, u32[]{:S(2)}, u32[]{:S(2)}) collective-permute-start(f32[2,2,2,1024]{3,2,1,0:T(2,128)S(1)} %pad_maximum_fusion.5), channel_id=1, source_target_pairs={{0,1},{1,0},{2,3},{3,2},{4,5},{5,4},{6,7},{7,6},{8,9},{9,8},{10,11... | collective-permute-start | bytes 98312 | tf_op jit(solution)/shard_map/ppermute | solution.py:291
  31.9 1.0 copy-start
  34.3 51.2 %all-to-all-start = ((f32[32,1,6144]{2,1,0:T(1,128)}), f32[32,1,6144]{2,1,0:T(1,128)S(1)}, u32[]{:S(2)}, u32[]{:S(2)}) async-start(f32[32,1,6144]{2,1,0:T(1,128)} %pack.1), calls=%async_computation | async-start | bytes 1572864 | tf_op jit(solution)/shard_map/all_to_all | solution.py:279
  45.3 6.9 %collective-permute-start.3 = (f32[2,2,4096]{2,1,0:T(2,128)S(1)}, f32[2,2,4096]{2,1,0:T(2,128)S(1)}, u32[]{:S(2)}, u32[]{:S(2)}) collective-permute-start(f32[2,2,4096]{2,1,0:T(2,128)S(1)} %pad_maximum_fusion.4), channel_id=1, source_target_pairs={{0,128},{64,192},{128,0},{192,64},{1,129},{65,193},{129,1},{193,65... | collective-permute-start | bytes 196616 | tf_op jit(solution)/shard_map/ppermute | solution.py:252
  52.3 7.2 %collective-permute-start.4 = (f32[2,4,4096]{2,1,0:T(4,128)S(1)}, f32[2,4,4096]{2,1,0:T(4,128)S(1)}, u32[]{:S(2)}, u32[]{:S(2)}) collective-permute-start(f32[2,4,4096]{2,1,0:T(4,128)S(1)} %pad_maximum_fusion.3), channel_id=1, source_target_pairs={{0,64},{64,0},{128,192},{192,128},{1,65},{65,1},{129,193},{193,129... | collective-permute-start | bytes 393224 | tf_op jit(solution)/shard_map/ppermute | solution.py:252
  59.6 0.8 copy-start.8
  59.6 3.3 %copy-start.3 = (f32[2,32,256]{2,1,0:T(8,128)S(1)}, f32[2,32,256]{2,1,0:T(8,128)}, u32[]{:S(2)}) copy-start(f32[2,32,256]{2,1,0:T(8,128)} %constant.57.clone.coarse_ref) | copy-start | bytes 196612
  59.6 3.3 %copy-start.4 = (f32[2,32,256]{2,1,0:T(8,128)S(1)}, f32[2,32,256]{2,1,0:T(8,128)}, u32[]{:S(2)}) copy-start(f32[2,32,256]{2,1,0:T(8,128)} %constant.58.clone.fine_ref) | copy-start | bytes 196612
  60.4 29.4 %collective-permute-start.5 = (f32[2,8,4096]{2,1,0:T(8,128)}, f32[2,8,4096]{2,1,0:T(8,128)}, u32[]{:S(2)}, u32[]{:S(2)}) collective-permute-start(f32[2,8,4096]{2,1,0:T(8,128)} %pad_maximum_fusion.1), channel_id=1, source_target_pairs={{0,32},{32,0},{1,33},{33,1},{2,34},{34,2},{3,35},{35,3},{4,36},{36... | collective-permute-start | bytes 786440 | tf_op jit(solution)/shard_map/ppermute | solution.py:252
  63.6 22.2 %copy-start.5 = (f32[2,32,1024]{2,1,0:T(8,128)S(1)}, f32[2,32,1024]{2,1,0:T(8,128)}, u32[]{:S(2)}) copy-start(f32[2,32,1024]{2,1,0:T(8,128)} %constant.61.clone.twiddle_ref) | copy-start | bytes 786436
  63.6 22.2 %copy-start.7 = (bf16[64,96]{1,0:T(8,128)(2,1)S(1)}, bf16[64,96]{1,0:T(8,128)(2,1)}, u32[]{:S(2)}) copy-start(bf16[64,96]{1,0:T(8,128)(2,1)} %constant.59.clone.small_ref) | copy-start | bytes 36868
  85.8 4.0 %copy-start.9 = (f32[2,4,4096]{2,1,0:T(4,128)S(1)}, f32[2,4,4096]{2,1,0:T(4,128)}, u32[]{:S(2)}) copy-start(f32[2,4,4096]{2,1,0:T(4,128)} %copy-done.8) | copy-start | bytes 393220
  87.9 3.4 %collective-permute-start.6 = (f32[2,8,4096]{2,1,0:T(8,128)S(1)}, f32[2,8,4096]{2,1,0:T(8,128)S(1)}, u32[]{:S(2)}, u32[]{:S(2)}) collective-permute-start(f32[2,8,4096]{2,1,0:T(8,128)S(1)} %get-tuple-element.16), channel_id=1, source_target_pairs={{0,32},{32,0},{1,33},{33,1},{2,34},{34,2},{3,35},{35,3},{4,36},{36... | collective-permute-start | bytes 786440 | tf_op jit(solution)/shard_map/ppermute | solution.py:321
  91.4 6.8 %collective-permute-start.7 = (f32[8,4096]{1,0:T(8,128)S(1)}, f32[8,4096]{1,0:T(8,128)S(1)}, u32[]{:S(2)}, u32[]{:S(2)}) collective-permute-start(f32[8,4096]{1,0:T(8,128)S(1)} %get-tuple-element.22), channel_id=1, source_target_pairs={{0,1},{1,0},{2,3},{3,2},{4,5},{5,4},{6,7},{7,6},{8,9},{9,8},{10,11... | collective-permute-start | bytes 393224 | tf_op jit(solution)/shard_map/ppermute | solution.py:323
  98.2 2.0 %copy-start.6 = (bf16[32,192]{1,0:T(8,128)(2,1)S(1)}, bf16[32,192]{1,0:T(8,128)(2,1)}, u32[]{:S(2)}) copy-start(bf16[32,192]{1,0:T(8,128)(2,1)} %constant.60.clone.small_ref) | copy-start | bytes 36868
  98.2 5.7 %collective-permute-start.8 = (f32[2,4,4096]{2,1,0:T(4,128)S(1)}, f32[2,4,4096]{2,1,0:T(4,128)S(1)}, u32[]{:S(2)}, u32[]{:S(2)}) collective-permute-start(f32[2,4,4096]{2,1,0:T(4,128)S(1)} %broadcast_select_fusion.6), channel_id=1, source_target_pairs={{0,64},{64,0},{128,192},{192,128},{1,65},{65,1},{129,193},{193,129... | collective-permute-start | bytes 393224 | tf_op jit(solution)/shard_map/ppermute | solution.py:248
  104.0 10.5 %collective-permute-start.9 = (f32[2,2,4096]{2,1,0:T(2,128)S(1)}, f32[2,2,4096]{2,1,0:T(2,128)S(1)}, u32[]{:S(2)}, u32[]{:S(2)}) collective-permute-start(f32[2,2,4096]{2,1,0:T(2,128)S(1)} %broadcast_select_fusion.3), channel_id=1, source_target_pairs={{0,128},{64,192},{128,0},{192,64},{1,129},{65,193},{129,1},{193,65... | collective-permute-start | bytes 196616 | tf_op jit(solution)/shard_map/ppermute | solution.py:248
  108.8 42.8 %all-to-all-start.1 = ((f32[32,1,4096]{2,1,0:T(1,128)}), f32[32,1,4096]{2,1,0:T(1,128)S(1)}, u32[]{:S(2)}, u32[]{:S(2)}) async-start(f32[32,1,4096]{2,1,0:T(1,128)} %back.1), calls=%async_computation.1 | async-start | bytes 1048576 | tf_op jit(solution)/shard_map/all_to_all | solution.py:344
  114.8 24.3 %collective-permute-start.10 = (f32[2,4096]{1,0:T(2,128)S(1)}, f32[2,4096]{1,0:T(2,128)S(1)}, u32[]{:S(2)}, u32[]{:S(2)}) collective-permute-start(f32[2,4096]{1,0:T(2,128)S(1)} %fusion.2), channel_id=1, source_target_pairs={{0,0},{256,1},{128,2},{384,3},{64,4},{320,5},{192,6},{448,7},{32,8... | collective-permute-start | bytes 98312 | tf_op jit(solution)/shard_map/ppermute | solution.py:350
  127.1 23.8 %collective-permute-start.11 = (f32[2,4096]{1,0:T(2,128)S(1)}, f32[2,4096]{1,0:T(2,128)S(1)}, u32[]{:S(2)}, u32[]{:S(2)}) collective-permute-start(f32[2,4096]{1,0:T(2,128)S(1)} %bitcast.35), channel_id=1, source_target_pairs={{256,0},{0,1},{384,2},{128,3},{320,4},{64,5},{448,6},{192,7},{288,... | collective-permute-start | bytes 98312 | tf_op jit(solution)/shard_map/ppermute | solution.py:350

commit v5 on v4

--- a/solution.py
+++ b/solution.py
@@ -162,15 +162,22 @@
 
 
 def inverse_rows(
-    sign, first_ref, filt_ref, small_ref, twiddle_ref, tables, rows_ref, turned_ref
+    sign, odd_ref, first_ref, mine_ref, other_ref, small_ref, twiddle_ref, tables, rows_ref,
+    turned_ref,
 ):
     cos_hi, cos_lo, sin_hi, sin_lo = tables
     classes = first_ref.shape[0]
     points = cos_hi.shape[0]
+    odd = odd_ref[0] == 1
+
+    def filt(at):
+        mine, other = mine_ref[:, at], other_ref[:, at]
+        return jnp.concatenate([jnp.where(odd, other, mine), jnp.where(odd, mine, other)], axis=0)
+
     for channel in range(2):
         real_at = slice(channel * points, (channel + 1) * points)
         imag_at = slice((2 + channel) * points, (3 + channel) * points)
-        filt_real, filt_imag = filt_ref[:, real_at], filt_ref[:, imag_at] * sign
+        filt_real, filt_imag = filt(real_at), filt(imag_at) * sign
         first_real, first_imag = first_ref[:, real_at], first_ref[:, imag_at]
         keep_quarters(
             rows_ref,
@@ -203,24 +210,26 @@
 
 
 def conv_kernel(
-    moved_ref, filt_ref, small_ref, twiddle_ref, cos_hi, cos_lo, sin_hi, sin_lo, conv_ref, rows_ref,
-    turned_ref,
+    odd_ref, moved_ref, mine_ref, other_ref, small_ref, twiddle_ref, cos_hi, cos_lo, sin_hi, sin_lo,
+    conv_ref, rows_ref, turned_ref,
 ):
     tables = (cos_hi, cos_lo, sin_hi, sin_lo)
     conv_ref[...] = inverse_rows(
-        1.0, moved_ref, filt_ref, small_ref, twiddle_ref, tables, rows_ref, turned_ref
+        1.0, odd_ref, moved_ref, mine_ref, other_ref, small_ref, twiddle_ref, tables, rows_ref,
+        turned_ref,
     )
 
 
 def back_kernel(
-    conv_ref, spec_ref, filt_ref, small_ref, twiddle_ref, cos_hi, cos_lo, sin_hi, sin_lo, packed_ref,
-    rows_ref, turned_ref,
+    odd_ref, conv_ref, spec_ref, mine_ref, other_ref, small_ref, twiddle_ref, cos_hi, cos_lo,
+    sin_hi, sin_lo, packed_ref, rows_ref, turned_ref,
 ):
     tables = (cos_hi, cos_lo, sin_hi, sin_lo)
     width = conv_ref.shape[1]
     packed_ref[:, 0, :width] = conv_ref[...]
     packed_ref[:, 0, width:] = inverse_rows(
-        -1.0, spec_ref, filt_ref, small_ref, twiddle_ref, tables, rows_ref, turned_ref
+        -1.0, odd_ref, spec_ref, mine_ref, other_ref, small_ref, twiddle_ref, tables, rows_ref,
+        turned_ref,
     )
 
 
@@ -251,7 +260,7 @@
 def doubling(values, upper, axis, pairs):
     other = lax.ppermute(values, axis, pairs)
     return jnp.concatenate(
-        [jnp.where(upper, other, values), jnp.where(upper, values, other)], axis=1
+        [jnp.where(upper, other, values), jnp.where(upper, values, other)], axis=0
     )
 
 
@@ -285,15 +294,18 @@
     cores = [(0, 1), (1, 0)]
     half_row = 4 * positions
     got = [lax.ppermute(filter_spectrum, everyone, pairs[number]) for number in range(2)]
-    ordered = [jnp.where(upper_zhi, got[1 - n], got[n]) for n in range(2)]
-    mine = jnp.stack([jnp.where(odd, v[:, per_seq:], v[:, :per_seq]) for v in ordered])
-    away = jnp.stack([jnp.where(odd, v[:, :per_seq], v[:, per_seq:]) for v in ordered])
-    other = lax.ppermute(away, "y", near_y)
-    mine, other = mine.reshape(2, half_row), other.reshape(2, half_row)
-    filters = jnp.stack([jnp.where(odd, other, mine), jnp.where(odd, mine, other)])
+    filters = jnp.stack([jnp.where(upper_zhi, got[1 - n], got[n]) for n in range(2)])
+    filters = (
+        filters.reshape(2, 2, 2, per_seq, positions)
+        .transpose(0, 2, 1, 3, 4)
+        .reshape(2, 2 * half_row)
+    )
     filters = doubling(filters, x_index >= 2, "x", far_x)
     filters = doubling(filters, x_index % 2 == 1, "x", near_x)
-    filters = doubling(filters, upper_core, "core", cores).reshape(seq_count, half_row)
+    filters = doubling(filters, upper_core, "core", cores)
+    mine = jnp.where(odd, filters[:, half_row:], filters[:, :half_row])
+    away = jnp.where(odd, filters[:, :half_row], filters[:, half_row:])
+    filters = (mine, lax.ppermute(away, "y", near_y))
 
     tables = root_tables(positions)
     small_out = small_table(seq_count, False)
@@ -307,11 +319,12 @@
     turned = [pltpu.VMEM((6 * seq_count, 2 * positions), bf16)]
     cost = pl.CostEstimate(flops=2 * 10**9, bytes_accessed=10**7, transcendentals=0)
 
-    vmem = pl.BlockSpec(memory_space=pltpu.VMEM)
+    smem, vmem = pl.BlockSpec(memory_space=pltpu.SMEM), pl.BlockSpec(memory_space=pltpu.VMEM)
+    parity = odd.astype(jnp.int32).reshape(1)
     spec, kept, away = pl.pallas_call(
         forward_kernel,
         out_shape=[wide, part, part],
-        in_specs=[pl.BlockSpec(memory_space=pltpu.SMEM)] + [vmem] * 7,
+        in_specs=[smem] + [vmem] * 7,
         scratch_shapes=rows,
         name="forward",
         compiler_params=params,
@@ -329,18 +342,20 @@
         conv_kernel,
         out_shape=jax.ShapeDtypeStruct((seq_count, 2 * positions), f32),
         scratch_shapes=rows + turned,
+        in_specs=[smem] + [vmem] * 9,
         name="conv",
         compiler_params=params,
         cost_estimate=cost,
-    )(moved, filters, small_back, twiddle, *tables)
+    )(parity, moved, *filters, small_back, twiddle, *tables)
     signals = pl.pallas_call(
         back_kernel,
         out_shape=jax.ShapeDtypeStruct((seq_count, 1, 4 * positions), f32),
         scratch_shapes=rows + turned,
+        in_specs=[smem] + [vmem] * 10,
         name="back",
         compiler_params=params,
         cost_estimate=cost,
-    )(conv, spec, filters, small_back, twiddle, *tables)
+    )(parity, conv, spec, *filters, small_back, twiddle, *tables)
     returned = lax.all_to_all(signals, SEQ, split_axis=0, concat_axis=0, tiled=True)
     returned = returned.reshape(seq_count, 4 * positions)
 

time: 154 us -> 160 us (1.039)
  starting transfers between devices: 69.1 us -> 74.2 us
  local copies, waits for them, and re-layouts: 3.2 us -> 4.84 us
    all_to_all x1, waiting for transfers between devices: 21.9 us -> 27.7 us  [step(): moved = lax.all_to_all(packed, SEQ, split_axis=0, concat_axis=0, tiled=True)]
    ppermute x3, waiting for transfers between devices: 10.2 us -> 4.71 us  [doubling(): other = lax.ppermute(values, axis, pairs)]
    ppermute x1, waiting for transfers between devices: 0.01 us -> 3.65 us  [step(): filters = (mine, lax.ppermute(away, 'y', near_y))]
    ppermute x1, waiting for transfers between devices: 4.84 us -> 1.23 us  [step(): other = lax.ppermute(jnp.where(odd, total[0], total[1]), 'y', near_y)]
    ppermute x1, starting transfers between devices: 1.92 us -> 4.66 us  [step(): total = kept + lax.ppermute(away, 'core', cores)]
    ppermute x2, starting transfers between devices: 3.84 us -> 5.94 us  [halving(): return kept + lax.ppermute(away, axis, pairs)]
    ppermute x2, waiting for transfers between devices: 1.73 us -> 0.01 us  [halving(): return kept + lax.ppermute(away, axis, pairs)]
    unnamed x23 -> x21, local copies, waits for them, and re-layouts: 1.67 us -> 3.27 us
  transfers between devices with their start and end apart: 14 -> 14, of which waited for: 9 -> 8; matrix products, arithmetic and copies ran while one was open for 2% -> 2% of each run, Pallas kernels for 6% -> 6%
where the time goes in v5:
time: 160 us; the launch traced here: 159 us
  starting transfers between devices  74.2 us (46%)
  waiting for transfers between devices  66.6 us (42%)
  Pallas kernels  9.04 us (6%)
  local copies, waits for them, and re-layouts  4.84 us (3%)
  other arithmetic  3.17 us (2%)
    all_to_all x1, waiting for transfers between devices, step(): moved = lax.all_to_all(packed, SEQ, split_axis=0, concat_axis=0, tiled=True)  27.7 us
    ppermute x2, waiting for transfers between devices, step(): lax.ppermute(rows_out[number], everyone, [(b, a) for a, b in pairs[number]])  22.6 us
    ppermute x2, starting transfers between devices, step(): lax.ppermute(filter_spectrum, everyone, pairs[number])  22.6 us
    ppermute x2, starting transfers between devices, step(): lax.ppermute(rows_out[number], everyone, [(b, a) for a, b in pairs[number]])  13.7 us
    all_to_all x1, starting transfers between devices, step(): moved = lax.all_to_all(packed, SEQ, split_axis=0, concat_axis=0, tiled=True)  9.5 us
    ppermute x3, starting transfers between devices, doubling(): other = lax.ppermute(values, axis, pairs)  6.9 us
    ppermute x2, waiting for transfers between devices, step(): lax.ppermute(filter_spectrum, everyone, pairs[number])  6.62 us
    ppermute x2, starting transfers between devices, halving(): return kept + lax.ppermute(away, axis, pairs)  5.94 us
  transfers between devices with their start and end apart: 14, of which 8 were waited for; matrix products, arithmetic and copies ran while one was open for 2% of the time, Pallas kernels for 6%

profile of v5, /device:TPU:7, one launch (start us, length us, event | category | flops | bytes accessed | tf_op | source)
XLA Modules:
  0.0 158.9 jit_solution(16655757626903346255)
XLA Ops:
  0.6 0.0 copy-start
  0.6 17.3 %collective-permute-start = (f32[2,4,1024]{2,1,0:T(4,128)}, f32[2,4,1024]{2,1,0:T(4,128)S(1)}, u32[]{:S(2)}, u32[]{:S(2)}) collective-permute-start(f32[2,4,1024]{2,1,0:T(4,128)} %param.12), channel_id=1, source_target_pairs={{0,256},{1,0},{2,384},{3,128},{4,320},{5,64},{6,448},{7,192},{8,28... | collective-permute-start | bytes 98312 | tf_op jit(solution)/shard_map/ppermute | solution.py:296
  18.0 5.2 %collective-permute-start.1 = (f32[2,4,1024]{2,1,0:T(4,128)}, f32[2,4,1024]{2,1,0:T(4,128)S(1)}, u32[]{:S(2)}, u32[]{:S(2)}) collective-permute-start(f32[2,4,1024]{2,1,0:T(4,128)} %param.12), channel_id=1, source_target_pairs={{0,0},{1,256},{2,128},{3,384},{4,64},{5,320},{6,192},{7,448},{8,32... | collective-permute-start | bytes 98312 | tf_op jit(solution)/shard_map/ppermute | solution.py:296
  23.2 0.0 collective-permute-done
  23.2 6.6 %collective-permute-done.1 = f32[2,4,1024]{2,1,0:T(4,128)S(1)} collective-permute-done((f32[2,4,1024]{2,1,0:T(4,128)}, f32[2,4,1024]{2,1,0:T(4,128)S(1)}, u32[]{:S(2)}, u32[]{:S(2)}) %collective-permute-start.1) | collective-permute-done | bytes 32800 | tf_op jit(solution)/shard_map/ppermute | solution.py:296
  30.0 0.1 reshape.80
  30.1 1.9 %collective-permute-start.2 = (f32[2,8192]{1,0:T(2,128)S(1)}, f32[2,8192]{1,0:T(2,128)S(1)}, u32[]{:S(2)}, u32[]{:S(2)}) collective-permute-start(f32[2,8192]{1,0:T(2,128)S(1)} %reshape.80), channel_id=1, source_target_pairs={{0,128},{64,192},{128,0},{192,64},{1,129},{65,193},{129,1},{193,65... | collective-permute-start | bytes 196616 | tf_op jit(solution)/shard_map/ppermute | solution.py:261
  32.0 0.0 copy-done
  32.0 0.0 copy-start.1
  32.0 0.9 copy-done.1
  32.9 0.0 copy-start.3
  32.9 0.9 copy-done.3
  33.8 1.4 pack.1
  35.2 9.5 %all-to-all-start = ((f32[32,1,6144]{2,1,0:T(1,128)}), f32[32,1,6144]{2,1,0:T(1,128)S(1)}, u32[]{:S(2)}, u32[]{:S(2)}) async-start(f32[32,1,6144]{2,1,0:T(1,128)} %pack.1), calls=%async_computation | async-start | bytes 1572864 | tf_op jit(solution)/shard_map/all_to_all | solution.py:288
  44.8 0.0 collective-permute-done.2
  44.8 0.1 pad_maximum_fusion.3
  44.9 1.9 %collective-permute-start.3 = (f32[4,8192]{1,0:T(4,128)S(1)}, f32[4,8192]{1,0:T(4,128)S(1)}, u32[]{:S(2)}, u32[]{:S(2)}) collective-permute-start(f32[4,8192]{1,0:T(4,128)S(1)} %pad_maximum_fusion.3), channel_id=1, source_target_pairs={{0,64},{64,0},{128,192},{192,128},{1,65},{65,1},{129,193},{193,129... | collective-permute-start | bytes 393224 | tf_op jit(solution)/shard_map/ppermute | solution.py:261
  46.8 4.7 %collective-permute-done.3 = f32[4,8192]{1,0:T(4,128)S(1)} collective-permute-done((f32[4,8192]{1,0:T(4,128)S(1)}, f32[4,8192]{1,0:T(4,128)S(1)}, u32[]{:S(2)}, u32[]{:S(2)}) %collective-permute-start.3) | collective-permute-done | bytes 131104 | tf_op jit(solution)/shard_map/ppermute | solution.py:261
  51.5 0.1 broadcast_select_fusion.10
  51.6 0.0 copy-start.4
  51.6 0.0 copy-start.5
  51.7 0.8 pad_maximum_fusion.1
  52.4 3.1 %collective-permute-start.4 = (f32[8,8192]{1,0:T(8,128)}, f32[8,8192]{1,0:T(8,128)}, u32[]{:S(2)}, u32[]{:S(2)}) collective-permute-start(f32[8,8192]{1,0:T(8,128)} %pad_maximum_fusion.1), channel_id=1, source_target_pairs={{0,32},{32,0},{1,33},{33,1},{2,34},{34,2},{3,35},{35,3},{4,36},{36... | collective-permute-start | bytes 786440 | tf_op jit(solution)/shard_map/ppermute | solution.py:261
  55.5 0.0 copy-done.4
  55.5 0.0 copy-done.5
  55.5 0.6 root_tables.1
  56.2 0.0 copy-start.6
  56.2 0.0 copy-start.8
  56.2 27.7 %all-to-all-done = f32[32,1,6144]{2,1,0:T(1,128)S(1)} async-done(((f32[32,1,6144]{2,1,0:T(1,128)}), f32[32,1,6144]{2,1,0:T(1,128)S(1)}, u32[]{:S(2)}, u32[]{:S(2)}) %all-to-all-start) | async-done | bytes 786464 | tf_op jit(solution)/shard_map/all_to_all | solution.py:288
  83.9 0.2 copy.40
  84.1 0.0 copy-done.6
  84.1 0.0 copy-done.8
  84.1 2.0 %forward.1 = (f32[32,4096]{1,0:T(8,128)S(1)}, f32[2,8,4096]{2,1,0:T(8,128)S(1)}, f32[2,8,4096]{2,1,0:T(8,128)S(1)}) custom-call(s32[1]{0:T(128)} %bitcast.2.core_ref, f32[32,6144]{1,0:T(8,128)S(1)} %bitcast.23, bf16[64,96]{1,0:T(8,128)(2,1)S(1)} %copy-done.8, f32[2,32,1024]{2,1,0:T(8,128)S(1)} %copy-done.6, bf16[1024,256]{1,0:T(8,128)(2,1)S(1)} %get-tuple-element.10.cos_hi, ...), custom_call_target="tpu_custom_call" | custom-call | flops 2000000000 | bytes 10000000 | tf_op jit(solution)/shard_map/forward/pallas_call | solution.py:324
  86.2 4.7 %collective-permute-start.6 = (f32[2,8,4096]{2,1,0:T(8,128)S(1)}, f32[2,8,4096]{2,1,0:T(8,128)S(1)}, u32[]{:S(2)}, u32[]{:S(2)}) collective-permute-start(f32[2,8,4096]{2,1,0:T(8,128)S(1)} %get-tuple-element.16), channel_id=1, source_target_pairs={{0,32},{32,0},{1,33},{33,1},{2,34},{34,2},{3,35},{35,3},{4,36},{36... | collective-permute-start | bytes 786440 | tf_op jit(solution)/shard_map/ppermute | solution.py:334
  90.9 0.0 collective-permute-done.4
  90.9 1.0 broadcast_select_fusion.1
  91.9 0.1 collective-permute-done.6
  92.1 1.9 %collective-permute-start.7 = (f32[8,4096]{1,0:T(8,128)S(1)}, f32[8,4096]{1,0:T(8,128)S(1)}, u32[]{:S(2)}, u32[]{:S(2)}) collective-permute-start(f32[8,4096]{1,0:T(8,128)S(1)} %get-tuple-element.24), channel_id=1, source_target_pairs={{0,1},{1,0},{2,3},{3,2},{4,5},{5,4},{6,7},{7,6},{8,9},{9,8},{10,11... | collective-permute-start | bytes 393224 | tf_op jit(solution)/shard_map/ppermute | solution.py:336
  94.1 3.4 %collective-permute-start.5 = (f32[16,4096]{1,0:T(8,128)S(1)}, f32[16,4096]{1,0:T(8,128)S(1)}, u32[]{:S(2)}, u32[]{:S(2)}) collective-permute-start(f32[16,4096]{1,0:T(8,128)S(1)} %get-tuple-element.19), channel_id=1, source_target_pairs={{0,1},{1,0},{2,3},{3,2},{4,5},{5,4},{6,7},{7,6},{8,9},{9,8},{10,11... | collective-permute-start | bytes 786440 | tf_op jit(solution)/shard_map/ppermute | solution.py:308
  97.4 1.2 collective-permute-done.7
  98.7 0.0 copy-start.7
  98.7 1.9 %collective-permute-start.8 = (f32[2,4,4096]{2,1,0:T(4,128)S(1)}, f32[2,4,4096]{2,1,0:T(4,128)S(1)}, u32[]{:S(2)}, u32[]{:S(2)}) collective-permute-start(f32[2,4,4096]{2,1,0:T(4,128)S(1)} %broadcast_select_fusion.5), channel_id=1, source_target_pairs={{0,64},{64,0},{128,192},{192,128},{1,65},{65,1},{129,193},{193,129... | collective-permute-start | bytes 393224 | tf_op jit(solution)/shard_map/ppermute | solution.py:257
  100.6 3.7 %collective-permute-done.5.other_ref = f32[16,4096]{1,0:T(8,128)S(1)} collective-permute-done((f32[16,4096]{1,0:T(8,128)S(1)}, f32[16,4096]{1,0:T(8,128)S(1)}, u32[]{:S(2)}, u32[]{:S(2)}) %collective-permute-start.5) | collective-permute-done | bytes 262176 | tf_op jit(solution)/shard_map/ppermute | solution.py:308
  104.3 0.0 copy-done.7
  104.3 2.1 %conv.1.conv_ref = f32[32,2048]{1,0:T(8,128)S(1)} custom-call(s32[1]{0:T(128)} %bitcast.odd_ref, f32[32,6144]{1,0:T(8,128)S(1)} %bitcast.24, f32[16,4096]{1,0:T(8,128)S(1)} %get-tuple-element.20.mine_ref, f32[16,4096]{1,0:T(8,128)S(1)} %collective-permute-done.5.other_ref, bf16[32,192]{1,0:T(8,128)(2,1)S(1)} %copy-done.7, f32[2,32,1024]{2,1,0:T(8,128)S(1)} %copy-done.6, ...), custom_call_target="tpu_custom_call" | custom-call | flops 2000000000 | bytes 10000000 | tf_op jit(solution)/shard_map/conv/pallas_call | solution.py:341
  106.3 0.0 collective-permute-done.8
  106.4 4.0 %collective-permute-start.9 = (f32[2,2,4096]{2,1,0:T(2,128)S(1)}, f32[2,2,4096]{2,1,0:T(2,128)S(1)}, u32[]{:S(2)}, u32[]{:S(2)}) collective-permute-start(f32[2,2,4096]{2,1,0:T(2,128)S(1)} %broadcast_select_fusion.6), channel_id=1, source_target_pairs={{0,128},{64,192},{128,0},{192,64},{1,129},{65,193},{129,1},{193,65... | collective-permute-start | bytes 196616 | tf_op jit(solution)/shard_map/ppermute | solution.py:257
  110.5 2.9 %back.1 = f32[32,1,4096]{2,1,0:T(1,128)} custom-call(s32[1]{0:T(128)} %bitcast.odd_ref, f32[32,2048]{1,0:T(8,128)S(1)} %conv.1.conv_ref, f32[32,4096]{1,0:T(8,128)S(1)} %get-tuple-element.14.spec_ref, f32[16,4096]{1,0:T(8,128)S(1)} %get-tuple-element.20.mine_ref, f32[16,4096]{1,0:T(8,128)S(1)} %collective-permute-done.5.other_ref, ...), custom_call_target="tpu_custom_call" | custom-call | flops 2000000000 | bytes 10000000 | tf_op jit(solution)/shard_map/back/pallas_call | solution.py:350
  113.3 5.6 %all-to-all-start.1 = ((f32[32,1,4096]{2,1,0:T(1,128)}), f32[32,1,4096]{2,1,0:T(1,128)S(1)}, u32[]{:S(2)}, u32[]{:S(2)}) async-start(f32[32,1,4096]{2,1,0:T(1,128)} %back.1), calls=%async_computation.1 | async-start | bytes 1048576 | tf_op jit(solution)/shard_map/all_to_all | solution.py:359
  118.9 0.0 collective-permute-done.9
  118.9 0.1 select_add_fusion.1
  119.0 0.1 broadcast_select_fusion.4
  119.2 8.7 %collective-permute-start.10 = (f32[2,4096]{1,0:T(2,128)S(1)}, f32[2,4096]{1,0:T(2,128)S(1)}, u32[]{:S(2)}, u32[]{:S(2)}) collective-permute-start(f32[2,4096]{1,0:T(2,128)S(1)} %fusion.3), channel_id=1, source_target_pairs={{0,0},{256,1},{128,2},{384,3},{64,4},{320,5},{192,6},{448,7},{32,8... | collective-permute-start | bytes 98312 | tf_op jit(solution)/shard_map/ppermute | solution.py:365
  127.9 5.0 %collective-permute-start.11 = (f32[2,4096]{1,0:T(2,128)S(1)}, f32[2,4096]{1,0:T(2,128)S(1)}, u32[]{:S(2)}, u32[]{:S(2)}) collective-permute-start(f32[2,4096]{1,0:T(2,128)S(1)} %bitcast.31), channel_id=1, source_target_pairs={{256,0},{0,1},{384,2},{128,3},{320,4},{64,5},{448,6},{192,7},{288,... | collective-permute-start | bytes 98312 | tf_op jit(solution)/shard_map/ppermute | solution.py:365
  133.0 6.4 %collective-permute-done.10 = f32[2,4096]{1,0:T(2,128)S(1)} collective-permute-done((f32[2,4096]{1,0:T(2,128)S(1)}, f32[2,4096]{1,0:T(2,128)S(1)}, u32[]{:S(2)}, u32[]{:S(2)}) %collective-permute-start.10) | collective-permute-done | bytes 32800 | tf_op jit(solution)/shard_map/ppermute | solution.py:365
  139.4 16.2 %collective-permute-done.11 = f32[2,4096]{1,0:T(2,128)S(1)} collective-permute-done((f32[2,4096]{1,0:T(2,128)S(1)}, f32[2,4096]{1,0:T(2,128)S(1)}, u32[]{:S(2)}, u32[]{:S(2)}) %collective-permute-start.11) | collective-permute-done | bytes 32800 | tf_op jit(solution)/shard_map/ppermute | solution.py:365
  155.6 0.6 reshape.85
  156.3 0.0 all-to-all-done.1
  156.3 0.3 copy.41
  156.6 0.0 copy-start.2
  156.7 0.8 copy-done.2
  157.6 0.7 multiply_convert_fusion
  158.2 0.7 convert_element_type.23
  (19 shorter events, 0.6 us)
Async XLA Ops:
  0.6 31.4 %copy-start = (f32[1,2,64,1024]{3,2,1,0:T(8,128)S(1)}, f32[1,2,64,1024]{3,2,1,0:T(8,128)}, u32[]{:S(2)}) copy-start(f32[1,2,64,1024]{3,2,1,0:T(8,128)} %spec_ref.1) | copy-start | bytes 1572868
  0.6 22.6 %collective-permute-start = (f32[2,4,1024]{2,1,0:T(4,128)}, f32[2,4,1024]{2,1,0:T(4,128)S(1)}, u32[]{:S(2)}, u32[]{:S(2)}) collective-permute-start(f32[2,4,1024]{2,1,0:T(4,128)} %param.12), channel_id=1, source_target_pairs={{0,256},{1,0},{2,384},{3,128},{4,320},{5,64},{6,448},{7,192},{8,28... | collective-permute-start | bytes 98312 | tf_op jit(solution)/shard_map/ppermute | solution.py:296
  18.0 11.9 %collective-permute-start.1 = (f32[2,4,1024]{2,1,0:T(4,128)}, f32[2,4,1024]{2,1,0:T(4,128)S(1)}, u32[]{:S(2)}, u32[]{:S(2)}) collective-permute-start(f32[2,4,1024]{2,1,0:T(4,128)} %param.12), channel_id=1, source_target_pairs={{0,0},{1,256},{2,128},{3,384},{4,64},{5,320},{6,192},{7,448},{8,32... | collective-permute-start | bytes 98312 | tf_op jit(solution)/shard_map/ppermute | solution.py:296
  30.1 14.7 %collective-permute-start.2 = (f32[2,8192]{1,0:T(2,128)S(1)}, f32[2,8192]{1,0:T(2,128)S(1)}, u32[]{:S(2)}, u32[]{:S(2)}) collective-permute-start(f32[2,8192]{1,0:T(2,128)S(1)} %reshape.80), channel_id=1, source_target_pairs={{0,128},{64,192},{128,0},{192,64},{1,129},{65,193},{129,1},{193,65... | collective-permute-start | bytes 196616 | tf_op jit(solution)/shard_map/ppermute | solution.py:261
  32.0 0.9 copy-start.1
  32.9 0.9 copy-start.3
  35.2 48.6 %all-to-all-start = ((f32[32,1,6144]{2,1,0:T(1,128)}), f32[32,1,6144]{2,1,0:T(1,128)S(1)}, u32[]{:S(2)}, u32[]{:S(2)}) async-start(f32[32,1,6144]{2,1,0:T(1,128)} %pack.1), calls=%async_computation | async-start | bytes 1572864 | tf_op jit(solution)/shard_map/all_to_all | solution.py:288
  44.9 6.6 %collective-permute-start.3 = (f32[4,8192]{1,0:T(4,128)S(1)}, f32[4,8192]{1,0:T(4,128)S(1)}, u32[]{:S(2)}, u32[]{:S(2)}) collective-permute-start(f32[4,8192]{1,0:T(4,128)S(1)} %pad_maximum_fusion.3), channel_id=1, source_target_pairs={{0,64},{64,0},{128,192},{192,128},{1,65},{65,1},{129,193},{193,129... | collective-permute-start | bytes 393224 | tf_op jit(solution)/shard_map/ppermute | solution.py:261
  51.6 3.9 %copy-start.4 = (f32[2,32,256]{2,1,0:T(8,128)S(1)}, f32[2,32,256]{2,1,0:T(8,128)}, u32[]{:S(2)}) copy-start(f32[2,32,256]{2,1,0:T(8,128)} %constant.57.clone.coarse_ref) | copy-start | bytes 196612
  51.6 3.9 %copy-start.5 = (f32[2,32,256]{2,1,0:T(8,128)S(1)}, f32[2,32,256]{2,1,0:T(8,128)}, u32[]{:S(2)}) copy-start(f32[2,32,256]{2,1,0:T(8,128)} %constant.58.clone.fine_ref) | copy-start | bytes 196612
  52.4 38.5 %collective-permute-start.4 = (f32[8,8192]{1,0:T(8,128)}, f32[8,8192]{1,0:T(8,128)}, u32[]{:S(2)}, u32[]{:S(2)}) collective-permute-start(f32[8,8192]{1,0:T(8,128)} %pad_maximum_fusion.1), channel_id=1, source_target_pairs={{0,32},{32,0},{1,33},{33,1},{2,34},{34,2},{3,35},{35,3},{4,36},{36... | collective-permute-start | bytes 786440 | tf_op jit(solution)/shard_map/ppermute | solution.py:261
  56.2 28.0 %copy-start.6 = (f32[2,32,1024]{2,1,0:T(8,128)S(1)}, f32[2,32,1024]{2,1,0:T(8,128)}, u32[]{:S(2)}) copy-start(f32[2,32,1024]{2,1,0:T(8,128)} %constant.61.clone.twiddle_ref) | copy-start | bytes 786436
  56.2 28.0 %copy-start.8 = (bf16[64,96]{1,0:T(8,128)(2,1)S(1)}, bf16[64,96]{1,0:T(8,128)(2,1)}, u32[]{:S(2)}) copy-start(bf16[64,96]{1,0:T(8,128)(2,1)} %constant.59.clone.small_ref) | copy-start | bytes 36868
  86.2 5.8 %collective-permute-start.6 = (f32[2,8,4096]{2,1,0:T(8,128)S(1)}, f32[2,8,4096]{2,1,0:T(8,128)S(1)}, u32[]{:S(2)}, u32[]{:S(2)}) collective-permute-start(f32[2,8,4096]{2,1,0:T(8,128)S(1)} %get-tuple-element.16), channel_id=1, source_target_pairs={{0,32},{32,0},{1,33},{33,1},{2,34},{34,2},{3,35},{35,3},{4,36},{36... | collective-permute-start | bytes 786440 | tf_op jit(solution)/shard_map/ppermute | solution.py:334
  92.1 6.6 %collective-permute-start.7 = (f32[8,4096]{1,0:T(8,128)S(1)}, f32[8,4096]{1,0:T(8,128)S(1)}, u32[]{:S(2)}, u32[]{:S(2)}) collective-permute-start(f32[8,4096]{1,0:T(8,128)S(1)} %get-tuple-element.24), channel_id=1, source_target_pairs={{0,1},{1,0},{2,3},{3,2},{4,5},{5,4},{6,7},{7,6},{8,9},{9,8},{10,11... | collective-permute-start | bytes 393224 | tf_op jit(solution)/shard_map/ppermute | solution.py:336
  94.1 10.2 %collective-permute-start.5 = (f32[16,4096]{1,0:T(8,128)S(1)}, f32[16,4096]{1,0:T(8,128)S(1)}, u32[]{:S(2)}, u32[]{:S(2)}) collective-permute-start(f32[16,4096]{1,0:T(8,128)S(1)} %get-tuple-element.19), channel_id=1, source_target_pairs={{0,1},{1,0},{2,3},{3,2},{4,5},{5,4},{6,7},{7,6},{8,9},{9,8},{10,11... | collective-permute-start | bytes 786440 | tf_op jit(solution)/shard_map/ppermute | solution.py:308
  98.7 5.6 %copy-start.7 = (bf16[32,192]{1,0:T(8,128)(2,1)S(1)}, bf16[32,192]{1,0:T(8,128)(2,1)}, u32[]{:S(2)}) copy-start(bf16[32,192]{1,0:T(8,128)(2,1)} %constant.60.clone.small_ref) | copy-start | bytes 36868
  98.7 7.6 %collective-permute-start.8 = (f32[2,4,4096]{2,1,0:T(4,128)S(1)}, f32[2,4,4096]{2,1,0:T(4,128)S(1)}, u32[]{:S(2)}, u32[]{:S(2)}) collective-permute-start(f32[2,4,4096]{2,1,0:T(4,128)S(1)} %broadcast_select_fusion.5), channel_id=1, source_target_pairs={{0,64},{64,0},{128,192},{192,128},{1,65},{65,1},{129,193},{193,129... | collective-permute-start | bytes 393224 | tf_op jit(solution)/shard_map/ppermute | solution.py:257
  106.4 12.5 %collective-permute-start.9 = (f32[2,2,4096]{2,1,0:T(2,128)S(1)}, f32[2,2,4096]{2,1,0:T(2,128)S(1)}, u32[]{:S(2)}, u32[]{:S(2)}) collective-permute-start(f32[2,2,4096]{2,1,0:T(2,128)S(1)} %broadcast_select_fusion.6), channel_id=1, source_target_pairs={{0,128},{64,192},{128,0},{192,64},{1,129},{65,193},{129,1},{193,65... | collective-permute-start | bytes 196616 | tf_op jit(solution)/shard_map/ppermute | solution.py:257
  113.3 42.9 %all-to-all-start.1 = ((f32[32,1,4096]{2,1,0:T(1,128)}), f32[32,1,4096]{2,1,0:T(1,128)S(1)}, u32[]{:S(2)}, u32[]{:S(2)}) async-start(f32[32,1,4096]{2,1,0:T(1,128)} %back.1), calls=%async_computation.1 | async-start | bytes 1048576 | tf_op jit(solution)/shard_map/all_to_all | solution.py:359
  119.2 20.2 %collective-permute-start.10 = (f32[2,4096]{1,0:T(2,128)S(1)}, f32[2,4096]{1,0:T(2,128)S(1)}, u32[]{:S(2)}, u32[]{:S(2)}) collective-permute-start(f32[2,4096]{1,0:T(2,128)S(1)} %fusion.3), channel_id=1, source_target_pairs={{0,0},{256,1},{128,2},{384,3},{64,4},{320,5},{192,6},{448,7},{32,8... | collective-permute-start | bytes 98312 | tf_op jit(solution)/shard_map/ppermute | solution.py:365
  127.9 27.6 %collective-permute-start.11 = (f32[2,4096]{1,0:T(2,128)S(1)}, f32[2,4096]{1,0:T(2,128)S(1)}, u32[]{:S(2)}, u32[]{:S(2)}) collective-permute-start(f32[2,4096]{1,0:T(2,128)S(1)} %bitcast.31), channel_id=1, source_target_pairs={{256,0},{0,1},{384,2},{128,3},{320,4},{64,5},{448,6},{192,7},{288,... | collective-permute-start | bytes 98312 | tf_op jit(solution)/shard_map/ppermute | solution.py:365
  156.6 0.9 copy-start.2

commit v6 on v4

--- a/solution.py
+++ b/solution.py
@@ -203,23 +203,21 @@
 
 
 def conv_kernel(
-    moved_ref, filt_ref, small_ref, twiddle_ref, cos_hi, cos_lo, sin_hi, sin_lo, conv_ref, rows_ref,
+    moved_ref, filt_ref, small_ref, twiddle_ref, cos_hi, cos_lo, sin_hi, sin_lo, packed_ref, rows_ref,
     turned_ref,
 ):
     tables = (cos_hi, cos_lo, sin_hi, sin_lo)
-    conv_ref[...] = inverse_rows(
+    packed_ref[:, 0, :] = inverse_rows(
         1.0, moved_ref, filt_ref, small_ref, twiddle_ref, tables, rows_ref, turned_ref
     )
 
 
 def back_kernel(
-    conv_ref, spec_ref, filt_ref, small_ref, twiddle_ref, cos_hi, cos_lo, sin_hi, sin_lo, packed_ref,
-    rows_ref, turned_ref,
+    spec_ref, filt_ref, small_ref, twiddle_ref, cos_hi, cos_lo, sin_hi, sin_lo, packed_ref, rows_ref,
+    turned_ref,
 ):
     tables = (cos_hi, cos_lo, sin_hi, sin_lo)
-    width = conv_ref.shape[1]
-    packed_ref[:, 0, :width] = conv_ref[...]
-    packed_ref[:, 0, width:] = inverse_rows(
+    packed_ref[:, 0, :] = inverse_rows(
         -1.0, spec_ref, filt_ref, small_ref, twiddle_ref, tables, rows_ref, turned_ref
     )
 
@@ -325,24 +323,21 @@
     total = halving(total, x_index % 2 == 1, "x", near_x)
     total = halving(total, x_index >= 2, "x", far_x)
 
-    conv = pl.pallas_call(
-        conv_kernel,
-        out_shape=jax.ShapeDtypeStruct((seq_count, 2 * positions), f32),
-        scratch_shapes=rows + turned,
-        name="conv",
-        compiler_params=params,
-        cost_estimate=cost,
-    )(moved, filters, small_back, twiddle, *tables)
-    signals = pl.pallas_call(
-        back_kernel,
-        out_shape=jax.ShapeDtypeStruct((seq_count, 1, 4 * positions), f32),
-        scratch_shapes=rows + turned,
-        name="back",
-        compiler_params=params,
-        cost_estimate=cost,
-    )(conv, spec, filters, small_back, twiddle, *tables)
-    returned = lax.all_to_all(signals, SEQ, split_axis=0, concat_axis=0, tiled=True)
-    returned = returned.reshape(seq_count, 4 * positions)
+    signal = jax.ShapeDtypeStruct((seq_count, 1, per_seq * positions), f32)
+
+    def inverse(kernel, first):
+        return pl.pallas_call(
+            kernel,
+            out_shape=signal,
+            scratch_shapes=rows + turned,
+            compiler_params=params,
+            cost_estimate=cost,
+        )(first, filters, small_back, twiddle, *tables)
+
+    signals = inverse(conv_kernel, moved)
+    conv = lax.all_to_all(signals, SEQ, split_axis=0, concat_axis=0, tiled=True)
+    signals = inverse(back_kernel, spec)
+    back = lax.all_to_all(signals, SEQ, split_axis=0, concat_axis=0, tiled=True)
 
     ordered = jnp.where(odd, total[::-1], total)
     rows_out = [jnp.where(upper_zhi, ordered[:, 1 - n], ordered[:, n]) for n in range(2)]
@@ -358,8 +353,8 @@
     )
 
     scale = 1.0 / math.sqrt(seq_count * positions)
-    conv = returned[:, : per_seq * positions].reshape(1, channels, positions) * scale
-    backward = returned[:, per_seq * positions :].reshape(1, channels, positions) * scale
+    conv = conv.reshape(1, channels, positions) * scale
+    backward = back.reshape(1, channels, positions) * scale
     grad_gate = (grad_out.astype(f32) * conv).astype(bf16)
     return (backward.astype(bf16), grad_gate, grad_filter)
 

time: 154 us -> 166 us (1.078)
  the two profiles are of different devices: /device:TPU:7 before, /device:TPU:1 now
where the time goes in v6:
time: 166 us; the launch traced here: 163 us
  starting transfers between devices  100 us (60%)
  waiting for transfers between devices  40.7 us (25%)
  Pallas kernels  9.68 us (6%)
  other arithmetic  6.8 us (4%)
  local copies, waits for them, and re-layouts  4.03 us (2%)
    ppermute x2, starting transfers between devices, step(): lax.ppermute(filter_spectrum, everyone, pairs[number])  24.2 us
    all_to_all x1, waiting for transfers between devices, step(): moved = lax.all_to_all(packed, SEQ, split_axis=0, concat_axis=0, tiled=True)  16.4 us
    ppermute x2, starting transfers between devices, step(): lax.ppermute(rows_out[number], everyone, [(b, a) for a, b in pairs[number]])  15.3 us
    ppermute x3, starting transfers between devices, doubling(): other = lax.ppermute(values, axis, pairs)  14.5 us
    all_to_all x1, starting transfers between devices, step(): moved = lax.all_to_all(packed, SEQ, split_axis=0, concat_axis=0, tiled=True)  11.2 us
    ppermute x2, starting transfers between devices, halving(): return kept + lax.ppermute(away, axis, pairs)  9.22 us
    all_to_all x1, starting transfers between devices, step(): back = lax.all_to_all(signals, SEQ, split_axis=0, concat_axis=0, tiled=True)  7.6 us
    ppermute x1, starting transfers between devices, step(): total = kept + lax.ppermute(away, 'core', cores)  7.32 us
  transfers between devices with their start and end apart: 15, of which 8 were waited for; matrix products, arithmetic and copies ran while one was open for 5% of the time, Pallas kernels for 6%

profile of v6, /device:TPU:1, one launch (start us, length us, event | category | flops | bytes accessed | tf_op | source)
XLA Modules:
  0.0 162.5 jit_solution(10841316069844608697)
XLA Ops:
  0.6 19.5 %collective-permute-start = (f32[2,4,1024]{2,1,0:T(4,128)}, f32[2,4,1024]{2,1,0:T(4,128)S(1)}, u32[]{:S(2)}, u32[]{:S(2)}) collective-permute-start(f32[2,4,1024]{2,1,0:T(4,128)} %param.12), channel_id=1, source_target_pairs={{0,256},{1,0},{2,384},{3,128},{4,320},{5,64},{6,448},{7,192},{8,28... | collective-permute-start | bytes 98312 | tf_op jit(solution)/shard_map/ppermute | solution.py:285
  20.1 4.7 %collective-permute-start.1 = (f32[2,4,1024]{2,1,0:T(4,128)}, f32[2,4,1024]{2,1,0:T(4,128)S(1)}, u32[]{:S(2)}, u32[]{:S(2)}) collective-permute-start(f32[2,4,1024]{2,1,0:T(4,128)} %param.12), channel_id=1, source_target_pairs={{0,0},{1,256},{2,128},{3,384},{4,64},{5,320},{6,192},{7,448},{8,32... | collective-permute-start | bytes 98312 | tf_op jit(solution)/shard_map/ppermute | solution.py:285
  24.8 0.0 collective-permute-done
  24.8 1.7 %collective-permute-done.1 = f32[2,4,1024]{2,1,0:T(4,128)S(1)} collective-permute-done((f32[2,4,1024]{2,1,0:T(4,128)}, f32[2,4,1024]{2,1,0:T(4,128)S(1)}, u32[]{:S(2)}, u32[]{:S(2)}) %collective-permute-start.1) | collective-permute-done | bytes 32800 | tf_op jit(solution)/shard_map/ppermute | solution.py:285
  26.5 0.0 copy-start.1
  26.6 3.1 %collective-permute-start.2 = (f32[2,2,2,1024]{3,2,1,0:T(2,128)S(1)}, f32[2,2,2,1024]{3,2,1,0:T(2,128)S(1)}, u32[]{:S(2)}, u32[]{:S(2)}) collective-permute-start(f32[2,2,2,1024]{3,2,1,0:T(2,128)S(1)} %pad_maximum_fusion.5), channel_id=1, source_target_pairs={{0,1},{1,0},{2,3},{3,2},{4,5},{5,4},{6,7},{7,6},{8,9},{9,8},{10,11... | collective-permute-start | bytes 98312 | tf_op jit(solution)/shard_map/ppermute | solution.py:289
  29.7 0.0 copy-done.2
  29.8 0.0 copy-done.1
  29.8 0.0 copy-start
  29.8 1.0 copy-done
  30.8 1.5 pack.1
  32.3 11.2 %all-to-all-start = ((f32[32,1,6144]{2,1,0:T(1,128)}), f32[32,1,6144]{2,1,0:T(1,128)}, u32[]{:S(2)}, u32[]{:S(2)}) async-start(f32[32,1,6144]{2,1,0:T(1,128)} %pack.1), calls=%async_computation | async-start | bytes 1572864 | tf_op jit(solution)/shard_map/all_to_all | solution.py:277
  43.5 0.0 collective-permute-done.2
  43.7 5.9 %collective-permute-start.3 = (f32[2,2,4096]{2,1,0:T(2,128)S(1)}, f32[2,2,4096]{2,1,0:T(2,128)S(1)}, u32[]{:S(2)}, u32[]{:S(2)}) collective-permute-start(f32[2,2,4096]{2,1,0:T(2,128)S(1)} %pad_maximum_fusion.4), channel_id=1, source_target_pairs={{0,128},{64,192},{128,0},{192,64},{1,129},{65,193},{129,1},{193,65... | collective-permute-start | bytes 196616 | tf_op jit(solution)/shard_map/ppermute | solution.py:250
  49.5 1.6 %collective-permute-done.3 = f32[2,2,4096]{2,1,0:T(2,128)S(1)} collective-permute-done((f32[2,2,4096]{2,1,0:T(2,128)S(1)}, f32[2,2,4096]{2,1,0:T(2,128)S(1)}, u32[]{:S(2)}, u32[]{:S(2)}) %collective-permute-start.3) | collective-permute-done | bytes 65568 | tf_op jit(solution)/shard_map/ppermute | solution.py:250
  51.2 0.1 broadcast_select_fusion.5
  51.2 0.1 pad_maximum_fusion.3
  51.3 4.1 %collective-permute-start.4 = (f32[2,4,4096]{2,1,0:T(4,128)S(1)}, f32[2,4,4096]{2,1,0:T(4,128)S(1)}, u32[]{:S(2)}, u32[]{:S(2)}) collective-permute-start(f32[2,4,4096]{2,1,0:T(4,128)S(1)} %pad_maximum_fusion.3), channel_id=1, source_target_pairs={{0,64},{64,0},{128,192},{192,128},{1,65},{65,1},{129,193},{193,129... | collective-permute-start | bytes 393224 | tf_op jit(solution)/shard_map/ppermute | solution.py:250
  55.4 2.7 %collective-permute-done.4 = f32[2,4,4096]{2,1,0:T(4,128)S(1)} collective-permute-done((f32[2,4,4096]{2,1,0:T(4,128)S(1)}, f32[2,4,4096]{2,1,0:T(4,128)S(1)}, u32[]{:S(2)}, u32[]{:S(2)}) %collective-permute-start.4) | collective-permute-done | bytes 131104 | tf_op jit(solution)/shard_map/ppermute | solution.py:250
  58.1 0.1 broadcast_select_fusion.8
  58.2 0.0 copy-start.3
  58.2 0.0 copy-start.4
  58.3 0.1 pad_maximum_fusion.1
  58.3 4.6 %collective-permute-start.5 = (f32[2,8,4096]{2,1,0:T(8,128)S(1)}, f32[2,8,4096]{2,1,0:T(8,128)}, u32[]{:S(2)}, u32[]{:S(2)}) collective-permute-start(f32[2,8,4096]{2,1,0:T(8,128)S(1)} %pad_maximum_fusion.1), channel_id=1, source_target_pairs={{0,32},{32,0},{1,33},{33,1},{2,34},{34,2},{3,35},{35,3},{4,36},{36... | collective-permute-start | bytes 786440 | tf_op jit(solution)/shard_map/ppermute | solution.py:250
  62.9 0.0 copy-done.3
  62.9 0.0 copy-done.4
  62.9 0.6 root_tables.1
  63.5 0.0 copy-start.5
  63.5 0.0 copy-start.7
  63.6 16.4 %all-to-all-done = f32[32,1,6144]{2,1,0:T(1,128)} async-done(((f32[32,1,6144]{2,1,0:T(1,128)}), f32[32,1,6144]{2,1,0:T(1,128)}, u32[]{:S(2)}, u32[]{:S(2)}) %all-to-all-start) | async-done | bytes 786464 | tf_op jit(solution)/shard_map/all_to_all | solution.py:277
  79.9 1.4 copy.38
  81.3 0.0 copy-done.5
  81.3 2.0 %forward.1 = (f32[32,4096]{1,0:T(8,128)S(1)}, f32[2,8,4096]{2,1,0:T(8,128)S(1)}, f32[2,8,4096]{2,1,0:T(8,128)S(1)}) custom-call(s32[1]{0:T(128)} %bitcast.core_ref, f32[32,6144]{1,0:T(8,128)S(1)} %bitcast.22, bf16[64,96]{1,0:T(8,128)(2,1)S(1)} %copy-done.7, f32[2,32,1024]{2,1,0:T(8,128)S(1)} %copy-done.5, bf16[1024,256]{1,0:T(8,128)(2,1)S(1)} %get-tuple-element.10.cos_hi, ...), custom_call_target="tpu_custom_call" | custom-call | flops 2000000000 | bytes 10000000 | tf_op jit(solution)/shard_map/forward/pallas_call | solution.py:309
  83.4 7.3 %collective-permute-start.6 = (f32[2,8,4096]{2,1,0:T(8,128)S(1)}, f32[2,8,4096]{2,1,0:T(8,128)S(1)}, u32[]{:S(2)}, u32[]{:S(2)}) collective-permute-start(f32[2,8,4096]{2,1,0:T(8,128)S(1)} %get-tuple-element.16), channel_id=1, source_target_pairs={{0,32},{32,0},{1,33},{33,1},{2,34},{34,2},{3,35},{35,3},{4,36},{36... | collective-permute-start | bytes 786440 | tf_op jit(solution)/shard_map/ppermute | solution.py:319
  90.7 0.0 collective-permute-done.5
  90.7 1.0 broadcast_select_fusion.1
  91.7 0.1 collective-permute-done.6
  91.9 0.0 copy-start.8
  91.9 1.9 %collective-permute-start.7 = (f32[8,4096]{1,0:T(8,128)S(1)}, f32[8,4096]{1,0:T(8,128)S(1)}, u32[]{:S(2)}, u32[]{:S(2)}) collective-permute-start(f32[8,4096]{1,0:T(8,128)S(1)} %get-tuple-element.20), channel_id=1, source_target_pairs={{0,1},{1,0},{2,3},{3,2},{4,5},{5,4},{6,7},{7,6},{8,9},{9,8},{10,11... | collective-permute-start | bytes 393224 | tf_op jit(solution)/shard_map/ppermute | solution.py:321
  93.9 4.6 %collective-permute-done.7 = f32[8,4096]{1,0:T(8,128)S(1)} collective-permute-done((f32[8,4096]{1,0:T(8,128)S(1)}, f32[8,4096]{1,0:T(8,128)S(1)}, u32[]{:S(2)}, u32[]{:S(2)}) %collective-permute-start.7) | collective-permute-done | bytes 131104 | tf_op jit(solution)/shard_map/ppermute | solution.py:321
  98.5 0.0 copy-done.8
  98.5 0.7 broadcast_select_fusion.6
  99.2 3.7 %collective-permute-start.8 = (f32[2,4,4096]{2,1,0:T(4,128)}, f32[2,4,4096]{2,1,0:T(4,128)}, u32[]{:S(2)}, u32[]{:S(2)}) collective-permute-start(f32[2,4,4096]{2,1,0:T(4,128)} %broadcast_select_fusion.6), channel_id=1, source_target_pairs={{0,64},{64,0},{128,192},{192,128},{1,65},{65,1},{129,193},{193,129... | collective-permute-start | bytes 393224 | tf_op jit(solution)/shard_map/ppermute | solution.py:246
  102.9 2.8 %shard_map.113 = f32[32,1,2048]{2,1,0:T(1,128)} custom-call(f32[32,6144]{1,0:T(8,128)S(1)} %bitcast.23, f32[32,4096]{1,0:T(8,128)S(1)} %bitcast.24, bf16[32,192]{1,0:T(8,128)(2,1)S(1)} %copy-done.6, f32[2,32,1024]{2,1,0:T(8,128)S(1)} %copy-done.5, bf16[1024,256]{1,0:T(8,128)(2,1)S(1)} %get-tuple-element.10.cos_hi, ...), custom_call_target="tpu_custom_call" | custom-call | flops 2000000000 | bytes 10000000 | tf_op jit(solution)/shard_map/pallas_call | solution.py:329
  105.6 5.8 %all-to-all-start.2 = ((f32[32,1,2048]{2,1,0:T(1,128)}), f32[32,1,2048]{2,1,0:T(1,128)}, u32[]{:S(2)}, u32[]{:S(2)}) async-start(f32[32,1,2048]{2,1,0:T(1,128)} %shard_map.113), calls=%async_computation.2 | async-start | bytes 524288 | tf_op jit(solution)/shard_map/all_to_all | solution.py:338
  111.5 0.0 collective-permute-done.8
  111.5 1.2 select_add_fusion
  112.8 5.6 %collective-permute-start.9 = (f32[2,2,4096]{2,1,0:T(2,128)S(1)}, f32[2,2,4096]{2,1,0:T(2,128)S(1)}, u32[]{:S(2)}, u32[]{:S(2)}) collective-permute-start(f32[2,2,4096]{2,1,0:T(2,128)S(1)} %broadcast_select_fusion.3), channel_id=1, source_target_pairs={{0,128},{64,192},{128,0},{192,64},{1,129},{65,193},{129,1},{193,65... | collective-permute-start | bytes 196616 | tf_op jit(solution)/shard_map/ppermute | solution.py:246
  118.3 2.8 %shard_map.112 = f32[32,1,2048]{2,1,0:T(1,128)} custom-call(f32[32,4096]{1,0:T(8,128)S(1)} %get-tuple-element.14.spec_ref, f32[32,4096]{1,0:T(8,128)S(1)} %bitcast.25, bf16[32,192]{1,0:T(8,128)(2,1)S(1)} %copy-done.6, f32[2,32,1024]{2,1,0:T(8,128)S(1)} %copy-done.5, bf16[1024,256]{1,0:T(8,128)(2,1)S(1)} %get-tuple-element.10.cos_hi, ...), custom_call_target="tpu_custom_call" | custom-call | flops 2000000000 | bytes 10000000 | tf_op jit(solution)/shard_map/pallas_call | solution.py:329
  121.1 0.0 collective-permute-done.9
  121.1 0.1 select_add_fusion.1
  121.2 0.1 broadcast_select_fusion.2
  121.3 6.9 %all-to-all-done.2 = f32[32,1,2048]{2,1,0:T(1,128)} async-done(((f32[32,1,2048]{2,1,0:T(1,128)}), f32[32,1,2048]{2,1,0:T(1,128)}, u32[]{:S(2)}, u32[]{:S(2)}) %all-to-all-start.2) | async-done | bytes 262176 | tf_op jit(solution)/shard_map/all_to_all | solution.py:338
  128.2 7.6 %all-to-all-start.1 = ((f32[32,1,2048]{2,1,0:T(1,128)}), f32[32,1,2048]{2,1,0:T(1,128)S(1)}, u32[]{:S(2)}, u32[]{:S(2)}) async-start(f32[32,1,2048]{2,1,0:T(1,128)} %shard_map.112), calls=%async_computation.1 | async-start | bytes 524288 | tf_op jit(solution)/shard_map/all_to_all | solution.py:340
  135.9 5.6 %collective-permute-start.10 = (f32[2,4096]{1,0:T(2,128)S(1)}, f32[2,4096]{1,0:T(2,128)S(1)}, u32[]{:S(2)}, u32[]{:S(2)}) collective-permute-start(f32[2,4096]{1,0:T(2,128)S(1)} %fusion.1), channel_id=1, source_target_pairs={{0,0},{256,1},{128,2},{384,3},{64,4},{320,5},{192,6},{448,7},{32,8... | collective-permute-start | bytes 98312 | tf_op jit(solution)/shard_map/ppermute | solution.py:345
  141.5 9.8 %collective-permute-start.11 = (f32[2,4096]{1,0:T(2,128)S(1)}, f32[2,4096]{1,0:T(2,128)S(1)}, u32[]{:S(2)}, u32[]{:S(2)}) collective-permute-start(f32[2,4096]{1,0:T(2,128)S(1)} %bitcast.31), channel_id=1, source_target_pairs={{256,0},{0,1},{384,2},{128,3},{320,4},{64,5},{448,6},{192,7},{288,... | collective-permute-start | bytes 98312 | tf_op jit(solution)/shard_map/ppermute | solution.py:345
  151.2 0.0 collective-permute-done.10
  151.2 6.6 %collective-permute-done.11 = f32[2,4096]{1,0:T(2,128)S(1)} collective-permute-done((f32[2,4096]{1,0:T(2,128)S(1)}, f32[2,4096]{1,0:T(2,128)S(1)}, u32[]{:S(2)}, u32[]{:S(2)}) %collective-permute-start.11) | collective-permute-done | bytes 32800 | tf_op jit(solution)/shard_map/ppermute | solution.py:345
  158.0 0.6 reshape.154
  158.6 1.7 %multiply_reduce_fusion = f32[32,2048]{1,0:T(8,128)S(1)} fusion(f32[32,1,2048]{2,1,0:T(1,128)} %all-to-all-done.2), kind=kLoop, calls=%fused_computation.6 | loop fusion | flops 65536 | bytes 524288 | tf_op jit(solution)/shard_map/mul | solution.py:356
  160.4 0.7 multiply_convert_fusion
  161.0 0.0 all-to-all-done.1
  161.0 0.8 convert_reduce_fusion
  161.8 0.7 convert_element_type.22
  (25 shorter events, 0.6 us)
Async XLA Ops:
  0.6 24.2 %collective-permute-start = (f32[2,4,1024]{2,1,0:T(4,128)}, f32[2,4,1024]{2,1,0:T(4,128)S(1)}, u32[]{:S(2)}, u32[]{:S(2)}) collective-permute-start(f32[2,4,1024]{2,1,0:T(4,128)} %param.12), channel_id=1, source_target_pairs={{0,256},{1,0},{2,384},{3,128},{4,320},{5,64},{6,448},{7,192},{8,28... | collective-permute-start | bytes 98312 | tf_op jit(solution)/shard_map/ppermute | solution.py:285
  20.1 6.4 %collective-permute-start.1 = (f32[2,4,1024]{2,1,0:T(4,128)}, f32[2,4,1024]{2,1,0:T(4,128)S(1)}, u32[]{:S(2)}, u32[]{:S(2)}) collective-permute-start(f32[2,4,1024]{2,1,0:T(4,128)} %param.12), channel_id=1, source_target_pairs={{0,0},{1,256},{2,128},{3,384},{4,64},{5,320},{6,192},{7,448},{8,32... | collective-permute-start | bytes 98312 | tf_op jit(solution)/shard_map/ppermute | solution.py:285
  26.5 3.2 %copy-start.2 = (bf16[1,64,1024]{2,1,0:T(8,128)(2,1)S(1)}, bf16[1,64,1024]{2,1,0:T(8,128)(2,1)}, u32[]{:S(2)}) copy-start(bf16[1,64,1024]{2,1,0:T(8,128)(2,1)} %gate_ref.1) | copy-start | bytes 393220
  26.5 3.2 %copy-start.1 = (bf16[1,64,1024]{2,1,0:T(8,128)(2,1)S(1)}, bf16[1,64,1024]{2,1,0:T(8,128)(2,1)}, u32[]{:S(2)}) copy-start(bf16[1,64,1024]{2,1,0:T(8,128)(2,1)} %out_ref.1) | copy-start | bytes 393220
  26.6 16.9 %collective-permute-start.2 = (f32[2,2,2,1024]{3,2,1,0:T(2,128)S(1)}, f32[2,2,2,1024]{3,2,1,0:T(2,128)S(1)}, u32[]{:S(2)}, u32[]{:S(2)}) collective-permute-start(f32[2,2,2,1024]{3,2,1,0:T(2,128)S(1)} %pad_maximum_fusion.5), channel_id=1, source_target_pairs={{0,1},{1,0},{2,3},{3,2},{4,5},{5,4},{6,7},{7,6},{8,9},{9,8},{10,11... | collective-permute-start | bytes 98312 | tf_op jit(solution)/shard_map/ppermute | solution.py:289
  29.8 1.0 copy-start
  32.3 47.7 %all-to-all-start = ((f32[32,1,6144]{2,1,0:T(1,128)}), f32[32,1,6144]{2,1,0:T(1,128)}, u32[]{:S(2)}, u32[]{:S(2)}) async-start(f32[32,1,6144]{2,1,0:T(1,128)} %pack.1), calls=%async_computation | async-start | bytes 1572864 | tf_op jit(solution)/shard_map/all_to_all | solution.py:277
  43.7 7.5 %collective-permute-start.3 = (f32[2,2,4096]{2,1,0:T(2,128)S(1)}, f32[2,2,4096]{2,1,0:T(2,128)S(1)}, u32[]{:S(2)}, u32[]{:S(2)}) collective-permute-start(f32[2,2,4096]{2,1,0:T(2,128)S(1)} %pad_maximum_fusion.4), channel_id=1, source_target_pairs={{0,128},{64,192},{128,0},{192,64},{1,129},{65,193},{129,1},{193,65... | collective-permute-start | bytes 196616 | tf_op jit(solution)/shard_map/ppermute | solution.py:250
  51.3 6.8 %collective-permute-start.4 = (f32[2,4,4096]{2,1,0:T(4,128)S(1)}, f32[2,4,4096]{2,1,0:T(4,128)S(1)}, u32[]{:S(2)}, u32[]{:S(2)}) collective-permute-start(f32[2,4,4096]{2,1,0:T(4,128)S(1)} %pad_maximum_fusion.3), channel_id=1, source_target_pairs={{0,64},{64,0},{128,192},{192,128},{1,65},{65,1},{129,193},{193,129... | collective-permute-start | bytes 393224 | tf_op jit(solution)/shard_map/ppermute | solution.py:250
  58.2 4.7 %copy-start.3 = (f32[2,32,256]{2,1,0:T(8,128)S(1)}, f32[2,32,256]{2,1,0:T(8,128)}, u32[]{:S(2)}) copy-start(f32[2,32,256]{2,1,0:T(8,128)} %constant.57.clone.coarse_ref) | copy-start | bytes 196612
  58.2 4.7 %copy-start.4 = (f32[2,32,256]{2,1,0:T(8,128)S(1)}, f32[2,32,256]{2,1,0:T(8,128)}, u32[]{:S(2)}) copy-start(f32[2,32,256]{2,1,0:T(8,128)} %constant.58.clone.fine_ref) | copy-start | bytes 196612
  58.3 32.4 %collective-permute-start.5 = (f32[2,8,4096]{2,1,0:T(8,128)S(1)}, f32[2,8,4096]{2,1,0:T(8,128)}, u32[]{:S(2)}, u32[]{:S(2)}) collective-permute-start(f32[2,8,4096]{2,1,0:T(8,128)S(1)} %pad_maximum_fusion.1), channel_id=1, source_target_pairs={{0,32},{32,0},{1,33},{33,1},{2,34},{34,2},{3,35},{35,3},{4,36},{36... | collective-permute-start | bytes 786440 | tf_op jit(solution)/shard_map/ppermute | solution.py:250
  63.5 17.8 %copy-start.5 = (f32[2,32,1024]{2,1,0:T(8,128)S(1)}, f32[2,32,1024]{2,1,0:T(8,128)}, u32[]{:S(2)}) copy-start(f32[2,32,1024]{2,1,0:T(8,128)} %constant.61.clone.twiddle_ref) | copy-start | bytes 786436
  63.5 17.8 %copy-start.7 = (bf16[64,96]{1,0:T(8,128)(2,1)S(1)}, bf16[64,96]{1,0:T(8,128)(2,1)}, u32[]{:S(2)}) copy-start(bf16[64,96]{1,0:T(8,128)(2,1)} %constant.59.clone.small_ref) | copy-start | bytes 36868
  83.4 8.5 %collective-permute-start.6 = (f32[2,8,4096]{2,1,0:T(8,128)S(1)}, f32[2,8,4096]{2,1,0:T(8,128)S(1)}, u32[]{:S(2)}, u32[]{:S(2)}) collective-permute-start(f32[2,8,4096]{2,1,0:T(8,128)S(1)} %get-tuple-element.16), channel_id=1, source_target_pairs={{0,32},{32,0},{1,33},{33,1},{2,34},{34,2},{3,35},{35,3},{4,36},{36... | collective-permute-start | bytes 786440 | tf_op jit(solution)/shard_map/ppermute | solution.py:319
  91.9 6.6 %copy-start.8 = (f32[1,8,4096]{2,1,0:T(8,128)}, f32[1,8,4096]{2,1,0:T(8,128)S(1)}, u32[]{:S(2)}) copy-start(f32[1,8,4096]{2,1,0:T(8,128)S(1)} %get-tuple-element.19) | copy-start | bytes 393220
  91.9 6.6 %collective-permute-start.7 = (f32[8,4096]{1,0:T(8,128)S(1)}, f32[8,4096]{1,0:T(8,128)S(1)}, u32[]{:S(2)}, u32[]{:S(2)}) collective-permute-start(f32[8,4096]{1,0:T(8,128)S(1)} %get-tuple-element.20), channel_id=1, source_target_pairs={{0,1},{1,0},{2,3},{3,2},{4,5},{5,4},{6,7},{7,6},{8,9},{9,8},{10,11... | collective-permute-start | bytes 393224 | tf_op jit(solution)/shard_map/ppermute | solution.py:321
  98.5 0.7 copy-start.9
  98.5 4.4 %copy-start.6 = (bf16[32,192]{1,0:T(8,128)(2,1)S(1)}, bf16[32,192]{1,0:T(8,128)(2,1)}, u32[]{:S(2)}) copy-start(bf16[32,192]{1,0:T(8,128)(2,1)} %constant.60.clone.small_ref) | copy-start | bytes 36868
  99.2 12.3 %collective-permute-start.8 = (f32[2,4,4096]{2,1,0:T(4,128)}, f32[2,4,4096]{2,1,0:T(4,128)}, u32[]{:S(2)}, u32[]{:S(2)}) collective-permute-start(f32[2,4,4096]{2,1,0:T(4,128)} %broadcast_select_fusion.6), channel_id=1, source_target_pairs={{0,64},{64,0},{128,192},{192,128},{1,65},{65,1},{129,193},{193,129... | collective-permute-start | bytes 393224 | tf_op jit(solution)/shard_map/ppermute | solution.py:246
  105.6 22.5 %all-to-all-start.2 = ((f32[32,1,2048]{2,1,0:T(1,128)}), f32[32,1,2048]{2,1,0:T(1,128)}, u32[]{:S(2)}, u32[]{:S(2)}) async-start(f32[32,1,2048]{2,1,0:T(1,128)} %shard_map.113), calls=%async_computation.2 | async-start | bytes 524288 | tf_op jit(solution)/shard_map/all_to_all | solution.py:338
  112.8 8.3 %collective-permute-start.9 = (f32[2,2,4096]{2,1,0:T(2,128)S(1)}, f32[2,2,4096]{2,1,0:T(2,128)S(1)}, u32[]{:S(2)}, u32[]{:S(2)}) collective-permute-start(f32[2,2,4096]{2,1,0:T(2,128)S(1)} %broadcast_select_fusion.3), channel_id=1, source_target_pairs={{0,128},{64,192},{128,0},{192,64},{1,129},{65,193},{129,1},{193,65... | collective-permute-start | bytes 196616 | tf_op jit(solution)/shard_map/ppermute | solution.py:246
  128.2 32.9 %all-to-all-start.1 = ((f32[32,1,2048]{2,1,0:T(1,128)}), f32[32,1,2048]{2,1,0:T(1,128)S(1)}, u32[]{:S(2)}, u32[]{:S(2)}) async-start(f32[32,1,2048]{2,1,0:T(1,128)} %shard_map.112), calls=%async_computation.1 | async-start | bytes 524288 | tf_op jit(solution)/shard_map/all_to_all | solution.py:340
  135.9 15.4 %collective-permute-start.10 = (f32[2,4096]{1,0:T(2,128)S(1)}, f32[2,4096]{1,0:T(2,128)S(1)}, u32[]{:S(2)}, u32[]{:S(2)}) collective-permute-start(f32[2,4096]{1,0:T(2,128)S(1)} %fusion.1), channel_id=1, source_target_pairs={{0,0},{256,1},{128,2},{384,3},{64,4},{320,5},{192,6},{448,7},{32,8... | collective-permute-start | bytes 98312 | tf_op jit(solution)/shard_map/ppermute | solution.py:345
  141.5 16.4 %collective-permute-start.11 = (f32[2,4096]{1,0:T(2,128)S(1)}, f32[2,4096]{1,0:T(2,128)S(1)}, u32[]{:S(2)}, u32[]{:S(2)}) collective-permute-start(f32[2,4096]{1,0:T(2,128)S(1)} %bitcast.31), channel_id=1, source_target_pairs={{256,0},{0,1},{384,2},{128,3},{320,4},{64,5},{448,6},{192,7},{288,... | collective-permute-start | bytes 98312 | tf_op jit(solution)/shard_map/ppermute | solution.py:345

commit v7 on v4

--- a/solution.py
+++ b/solution.py
@@ -103,17 +103,30 @@
     return both[:rows] + both[rows:] + dot16(high_low[:rows], lo_ref[...])
 
 
-def pack_kernel(out_ref, gate_ref, spec_ref, packed_ref, rows_ref):
-    points = out_ref.shape[2]
+def pack_kernel(
+    out_hbm, gate_hbm, spec_hbm, packed_ref, out_ref, gate_ref, spec_ref, rows_ref, semaphores
+):
+    copies = [
+        pltpu.make_async_copy(spec_hbm.at[0, 0], spec_ref.at[0], semaphores.at[0]),
+        pltpu.make_async_copy(spec_hbm.at[0, 1], spec_ref.at[1], semaphores.at[1]),
+        pltpu.make_async_copy(out_hbm.at[0], out_ref, semaphores.at[2]),
+        pltpu.make_async_copy(gate_hbm.at[0], gate_ref, semaphores.at[3]),
+    ]
+    for copy in copies:
+        copy.start()
+    points = out_ref.shape[1]
     count = packed_ref.shape[0]
     for source in range(3):
+        copies[source].wait()
+        if source == 2:
+            copies[3].wait()
         for start in range(0, points, 128):
             cut = slice(start, start + 128)
             slot = source * (points // 128) + start // 128
             if source == 2:
-                rows_ref[slot] = out_ref[0, :, cut].astype(f32) * gate_ref[0, :, cut].astype(f32)
+                rows_ref[slot] = out_ref[:, cut].astype(f32) * gate_ref[:, cut].astype(f32)
             else:
-                rows_ref[slot] = spec_ref[0, source, :, cut]
+                rows_ref[slot] = spec_ref[source, :, cut]
             for channel in range(2):
                 at = (2 * source + channel) * points + start
                 packed_ref[:, 0, at : at + 128] = rows_ref[slot, pl.ds(channel, count, stride=2), :]
@@ -271,9 +284,16 @@
     packed = pl.pallas_call(
         pack_kernel,
         out_shape=jax.ShapeDtypeStruct((seq_count, 1, 3 * per_seq * positions), f32),
-        scratch_shapes=[pltpu.VMEM((3 * positions // 128, channels, 128), f32)],
+        in_specs=[pl.BlockSpec(memory_space=pltpu.HBM)] * 3,
+        scratch_shapes=[
+            pltpu.VMEM((channels, positions), bf16),
+            pltpu.VMEM((channels, positions), bf16),
+            pltpu.VMEM((2, channels, positions), f32),
+            pltpu.VMEM((3 * positions // 128, channels, 128), f32),
+            pltpu.SemaphoreType.DMA((4,)),
+        ],
         name="pack",
-        compiler_params=params,
+        compiler_params=pltpu.CompilerParams(vmem_limit_bytes=63 * MIB),
         cost_estimate=pl.CostEstimate(flops=10**5, bytes_accessed=2 * 10**6, transcendentals=0),
     )(grad_out, gate, input_spectrum)
     moved = lax.all_to_all(packed, SEQ, split_axis=0, concat_axis=0, tiled=True)

time: 154 us -> 155 us (level)
  no operation moved by 1% of the time
where the time goes in v7:
time: 155 us; the launch traced here: 154 us
  starting transfers between devices  69 us (45%)
  waiting for transfers between devices  67.6 us (44%)
  Pallas kernels  10 us (6%)
  other arithmetic  3.3 us (2%)
  local copies, waits for them, and re-layouts  2.99 us (2%)
    ppermute x2, starting transfers between devices, step(): lax.ppermute(filter_spectrum, everyone, pairs[number])  22.4 us
    all_to_all x1, waiting for transfers between devices, step(): moved = lax.all_to_all(packed, SEQ, split_axis=0, concat_axis=0, tiled=True)  21.9 us
    ppermute x2, waiting for transfers between devices, step(): lax.ppermute(rows_out[number], everyone, [(b, a) for a, b in pairs[number]])  21.9 us
    ppermute x2, starting transfers between devices, step(): lax.ppermute(rows_out[number], everyone, [(b, a) for a, b in pairs[number]])  14.2 us
    all_to_all x1, starting transfers between devices, step(): moved = lax.all_to_all(packed, SEQ, split_axis=0, concat_axis=0, tiled=True)  10.8 us
    ppermute x3, waiting for transfers between devices, doubling(): other = lax.ppermute(values, axis, pairs)  10.2 us
    ppermute x2, waiting for transfers between devices, step(): lax.ppermute(filter_spectrum, everyone, pairs[number])  6.61 us
    ppermute x3, starting transfers between devices, doubling(): other = lax.ppermute(values, axis, pairs)  6.35 us
  transfers between devices with their start and end apart: 14, of which 9 were waited for; matrix products, arithmetic and copies ran while one was open for 2% of the time, Pallas kernels for 6%

profile of v7, /device:TPU:7, one launch (start us, length us, event | category | flops | bytes accessed | tf_op | source)
XLA Modules:
  0.0 154.1 jit_solution(8107651856705983486)
XLA Ops:
  0.6 17.2 %collective-permute-start = (f32[2,4,1024]{2,1,0:T(4,128)}, f32[2,4,1024]{2,1,0:T(4,128)S(1)}, u32[]{:S(2)}, u32[]{:S(2)}) collective-permute-start(f32[2,4,1024]{2,1,0:T(4,128)} %param.12), channel_id=1, source_target_pairs={{0,256},{1,0},{2,384},{3,128},{4,320},{5,64},{6,448},{7,192},{8,28... | collective-permute-start | bytes 98312 | tf_op jit(solution)/shard_map/ppermute | solution.py:307
  17.9 5.2 %collective-permute-start.1 = (f32[2,4,1024]{2,1,0:T(4,128)}, f32[2,4,1024]{2,1,0:T(4,128)S(1)}, u32[]{:S(2)}, u32[]{:S(2)}) collective-permute-start(f32[2,4,1024]{2,1,0:T(4,128)} %param.12), channel_id=1, source_target_pairs={{0,0},{1,256},{2,128},{3,384},{4,64},{5,320},{6,192},{7,448},{8,32... | collective-permute-start | bytes 98312 | tf_op jit(solution)/shard_map/ppermute | solution.py:307
  23.1 0.0 collective-permute-done
  23.1 6.6 %collective-permute-done.1 = f32[2,4,1024]{2,1,0:T(4,128)S(1)} collective-permute-done((f32[2,4,1024]{2,1,0:T(4,128)}, f32[2,4,1024]{2,1,0:T(4,128)S(1)}, u32[]{:S(2)}, u32[]{:S(2)}) %collective-permute-start.1) | collective-permute-done | bytes 32800 | tf_op jit(solution)/shard_map/ppermute | solution.py:307
  29.8 1.9 %collective-permute-start.2 = (f32[2,2,2,1024]{3,2,1,0:T(2,128)S(1)}, f32[2,2,2,1024]{3,2,1,0:T(2,128)S(1)}, u32[]{:S(2)}, u32[]{:S(2)}) collective-permute-start(f32[2,2,2,1024]{3,2,1,0:T(2,128)S(1)} %pad_maximum_fusion.5), channel_id=1, source_target_pairs={{0,1},{1,0},{2,3},{3,2},{4,5},{5,4},{6,7},{7,6},{8,9},{9,8},{10,11... | collective-permute-start | bytes 98312 | tf_op jit(solution)/shard_map/ppermute | solution.py:311
  31.7 2.4 %pack.1 = f32[32,1,6144]{2,1,0:T(1,128)} custom-call(bf16[1,64,1024]{2,1,0:T(8,128)(2,1)} %out_hbm.1, bf16[1,64,1024]{2,1,0:T(8,128)(2,1)} %gate_hbm.1, f32[1,2,64,1024]{3,2,1,0:T(8,128)} %spec_hbm.1), custom_call_target="tpu_custom_call" | custom-call | flops 100000 | bytes 2000000 | tf_op jit(solution)/shard_map/pack/pallas_call | solution.py:284
  34.1 10.8 %all-to-all-start = ((f32[32,1,6144]{2,1,0:T(1,128)}), f32[32,1,6144]{2,1,0:T(1,128)S(1)}, u32[]{:S(2)}, u32[]{:S(2)}) async-start(f32[32,1,6144]{2,1,0:T(1,128)} %pack.1), calls=%async_computation | async-start | bytes 1572864 | tf_op jit(solution)/shard_map/all_to_all | solution.py:299
  45.0 0.0 collective-permute-done.2
  45.1 1.9 %collective-permute-start.3 = (f32[2,2,4096]{2,1,0:T(2,128)S(1)}, f32[2,2,4096]{2,1,0:T(2,128)S(1)}, u32[]{:S(2)}, u32[]{:S(2)}) collective-permute-start(f32[2,2,4096]{2,1,0:T(2,128)S(1)} %pad_maximum_fusion.4), channel_id=1, source_target_pairs={{0,128},{64,192},{128,0},{192,64},{1,129},{65,193},{129,1},{193,65... | collective-permute-start | bytes 196616 | tf_op jit(solution)/shard_map/ppermute | solution.py:265
  47.1 4.9 %collective-permute-done.3 = f32[2,2,4096]{2,1,0:T(2,128)S(1)} collective-permute-done((f32[2,2,4096]{2,1,0:T(2,128)S(1)}, f32[2,2,4096]{2,1,0:T(2,128)S(1)}, u32[]{:S(2)}, u32[]{:S(2)}) %collective-permute-start.3) | collective-permute-done | bytes 65568 | tf_op jit(solution)/shard_map/ppermute | solution.py:265
  52.0 0.1 broadcast_select_fusion.5
  52.1 0.1 pad_maximum_fusion.3
  52.1 1.9 %collective-permute-start.4 = (f32[2,4,4096]{2,1,0:T(4,128)S(1)}, f32[2,4,4096]{2,1,0:T(4,128)S(1)}, u32[]{:S(2)}, u32[]{:S(2)}) collective-permute-start(f32[2,4,4096]{2,1,0:T(4,128)S(1)} %pad_maximum_fusion.3), channel_id=1, source_target_pairs={{0,64},{64,0},{128,192},{192,128},{1,65},{65,1},{129,193},{193,129... | collective-permute-start | bytes 393224 | tf_op jit(solution)/shard_map/ppermute | solution.py:265
  54.1 5.3 %collective-permute-done.4 = f32[2,4,4096]{2,1,0:T(4,128)S(1)} collective-permute-done((f32[2,4,4096]{2,1,0:T(4,128)S(1)}, f32[2,4,4096]{2,1,0:T(4,128)S(1)}, u32[]{:S(2)}, u32[]{:S(2)}) %collective-permute-start.4) | collective-permute-done | bytes 131104 | tf_op jit(solution)/shard_map/ppermute | solution.py:265
  59.3 0.1 broadcast_select_fusion.8
  59.4 0.0 copy-start
  59.4 0.0 copy-start.1
  59.4 0.8 pad_maximum_fusion.1
  60.2 2.5 %collective-permute-start.5 = (f32[2,8,4096]{2,1,0:T(8,128)}, f32[2,8,4096]{2,1,0:T(8,128)}, u32[]{:S(2)}, u32[]{:S(2)}) collective-permute-start(f32[2,8,4096]{2,1,0:T(8,128)} %pad_maximum_fusion.1), channel_id=1, source_target_pairs={{0,32},{32,0},{1,33},{33,1},{2,34},{34,2},{3,35},{35,3},{4,36},{36... | collective-permute-start | bytes 786440 | tf_op jit(solution)/shard_map/ppermute | solution.py:265
  62.7 0.0 copy-done
  62.8 0.0 copy-done.1
  62.8 0.6 root_tables.1
  63.4 0.0 copy-start.2
  63.4 0.0 copy-start.4
  63.4 21.9 %all-to-all-done = f32[32,1,6144]{2,1,0:T(1,128)S(1)} async-done(((f32[32,1,6144]{2,1,0:T(1,128)}), f32[32,1,6144]{2,1,0:T(1,128)S(1)}, u32[]{:S(2)}, u32[]{:S(2)}) %all-to-all-start) | async-done | bytes 786464 | tf_op jit(solution)/shard_map/all_to_all | solution.py:299
  85.3 0.2 copy.34
  85.6 0.0 copy-done.2
  85.6 0.0 copy-done.4
  85.6 2.0 %forward.1 = (f32[32,4096]{1,0:T(8,128)S(1)}, f32[2,8,4096]{2,1,0:T(8,128)S(1)}, f32[2,8,4096]{2,1,0:T(8,128)S(1)}) custom-call(s32[1]{0:T(128)} %bitcast.3.core_ref, f32[32,6144]{1,0:T(8,128)S(1)} %bitcast.25, bf16[64,96]{1,0:T(8,128)(2,1)S(1)} %copy-done.4, f32[2,32,1024]{2,1,0:T(8,128)S(1)} %copy-done.2, bf16[1024,256]{1,0:T(8,128)(2,1)S(1)} %get-tuple-element.10.cos_hi, ...), custom_call_target="tpu_custom_call" | custom-call | flops 2000000000 | bytes 10000000 | tf_op jit(solution)/shard_map/forward/pallas_call | solution.py:331
  87.6 1.9 %collective-permute-start.6 = (f32[2,8,4096]{2,1,0:T(8,128)S(1)}, f32[2,8,4096]{2,1,0:T(8,128)S(1)}, u32[]{:S(2)}, u32[]{:S(2)}) collective-permute-start(f32[2,8,4096]{2,1,0:T(8,128)S(1)} %get-tuple-element.16), channel_id=1, source_target_pairs={{0,32},{32,0},{1,33},{33,1},{2,34},{34,2},{3,35},{35,3},{4,36},{36... | collective-permute-start | bytes 786440 | tf_op jit(solution)/shard_map/ppermute | solution.py:341
  89.6 0.0 collective-permute-done.5
  89.6 1.0 broadcast_select_fusion.1
  90.6 0.5 collective-permute-done.6
  91.1 1.9 %collective-permute-start.7 = (f32[8,4096]{1,0:T(8,128)S(1)}, f32[8,4096]{1,0:T(8,128)S(1)}, u32[]{:S(2)}, u32[]{:S(2)}) collective-permute-start(f32[8,4096]{1,0:T(8,128)S(1)} %get-tuple-element.22), channel_id=1, source_target_pairs={{0,1},{1,0},{2,3},{3,2},{4,5},{5,4},{6,7},{7,6},{8,9},{9,8},{10,11... | collective-permute-start | bytes 393224 | tf_op jit(solution)/shard_map/ppermute | solution.py:343
  93.1 0.1 pad_maximum_fusion
  93.1 4.8 %collective-permute-done.7 = f32[8,4096]{1,0:T(8,128)S(1)} collective-permute-done((f32[8,4096]{1,0:T(8,128)S(1)}, f32[8,4096]{1,0:T(8,128)S(1)}, u32[]{:S(2)}, u32[]{:S(2)}) %collective-permute-start.7) | collective-permute-done | bytes 131104 | tf_op jit(solution)/shard_map/ppermute | solution.py:343
  97.9 0.0 copy-start.3
  98.0 1.9 %collective-permute-start.8 = (f32[2,4,4096]{2,1,0:T(4,128)S(1)}, f32[2,4,4096]{2,1,0:T(4,128)S(1)}, u32[]{:S(2)}, u32[]{:S(2)}) collective-permute-start(f32[2,4,4096]{2,1,0:T(4,128)S(1)} %broadcast_select_fusion.6), channel_id=1, source_target_pairs={{0,64},{64,0},{128,192},{192,128},{1,65},{65,1},{129,193},{193,129... | collective-permute-start | bytes 393224 | tf_op jit(solution)/shard_map/ppermute | solution.py:261
  99.9 0.0 copy-done.3
  99.9 2.0 %conv.1.conv_ref = f32[32,2048]{1,0:T(8,128)S(1)} custom-call(f32[32,6144]{1,0:T(8,128)S(1)} %bitcast.26, f32[32,4096]{1,0:T(8,128)S(1)} %bitcast.27, bf16[32,192]{1,0:T(8,128)(2,1)S(1)} %copy-done.3, f32[2,32,1024]{2,1,0:T(8,128)S(1)} %copy-done.2, bf16[1024,256]{1,0:T(8,128)(2,1)S(1)} %get-tuple-element.10.cos_hi, ...), custom_call_target="tpu_custom_call" | custom-call | flops 2000000000 | bytes 10000000 | tf_op jit(solution)/shard_map/conv/pallas_call | solution.py:348
  102.0 1.7 %collective-permute-done.8 = f32[2,4,4096]{2,1,0:T(4,128)S(1)} collective-permute-done((f32[2,4,4096]{2,1,0:T(4,128)S(1)}, f32[2,4,4096]{2,1,0:T(4,128)S(1)}, u32[]{:S(2)}, u32[]{:S(2)}) %collective-permute-start.8) | collective-permute-done | bytes 131104 | tf_op jit(solution)/shard_map/ppermute | solution.py:261
  103.8 1.9 %collective-permute-start.9 = (f32[2,2,4096]{2,1,0:T(2,128)S(1)}, f32[2,2,4096]{2,1,0:T(2,128)S(1)}, u32[]{:S(2)}, u32[]{:S(2)}) collective-permute-start(f32[2,2,4096]{2,1,0:T(2,128)S(1)} %broadcast_select_fusion.3), channel_id=1, source_target_pairs={{0,128},{64,192},{128,0},{192,64},{1,129},{65,193},{129,1},{193,65... | collective-permute-start | bytes 196616 | tf_op jit(solution)/shard_map/ppermute | solution.py:261
  105.7 2.9 %back.1 = f32[32,1,4096]{2,1,0:T(1,128)} custom-call(f32[32,2048]{1,0:T(8,128)S(1)} %conv.1.conv_ref, f32[32,4096]{1,0:T(8,128)S(1)} %get-tuple-element.14.spec_ref, f32[32,4096]{1,0:T(8,128)S(1)} %bitcast.28, bf16[32,192]{1,0:T(8,128)(2,1)S(1)} %copy-done.3, f32[2,32,1024]{2,1,0:T(8,128)S(1)} %copy-done.2, bf16[1024,256]{1,0:T(8,128)(2,1)S(1)} %get-tuple-element.10.cos_hi, ...), custom_call_target="tpu_custom_call" | custom-call | flops 2000000000 | bytes 10000000 | tf_op jit(solution)/shard_map/back/pallas_call | solution.py:356
  108.6 5.7 %all-to-all-start.1 = ((f32[32,1,4096]{2,1,0:T(1,128)}), f32[32,1,4096]{2,1,0:T(1,128)S(1)}, u32[]{:S(2)}, u32[]{:S(2)}) async-start(f32[32,1,4096]{2,1,0:T(1,128)} %back.1), calls=%async_computation.1 | async-start | bytes 1048576 | tf_op jit(solution)/shard_map/all_to_all | solution.py:364
  114.3 0.0 collective-permute-done.9
  114.3 0.1 select_add_fusion.1
  114.4 0.1 broadcast_select_fusion.2
  114.5 12.3 %collective-permute-start.10 = (f32[2,4096]{1,0:T(2,128)S(1)}, f32[2,4096]{1,0:T(2,128)S(1)}, u32[]{:S(2)}, u32[]{:S(2)}) collective-permute-start(f32[2,4096]{1,0:T(2,128)S(1)} %fusion.2), channel_id=1, source_target_pairs={{0,0},{256,1},{128,2},{384,3},{64,4},{320,5},{192,6},{448,7},{32,8... | collective-permute-start | bytes 98312 | tf_op jit(solution)/shard_map/ppermute | solution.py:370
  126.9 1.9 %collective-permute-start.11 = (f32[2,4096]{1,0:T(2,128)S(1)}, f32[2,4096]{1,0:T(2,128)S(1)}, u32[]{:S(2)}, u32[]{:S(2)}) collective-permute-start(f32[2,4096]{1,0:T(2,128)S(1)} %bitcast.35), channel_id=1, source_target_pairs={{256,0},{0,1},{384,2},{128,3},{320,4},{64,5},{448,6},{192,7},{288,... | collective-permute-start | bytes 98312 | tf_op jit(solution)/shard_map/ppermute | solution.py:370
  128.8 10.1 %collective-permute-done.10 = f32[2,4096]{1,0:T(2,128)S(1)} collective-permute-done((f32[2,4096]{1,0:T(2,128)S(1)}, f32[2,4096]{1,0:T(2,128)S(1)}, u32[]{:S(2)}, u32[]{:S(2)}) %collective-permute-start.10) | collective-permute-done | bytes 32800 | tf_op jit(solution)/shard_map/ppermute | solution.py:370
  138.9 11.8 %collective-permute-done.11 = f32[2,4096]{1,0:T(2,128)S(1)} collective-permute-done((f32[2,4096]{1,0:T(2,128)S(1)}, f32[2,4096]{1,0:T(2,128)S(1)}, u32[]{:S(2)}, u32[]{:S(2)}) %collective-permute-start.11) | collective-permute-done | bytes 32800 | tf_op jit(solution)/shard_map/ppermute | solution.py:370
  150.8 0.6 reshape.158
  151.4 0.0 all-to-all-done.1
  151.4 0.3 copy.35
  151.8 0.0 copy-start.5
  151.8 0.8 copy-done.5
  152.7 0.7 multiply_convert_fusion
  153.4 0.7 convert_element_type.22
  (21 shorter events, 0.7 us)
Async XLA Ops:
  0.6 22.5 %collective-permute-start = (f32[2,4,1024]{2,1,0:T(4,128)}, f32[2,4,1024]{2,1,0:T(4,128)S(1)}, u32[]{:S(2)}, u32[]{:S(2)}) collective-permute-start(f32[2,4,1024]{2,1,0:T(4,128)} %param.12), channel_id=1, source_target_pairs={{0,256},{1,0},{2,384},{3,128},{4,320},{5,64},{6,448},{7,192},{8,28... | collective-permute-start | bytes 98312 | tf_op jit(solution)/shard_map/ppermute | solution.py:307
  17.9 11.9 %collective-permute-start.1 = (f32[2,4,1024]{2,1,0:T(4,128)}, f32[2,4,1024]{2,1,0:T(4,128)S(1)}, u32[]{:S(2)}, u32[]{:S(2)}) collective-permute-start(f32[2,4,1024]{2,1,0:T(4,128)} %param.12), channel_id=1, source_target_pairs={{0,0},{1,256},{2,128},{3,384},{4,64},{5,320},{6,192},{7,448},{8,32... | collective-permute-start | bytes 98312 | tf_op jit(solution)/shard_map/ppermute | solution.py:307
  29.8 15.2 %collective-permute-start.2 = (f32[2,2,2,1024]{3,2,1,0:T(2,128)S(1)}, f32[2,2,2,1024]{3,2,1,0:T(2,128)S(1)}, u32[]{:S(2)}, u32[]{:S(2)}) collective-permute-start(f32[2,2,2,1024]{3,2,1,0:T(2,128)S(1)} %pad_maximum_fusion.5), channel_id=1, source_target_pairs={{0,1},{1,0},{2,3},{3,2},{4,5},{5,4},{6,7},{7,6},{8,9},{9,8},{10,11... | collective-permute-start | bytes 98312 | tf_op jit(solution)/shard_map/ppermute | solution.py:311
  34.1 51.2 %all-to-all-start = ((f32[32,1,6144]{2,1,0:T(1,128)}), f32[32,1,6144]{2,1,0:T(1,128)S(1)}, u32[]{:S(2)}, u32[]{:S(2)}) async-start(f32[32,1,6144]{2,1,0:T(1,128)} %pack.1), calls=%async_computation | async-start | bytes 1572864 | tf_op jit(solution)/shard_map/all_to_all | solution.py:299
  45.1 6.9 %collective-permute-start.3 = (f32[2,2,4096]{2,1,0:T(2,128)S(1)}, f32[2,2,4096]{2,1,0:T(2,128)S(1)}, u32[]{:S(2)}, u32[]{:S(2)}) collective-permute-start(f32[2,2,4096]{2,1,0:T(2,128)S(1)} %pad_maximum_fusion.4), channel_id=1, source_target_pairs={{0,128},{64,192},{128,0},{192,64},{1,129},{65,193},{129,1},{193,65... | collective-permute-start | bytes 196616 | tf_op jit(solution)/shard_map/ppermute | solution.py:265
  52.1 7.2 %collective-permute-start.4 = (f32[2,4,4096]{2,1,0:T(4,128)S(1)}, f32[2,4,4096]{2,1,0:T(4,128)S(1)}, u32[]{:S(2)}, u32[]{:S(2)}) collective-permute-start(f32[2,4,4096]{2,1,0:T(4,128)S(1)} %pad_maximum_fusion.3), channel_id=1, source_target_pairs={{0,64},{64,0},{128,192},{192,128},{1,65},{65,1},{129,193},{193,129... | collective-permute-start | bytes 393224 | tf_op jit(solution)/shard_map/ppermute | solution.py:265
  59.4 3.3 %copy-start = (f32[2,32,256]{2,1,0:T(8,128)S(1)}, f32[2,32,256]{2,1,0:T(8,128)}, u32[]{:S(2)}) copy-start(f32[2,32,256]{2,1,0:T(8,128)} %constant.57.clone.coarse_ref) | copy-start | bytes 196612
  59.4 3.3 %copy-start.1 = (f32[2,32,256]{2,1,0:T(8,128)S(1)}, f32[2,32,256]{2,1,0:T(8,128)}, u32[]{:S(2)}) copy-start(f32[2,32,256]{2,1,0:T(8,128)} %constant.58.clone.fine_ref) | copy-start | bytes 196612
  60.2 29.3 %collective-permute-start.5 = (f32[2,8,4096]{2,1,0:T(8,128)}, f32[2,8,4096]{2,1,0:T(8,128)}, u32[]{:S(2)}, u32[]{:S(2)}) collective-permute-start(f32[2,8,4096]{2,1,0:T(8,128)} %pad_maximum_fusion.1), channel_id=1, source_target_pairs={{0,32},{32,0},{1,33},{33,1},{2,34},{34,2},{3,35},{35,3},{4,36},{36... | collective-permute-start | bytes 786440 | tf_op jit(solution)/shard_map/ppermute | solution.py:265
  63.4 22.2 %copy-start.2 = (f32[2,32,1024]{2,1,0:T(8,128)S(1)}, f32[2,32,1024]{2,1,0:T(8,128)}, u32[]{:S(2)}) copy-start(f32[2,32,1024]{2,1,0:T(8,128)} %constant.61.clone.twiddle_ref) | copy-start | bytes 786436
  63.4 22.2 %copy-start.4 = (bf16[64,96]{1,0:T(8,128)(2,1)S(1)}, bf16[64,96]{1,0:T(8,128)(2,1)}, u32[]{:S(2)}) copy-start(bf16[64,96]{1,0:T(8,128)(2,1)} %constant.59.clone.small_ref) | copy-start | bytes 36868
  87.6 3.4 %collective-permute-start.6 = (f32[2,8,4096]{2,1,0:T(8,128)S(1)}, f32[2,8,4096]{2,1,0:T(8,128)S(1)}, u32[]{:S(2)}, u32[]{:S(2)}) collective-permute-start(f32[2,8,4096]{2,1,0:T(8,128)S(1)} %get-tuple-element.16), channel_id=1, source_target_pairs={{0,32},{32,0},{1,33},{33,1},{2,34},{34,2},{3,35},{35,3},{4,36},{36... | collective-permute-start | bytes 786440 | tf_op jit(solution)/shard_map/ppermute | solution.py:341
  91.1 6.8 %collective-permute-start.7 = (f32[8,4096]{1,0:T(8,128)S(1)}, f32[8,4096]{1,0:T(8,128)S(1)}, u32[]{:S(2)}, u32[]{:S(2)}) collective-permute-start(f32[8,4096]{1,0:T(8,128)S(1)} %get-tuple-element.22), channel_id=1, source_target_pairs={{0,1},{1,0},{2,3},{3,2},{4,5},{5,4},{6,7},{7,6},{8,9},{9,8},{10,11... | collective-permute-start | bytes 393224 | tf_op jit(solution)/shard_map/ppermute | solution.py:343
  97.9 2.0 %copy-start.3 = (bf16[32,192]{1,0:T(8,128)(2,1)S(1)}, bf16[32,192]{1,0:T(8,128)(2,1)}, u32[]{:S(2)}) copy-start(bf16[32,192]{1,0:T(8,128)(2,1)} %constant.60.clone.small_ref) | copy-start | bytes 36868
  98.0 5.7 %collective-permute-start.8 = (f32[2,4,4096]{2,1,0:T(4,128)S(1)}, f32[2,4,4096]{2,1,0:T(4,128)S(1)}, u32[]{:S(2)}, u32[]{:S(2)}) collective-permute-start(f32[2,4,4096]{2,1,0:T(4,128)S(1)} %broadcast_select_fusion.6), channel_id=1, source_target_pairs={{0,64},{64,0},{128,192},{192,128},{1,65},{65,1},{129,193},{193,129... | collective-permute-start | bytes 393224 | tf_op jit(solution)/shard_map/ppermute | solution.py:261
  103.8 10.5 %collective-permute-start.9 = (f32[2,2,4096]{2,1,0:T(2,128)S(1)}, f32[2,2,4096]{2,1,0:T(2,128)S(1)}, u32[]{:S(2)}, u32[]{:S(2)}) collective-permute-start(f32[2,2,4096]{2,1,0:T(2,128)S(1)} %broadcast_select_fusion.3), channel_id=1, source_target_pairs={{0,128},{64,192},{128,0},{192,64},{1,129},{65,193},{129,1},{193,65... | collective-permute-start | bytes 196616 | tf_op jit(solution)/shard_map/ppermute | solution.py:261
  108.6 42.8 %all-to-all-start.1 = ((f32[32,1,4096]{2,1,0:T(1,128)}), f32[32,1,4096]{2,1,0:T(1,128)S(1)}, u32[]{:S(2)}, u32[]{:S(2)}) async-start(f32[32,1,4096]{2,1,0:T(1,128)} %back.1), calls=%async_computation.1 | async-start | bytes 1048576 | tf_op jit(solution)/shard_map/all_to_all | solution.py:364
  114.5 24.3 %collective-permute-start.10 = (f32[2,4096]{1,0:T(2,128)S(1)}, f32[2,4096]{1,0:T(2,128)S(1)}, u32[]{:S(2)}, u32[]{:S(2)}) collective-permute-start(f32[2,4096]{1,0:T(2,128)S(1)} %fusion.2), channel_id=1, source_target_pairs={{0,0},{256,1},{128,2},{384,3},{64,4},{320,5},{192,6},{448,7},{32,8... | collective-permute-start | bytes 98312 | tf_op jit(solution)/shard_map/ppermute | solution.py:370
  126.9 23.8 %collective-permute-start.11 = (f32[2,4096]{1,0:T(2,128)S(1)}, f32[2,4096]{1,0:T(2,128)S(1)}, u32[]{:S(2)}, u32[]{:S(2)}) collective-permute-start(f32[2,4096]{1,0:T(2,128)S(1)} %bitcast.35), channel_id=1, source_target_pairs={{256,0},{0,1},{384,2},{128,3},{320,4},{64,5},{448,6},{192,7},{288,... | collective-permute-start | bytes 98312 | tf_op jit(solution)/shard_map/ppermute | solution.py:370
  151.8 0.9 copy-start.5

commit v8 on v7

--- a/solution.py
+++ b/solution.py
@@ -1,3 +1,4 @@
+import functools
 import math
 
 import jax
@@ -130,6 +131,23 @@
             for channel in range(2):
                 at = (2 * source + channel) * points + start
                 packed_ref[:, 0, at : at + 128] = rows_ref[slot, pl.ds(channel, count, stride=2), :]
+
+
+def finish_kernel(scale, returned_ref, out_ref, input_grad_ref, gate_grad_ref, rows_ref):
+    points = out_ref.shape[2]
+    count = returned_ref.shape[0]
+    for source in range(2):
+        for start in range(0, points, 128):
+            cut = slice(start, start + 128)
+            slot = source * (points // 128) + start // 128
+            for channel in range(2):
+                at = (2 * source + channel) * points + start
+                rows_ref[slot, pl.ds(channel, count, stride=2), :] = returned_ref[:, 0, at : at + 128]
+            values = rows_ref[slot] * scale
+            if source == 0:
+                gate_grad_ref[0, :, cut] = (out_ref[0, :, cut].astype(f32) * values).astype(bf16)
+            else:
+                input_grad_ref[0, :, cut] = values.astype(bf16)
 
 
 def forward_kernel(
@@ -339,11 +357,10 @@
     )(core_flag, moved, small_out, twiddle, *tables)
 
     total = kept + lax.ppermute(away, "core", cores)
+    total = halving(total, x_index % 2 == 1, "x", near_x)
+    total = halving(total, x_index >= 2, "x", far_x)
     mine = jnp.where(odd, total[1], total[0])
     other = lax.ppermute(jnp.where(odd, total[0], total[1]), "y", near_y)
-    total = jnp.stack([mine, other])
-    total = halving(total, x_index % 2 == 1, "x", near_x)
-    total = halving(total, x_index >= 2, "x", far_x)
 
     conv = pl.pallas_call(
         conv_kernel,
@@ -362,9 +379,8 @@
         cost_estimate=cost,
     )(conv, spec, filters, small_back, twiddle, *tables)
     returned = lax.all_to_all(signals, SEQ, split_axis=0, concat_axis=0, tiled=True)
-    returned = returned.reshape(seq_count, 4 * positions)
-
-    ordered = jnp.where(odd, total[::-1], total)
+
+    ordered = jnp.stack([jnp.where(odd, other, mine), jnp.where(odd, mine, other)])
     rows_out = [jnp.where(upper_zhi, ordered[:, 1 - n], ordered[:, n]) for n in range(2)]
     ends = [
         lax.ppermute(rows_out[number], everyone, [(b, a) for a, b in pairs[number]])
@@ -378,10 +394,15 @@
     )
 
     scale = 1.0 / math.sqrt(seq_count * positions)
-    conv = returned[:, : per_seq * positions].reshape(1, channels, positions) * scale
-    backward = returned[:, per_seq * positions :].reshape(1, channels, positions) * scale
-    grad_gate = (grad_out.astype(f32) * conv).astype(bf16)
-    return (backward.astype(bf16), grad_gate, grad_filter)
+    grad_input, grad_gate = pl.pallas_call(
+        functools.partial(finish_kernel, scale),
+        out_shape=[jax.ShapeDtypeStruct((1, channels, positions), bf16)] * 2,
+        scratch_shapes=[pltpu.VMEM((2 * positions // 128, channels, 128), f32)],
+        name="finish",
+        compiler_params=params,
+        cost_estimate=pl.CostEstimate(flops=10**5, bytes_accessed=2 * 10**6, transcendentals=0),
+    )(returned, grad_out)
+    return (grad_input, grad_gate, grad_filter)
 
 
 def solution(mesh):

time: 155 us -> 154 us (level)
  local copies, waits for them, and re-layouts: 2.99 us -> 1.1 us
    ppermute x2, waiting for transfers between devices: 1.73 us -> 7.37 us  [halving(): return kept + lax.ppermute(away, axis, pairs)]
    ppermute x1, waiting for transfers between devices: 4.82 us -> 0.01 us  [step(): other = lax.ppermute(jnp.where(odd, total[0], total[1]), 'y', near_y)]
  transfers between devices with their start and end apart: 14 -> 14, of which waited for: 9 -> 9; matrix products, arithmetic and copies ran while one was open for 2% -> 2% of each run, Pallas kernels for 6% -> 7%
where the time goes in v8:
time: 154 us
  starting transfers between devices  69.6 us (45%)
  waiting for transfers between devices  68.1 us (44%)
  Pallas kernels  11.1 us (7%)
  other arithmetic  2.57 us (2%)
    ppermute x2, starting transfers between devices, step(): lax.ppermute(filter_spectrum, everyone, pairs[number])  22.4 us
    all_to_all x1, waiting for transfers between devices, step(): moved = lax.all_to_all(packed, SEQ, split_axis=0, concat_axis=0, tiled=True)  21.9 us
    ppermute x2, waiting for transfers between devices, step(): lax.ppermute(rows_out[number], everyone, [(b, a) for a, b in pairs[number]])  21.5 us
    ppermute x2, starting transfers between devices, step(): lax.ppermute(rows_out[number], everyone, [(b, a) for a, b in pairs[number]])  13.9 us
    all_to_all x1, starting transfers between devices, step(): moved = lax.all_to_all(packed, SEQ, split_axis=0, concat_axis=0, tiled=True)  10.8 us
    ppermute x3, waiting for transfers between devices, doubling(): other = lax.ppermute(values, axis, pairs)  10.2 us
    ppermute x2, waiting for transfers between devices, halving(): return kept + lax.ppermute(away, axis, pairs)  7.37 us
    ppermute x2, waiting for transfers between devices, step(): lax.ppermute(filter_spectrum, everyone, pairs[number])  6.61 us
  transfers between devices with their start and end apart: 14, of which 9 were waited for; matrix products, arithmetic and copies ran while one was open for 2% of the time, Pallas kernels for 7%

profile of v8, /device:TPU:7, one launch (start us, length us, event | category | flops | bytes accessed | tf_op | source)
XLA Modules:
  0.0 153.5 jit_solution(9947830817963060751)
XLA Ops:
  0.6 17.2 %collective-permute-start = (f32[2,4,1024]{2,1,0:T(4,128)}, f32[2,4,1024]{2,1,0:T(4,128)S(1)}, u32[]{:S(2)}, u32[]{:S(2)}) collective-permute-start(f32[2,4,1024]{2,1,0:T(4,128)} %param.12), channel_id=1, source_target_pairs={{0,256},{1,0},{2,384},{3,128},{4,320},{5,64},{6,448},{7,192},{8,28... | collective-permute-start | bytes 98312 | tf_op jit(solution)/shard_map/ppermute | solution.py:325
  17.9 5.2 %collective-permute-start.1 = (f32[2,4,1024]{2,1,0:T(4,128)}, f32[2,4,1024]{2,1,0:T(4,128)S(1)}, u32[]{:S(2)}, u32[]{:S(2)}) collective-permute-start(f32[2,4,1024]{2,1,0:T(4,128)} %param.12), channel_id=1, source_target_pairs={{0,0},{1,256},{2,128},{3,384},{4,64},{5,320},{6,192},{7,448},{8,32... | collective-permute-start | bytes 98312 | tf_op jit(solution)/shard_map/ppermute | solution.py:325
  23.1 0.0 collective-permute-done
  23.1 6.6 %collective-permute-done.1 = f32[2,4,1024]{2,1,0:T(4,128)S(1)} collective-permute-done((f32[2,4,1024]{2,1,0:T(4,128)}, f32[2,4,1024]{2,1,0:T(4,128)S(1)}, u32[]{:S(2)}, u32[]{:S(2)}) %collective-permute-start.1) | collective-permute-done | bytes 32800 | tf_op jit(solution)/shard_map/ppermute | solution.py:325
  29.8 1.9 %collective-permute-start.2 = (f32[2,2,2,1024]{3,2,1,0:T(2,128)S(1)}, f32[2,2,2,1024]{3,2,1,0:T(2,128)S(1)}, u32[]{:S(2)}, u32[]{:S(2)}) collective-permute-start(f32[2,2,2,1024]{3,2,1,0:T(2,128)S(1)} %pad_maximum_fusion.5), channel_id=1, source_target_pairs={{0,1},{1,0},{2,3},{3,2},{4,5},{5,4},{6,7},{7,6},{8,9},{9,8},{10,11... | collective-permute-start | bytes 98312 | tf_op jit(solution)/shard_map/ppermute | solution.py:329
  31.7 2.4 %pack.1 = f32[32,1,6144]{2,1,0:T(1,128)} custom-call(bf16[1,64,1024]{2,1,0:T(8,128)(2,1)} %out_ref.1, bf16[1,64,1024]{2,1,0:T(8,128)(2,1)} %gate_hbm.1, f32[1,2,64,1024]{3,2,1,0:T(8,128)} %spec_hbm.1), custom_call_target="tpu_custom_call" | custom-call | flops 100000 | bytes 2000000 | tf_op jit(solution)/shard_map/pack/pallas_call | solution.py:302
  34.1 10.8 %all-to-all-start = ((f32[32,1,6144]{2,1,0:T(1,128)}), f32[32,1,6144]{2,1,0:T(1,128)S(1)}, u32[]{:S(2)}, u32[]{:S(2)}) async-start(f32[32,1,6144]{2,1,0:T(1,128)} %pack.1), calls=%async_computation | async-start | bytes 1572864 | tf_op jit(solution)/shard_map/all_to_all | solution.py:317
  45.0 0.0 collective-permute-done.2
  45.1 1.9 %collective-permute-start.3 = (f32[2,2,4096]{2,1,0:T(2,128)S(1)}, f32[2,2,4096]{2,1,0:T(2,128)S(1)}, u32[]{:S(2)}, u32[]{:S(2)}) collective-permute-start(f32[2,2,4096]{2,1,0:T(2,128)S(1)} %pad_maximum_fusion.3), channel_id=1, source_target_pairs={{0,128},{64,192},{128,0},{192,64},{1,129},{65,193},{129,1},{193,65... | collective-permute-start | bytes 196616 | tf_op jit(solution)/shard_map/ppermute | solution.py:283
  47.1 4.9 %collective-permute-done.3 = f32[2,2,4096]{2,1,0:T(2,128)S(1)} collective-permute-done((f32[2,2,4096]{2,1,0:T(2,128)S(1)}, f32[2,2,4096]{2,1,0:T(2,128)S(1)}, u32[]{:S(2)}, u32[]{:S(2)}) %collective-permute-start.3) | collective-permute-done | bytes 65568 | tf_op jit(solution)/shard_map/ppermute | solution.py:283
  52.0 0.1 broadcast_select_fusion.5
  52.1 0.1 pad_maximum_fusion.2
  52.1 1.9 %collective-permute-start.4 = (f32[2,4,4096]{2,1,0:T(4,128)S(1)}, f32[2,4,4096]{2,1,0:T(4,128)S(1)}, u32[]{:S(2)}, u32[]{:S(2)}) collective-permute-start(f32[2,4,4096]{2,1,0:T(4,128)S(1)} %pad_maximum_fusion.2), channel_id=1, source_target_pairs={{0,64},{64,0},{128,192},{192,128},{1,65},{65,1},{129,193},{193,129... | collective-permute-start | bytes 393224 | tf_op jit(solution)/shard_map/ppermute | solution.py:283
  54.1 5.3 %collective-permute-done.4 = f32[2,4,4096]{2,1,0:T(4,128)S(1)} collective-permute-done((f32[2,4,4096]{2,1,0:T(4,128)S(1)}, f32[2,4,4096]{2,1,0:T(4,128)S(1)}, u32[]{:S(2)}, u32[]{:S(2)}) %collective-permute-start.4) | collective-permute-done | bytes 131104 | tf_op jit(solution)/shard_map/ppermute | solution.py:283
  59.3 0.1 broadcast_select_fusion.7
  59.4 0.0 copy-start.1
  59.4 0.0 copy-start.2
  59.4 0.8 pad_maximum_fusion.1
  60.2 2.5 %collective-permute-start.5 = (f32[2,8,4096]{2,1,0:T(8,128)}, f32[2,8,4096]{2,1,0:T(8,128)}, u32[]{:S(2)}, u32[]{:S(2)}) collective-permute-start(f32[2,8,4096]{2,1,0:T(8,128)} %pad_maximum_fusion.1), channel_id=1, source_target_pairs={{0,32},{32,0},{1,33},{33,1},{2,34},{34,2},{3,35},{35,3},{4,36},{36... | collective-permute-start | bytes 786440 | tf_op jit(solution)/shard_map/ppermute | solution.py:283
  62.7 0.0 copy-done.1
  62.8 0.0 copy-done.2
  62.8 0.6 root_tables.1
  63.4 0.0 copy-start.3
  63.4 0.0 copy-start.5
  63.4 21.9 %all-to-all-done = f32[32,1,6144]{2,1,0:T(1,128)S(1)} async-done(((f32[32,1,6144]{2,1,0:T(1,128)}), f32[32,1,6144]{2,1,0:T(1,128)S(1)}, u32[]{:S(2)}, u32[]{:S(2)}) %all-to-all-start) | async-done | bytes 786464 | tf_op jit(solution)/shard_map/all_to_all | solution.py:317
  85.3 0.2 copy.32
  85.6 0.0 copy-done.3
  85.6 0.0 copy-done.5
  85.6 2.0 %forward.1 = (f32[32,4096]{1,0:T(8,128)S(1)}, f32[2,8,4096]{2,1,0:T(8,128)S(1)}, f32[2,8,4096]{2,1,0:T(8,128)S(1)}) custom-call(s32[1]{0:T(128)} %bitcast.3.core_ref, f32[32,6144]{1,0:T(8,128)S(1)} %bitcast.32, bf16[64,96]{1,0:T(8,128)(2,1)S(1)} %copy-done.5, f32[2,32,1024]{2,1,0:T(8,128)S(1)} %copy-done.3, bf16[1024,256]{1,0:T(8,128)(2,1)S(1)} %get-tuple-element.12.cos_hi, ...), custom_call_target="tpu_custom_call" | custom-call | flops 2000000000 | bytes 10000000 | tf_op jit(solution)/shard_map/forward/pallas_call | solution.py:349
  87.6 1.9 %collective-permute-start.6 = (f32[2,8,4096]{2,1,0:T(8,128)S(1)}, f32[2,8,4096]{2,1,0:T(8,128)S(1)}, u32[]{:S(2)}, u32[]{:S(2)}) collective-permute-start(f32[2,8,4096]{2,1,0:T(8,128)S(1)} %get-tuple-element.20), channel_id=1, source_target_pairs={{0,32},{32,0},{1,33},{33,1},{2,34},{34,2},{3,35},{35,3},{4,36},{36... | collective-permute-start | bytes 786440 | tf_op jit(solution)/shard_map/ppermute | solution.py:359
  89.6 0.0 collective-permute-done.5
  89.6 1.0 broadcast_select_fusion.1
  90.6 0.5 collective-permute-done.6
  91.1 1.9 %collective-permute-start.7 = (f32[2,4,4096]{2,1,0:T(4,128)S(1)}, f32[2,4,4096]{2,1,0:T(4,128)S(1)}, u32[]{:S(2)}, u32[]{:S(2)}) collective-permute-start(f32[2,4,4096]{2,1,0:T(4,128)S(1)} %slice_select_fusion), channel_id=1, source_target_pairs={{0,64},{64,0},{128,192},{192,128},{1,65},{65,1},{129,193},{193,129... | collective-permute-start | bytes 393224 | tf_op jit(solution)/shard_map/ppermute | solution.py:279
  93.1 4.8 %collective-permute-done.7 = f32[2,4,4096]{2,1,0:T(4,128)S(1)} collective-permute-done((f32[2,4,4096]{2,1,0:T(4,128)S(1)}, f32[2,4,4096]{2,1,0:T(4,128)S(1)}, u32[]{:S(2)}, u32[]{:S(2)}) %collective-permute-start.7) | collective-permute-done | bytes 131104 | tf_op jit(solution)/shard_map/ppermute | solution.py:279
  98.0 0.0 copy-start.4
  98.1 1.9 %collective-permute-start.8 = (f32[2,2,4096]{2,1,0:T(2,128)S(1)}, f32[2,2,4096]{2,1,0:T(2,128)S(1)}, u32[]{:S(2)}, u32[]{:S(2)}) collective-permute-start(f32[2,2,4096]{2,1,0:T(2,128)S(1)} %broadcast_select_fusion.3), channel_id=1, source_target_pairs={{0,128},{64,192},{128,0},{192,64},{1,129},{65,193},{129,1},{193,65... | collective-permute-start | bytes 196616 | tf_op jit(solution)/shard_map/ppermute | solution.py:279
  100.0 0.0 copy-done.4
  100.0 2.1 %conv.1.conv_ref = f32[32,2048]{1,0:T(8,128)S(1)} custom-call(f32[32,6144]{1,0:T(8,128)S(1)} %bitcast.33, f32[32,4096]{1,0:T(8,128)S(1)} %bitcast.34, bf16[32,192]{1,0:T(8,128)(2,1)S(1)} %copy-done.4, f32[2,32,1024]{2,1,0:T(8,128)S(1)} %copy-done.3, bf16[1024,256]{1,0:T(8,128)(2,1)S(1)} %get-tuple-element.12.cos_hi, ...), custom_call_target="tpu_custom_call" | custom-call | flops 2000000000 | bytes 10000000 | tf_op jit(solution)/shard_map/conv/pallas_call | solution.py:365
  102.1 2.5 %collective-permute-done.8 = f32[2,2,4096]{2,1,0:T(2,128)S(1)} collective-permute-done((f32[2,2,4096]{2,1,0:T(2,128)S(1)}, f32[2,2,4096]{2,1,0:T(2,128)S(1)}, u32[]{:S(2)}, u32[]{:S(2)}) %collective-permute-start.8) | collective-permute-done | bytes 65568 | tf_op jit(solution)/shard_map/ppermute | solution.py:279
  104.6 0.1 select_add_fusion.1
  104.7 1.9 %collective-permute-start.9 = (f32[2,4096]{1,0:T(2,128)S(1)}, f32[2,4096]{1,0:T(2,128)S(1)}, u32[]{:S(2)}, u32[]{:S(2)}) collective-permute-start(f32[2,4096]{1,0:T(2,128)S(1)} %select_bitcast_fusion), channel_id=1, source_target_pairs={{0,1},{1,0},{2,3},{3,2},{4,5},{5,4},{6,7},{7,6},{8,9},{9,8},{10,11... | collective-permute-start | bytes 98312 | tf_op jit(solution)/shard_map/ppermute | solution.py:363
  106.6 2.9 %back.1 = f32[32,1,4096]{2,1,0:T(1,128)} custom-call(f32[32,2048]{1,0:T(8,128)S(1)} %conv.1.conv_ref, f32[32,4096]{1,0:T(8,128)S(1)} %get-tuple-element.16.spec_ref, f32[32,4096]{1,0:T(8,128)S(1)} %bitcast.35, bf16[32,192]{1,0:T(8,128)(2,1)S(1)} %copy-done.4, f32[2,32,1024]{2,1,0:T(8,128)S(1)} %copy-done.3, bf16[1024,256]{1,0:T(8,128)(2,1)S(1)} %get-tuple-element.12.cos_hi, ...), custom_call_target="tpu_custom_call" | custom-call | flops 2000000000 | bytes 10000000 | tf_op jit(solution)/shard_map/back/pallas_call | solution.py:373
  109.5 6.6 %all-to-all-start.1 = ((f32[32,1,4096]{2,1,0:T(1,128)}), f32[32,1,4096]{2,1,0:T(1,128)S(1)}, u32[]{:S(2)}, u32[]{:S(2)}) async-start(f32[32,1,4096]{2,1,0:T(1,128)} %back.1), calls=%async_computation.1 | async-start | bytes 1048576 | tf_op jit(solution)/shard_map/all_to_all | solution.py:381
  116.1 0.0 collective-permute-done.9
  116.1 0.1 broadcast_select_fusion.2
  116.3 9.3 %collective-permute-start.10 = (f32[2,4096]{1,0:T(2,128)S(1)}, f32[2,4096]{1,0:T(2,128)S(1)}, u32[]{:S(2)}, u32[]{:S(2)}) collective-permute-start(f32[2,4096]{1,0:T(2,128)S(1)} %fusion.1), channel_id=1, source_target_pairs={{0,0},{256,1},{128,2},{384,3},{64,4},{320,5},{192,6},{448,7},{32,8... | collective-permute-start | bytes 98312 | tf_op jit(solution)/shard_map/ppermute | solution.py:386
  125.6 0.0 copy-start
  125.6 4.5 %collective-permute-start.11 = (f32[2,4096]{1,0:T(2,128)S(1)}, f32[2,4096]{1,0:T(2,128)S(1)}, u32[]{:S(2)}, u32[]{:S(2)}) collective-permute-start(f32[2,4096]{1,0:T(2,128)S(1)} %bitcast.39), channel_id=1, source_target_pairs={{256,0},{0,1},{384,2},{128,3},{320,4},{64,5},{448,6},{192,7},{288,... | collective-permute-start | bytes 98312 | tf_op jit(solution)/shard_map/ppermute | solution.py:386
  130.2 7.1 %collective-permute-done.10 = f32[2,4096]{1,0:T(2,128)S(1)} collective-permute-done((f32[2,4096]{1,0:T(2,128)S(1)}, f32[2,4096]{1,0:T(2,128)S(1)}, u32[]{:S(2)}, u32[]{:S(2)}) %collective-permute-start.10) | collective-permute-done | bytes 32800 | tf_op jit(solution)/shard_map/ppermute | solution.py:386
  137.3 14.4 %collective-permute-done.11 = f32[2,4096]{1,0:T(2,128)S(1)} collective-permute-done((f32[2,4096]{1,0:T(2,128)S(1)}, f32[2,4096]{1,0:T(2,128)S(1)}, u32[]{:S(2)}, u32[]{:S(2)}) %collective-permute-start.11) | collective-permute-done | bytes 32800 | tf_op jit(solution)/shard_map/ppermute | solution.py:386
  151.8 0.6 reshape.121
  152.4 0.0 all-to-all-done.1.returned_ref
  152.4 0.0 copy-done
  152.4 1.1 finish.1
  (20 shorter events, 0.6 us)
Async XLA Ops:
  0.6 22.5 %collective-permute-start = (f32[2,4,1024]{2,1,0:T(4,128)}, f32[2,4,1024]{2,1,0:T(4,128)S(1)}, u32[]{:S(2)}, u32[]{:S(2)}) collective-permute-start(f32[2,4,1024]{2,1,0:T(4,128)} %param.12), channel_id=1, source_target_pairs={{0,256},{1,0},{2,384},{3,128},{4,320},{5,64},{6,448},{7,192},{8,28... | collective-permute-start | bytes 98312 | tf_op jit(solution)/shard_map/ppermute | solution.py:325
  17.9 11.9 %collective-permute-start.1 = (f32[2,4,1024]{2,1,0:T(4,128)}, f32[2,4,1024]{2,1,0:T(4,128)S(1)}, u32[]{:S(2)}, u32[]{:S(2)}) collective-permute-start(f32[2,4,1024]{2,1,0:T(4,128)} %param.12), channel_id=1, source_target_pairs={{0,0},{1,256},{2,128},{3,384},{4,64},{5,320},{6,192},{7,448},{8,32... | collective-permute-start | bytes 98312 | tf_op jit(solution)/shard_map/ppermute | solution.py:325
  29.8 15.2 %collective-permute-start.2 = (f32[2,2,2,1024]{3,2,1,0:T(2,128)S(1)}, f32[2,2,2,1024]{3,2,1,0:T(2,128)S(1)}, u32[]{:S(2)}, u32[]{:S(2)}) collective-permute-start(f32[2,2,2,1024]{3,2,1,0:T(2,128)S(1)} %pad_maximum_fusion.5), channel_id=1, source_target_pairs={{0,1},{1,0},{2,3},{3,2},{4,5},{5,4},{6,7},{7,6},{8,9},{9,8},{10,11... | collective-permute-start | bytes 98312 | tf_op jit(solution)/shard_map/ppermute | solution.py:329
  34.1 51.2 %all-to-all-start = ((f32[32,1,6144]{2,1,0:T(1,128)}), f32[32,1,6144]{2,1,0:T(1,128)S(1)}, u32[]{:S(2)}, u32[]{:S(2)}) async-start(f32[32,1,6144]{2,1,0:T(1,128)} %pack.1), calls=%async_computation | async-start | bytes 1572864 | tf_op jit(solution)/shard_map/all_to_all | solution.py:317
  45.1 6.9 %collective-permute-start.3 = (f32[2,2,4096]{2,1,0:T(2,128)S(1)}, f32[2,2,4096]{2,1,0:T(2,128)S(1)}, u32[]{:S(2)}, u32[]{:S(2)}) collective-permute-start(f32[2,2,4096]{2,1,0:T(2,128)S(1)} %pad_maximum_fusion.3), channel_id=1, source_target_pairs={{0,128},{64,192},{128,0},{192,64},{1,129},{65,193},{129,1},{193,65... | collective-permute-start | bytes 196616 | tf_op jit(solution)/shard_map/ppermute | solution.py:283
  52.1 7.2 %collective-permute-start.4 = (f32[2,4,4096]{2,1,0:T(4,128)S(1)}, f32[2,4,4096]{2,1,0:T(4,128)S(1)}, u32[]{:S(2)}, u32[]{:S(2)}) collective-permute-start(f32[2,4,4096]{2,1,0:T(4,128)S(1)} %pad_maximum_fusion.2), channel_id=1, source_target_pairs={{0,64},{64,0},{128,192},{192,128},{1,65},{65,1},{129,193},{193,129... | collective-permute-start | bytes 393224 | tf_op jit(solution)/shard_map/ppermute | solution.py:283
  59.4 3.3 %copy-start.1 = (f32[2,32,256]{2,1,0:T(8,128)S(1)}, f32[2,32,256]{2,1,0:T(8,128)}, u32[]{:S(2)}) copy-start(f32[2,32,256]{2,1,0:T(8,128)} %constant.55.clone.coarse_ref) | copy-start | bytes 196612
  59.4 3.3 %copy-start.2 = (f32[2,32,256]{2,1,0:T(8,128)S(1)}, f32[2,32,256]{2,1,0:T(8,128)}, u32[]{:S(2)}) copy-start(f32[2,32,256]{2,1,0:T(8,128)} %constant.56.clone.fine_ref) | copy-start | bytes 196612
  60.2 29.3 %collective-permute-start.5 = (f32[2,8,4096]{2,1,0:T(8,128)}, f32[2,8,4096]{2,1,0:T(8,128)}, u32[]{:S(2)}, u32[]{:S(2)}) collective-permute-start(f32[2,8,4096]{2,1,0:T(8,128)} %pad_maximum_fusion.1), channel_id=1, source_target_pairs={{0,32},{32,0},{1,33},{33,1},{2,34},{34,2},{3,35},{35,3},{4,36},{36... | collective-permute-start | bytes 786440 | tf_op jit(solution)/shard_map/ppermute | solution.py:283
  63.4 22.2 %copy-start.3 = (f32[2,32,1024]{2,1,0:T(8,128)S(1)}, f32[2,32,1024]{2,1,0:T(8,128)}, u32[]{:S(2)}) copy-start(f32[2,32,1024]{2,1,0:T(8,128)} %constant.59.clone.twiddle_ref) | copy-start | bytes 786436
  63.4 22.2 %copy-start.5 = (bf16[64,96]{1,0:T(8,128)(2,1)S(1)}, bf16[64,96]{1,0:T(8,128)(2,1)}, u32[]{:S(2)}) copy-start(bf16[64,96]{1,0:T(8,128)(2,1)} %constant.57.clone.small_ref) | copy-start | bytes 36868
  87.6 3.4 %collective-permute-start.6 = (f32[2,8,4096]{2,1,0:T(8,128)S(1)}, f32[2,8,4096]{2,1,0:T(8,128)S(1)}, u32[]{:S(2)}, u32[]{:S(2)}) collective-permute-start(f32[2,8,4096]{2,1,0:T(8,128)S(1)} %get-tuple-element.20), channel_id=1, source_target_pairs={{0,32},{32,0},{1,33},{33,1},{2,34},{34,2},{3,35},{35,3},{4,36},{36... | collective-permute-start | bytes 786440 | tf_op jit(solution)/shard_map/ppermute | solution.py:359
  91.1 6.8 %collective-permute-start.7 = (f32[2,4,4096]{2,1,0:T(4,128)S(1)}, f32[2,4,4096]{2,1,0:T(4,128)S(1)}, u32[]{:S(2)}, u32[]{:S(2)}) collective-permute-start(f32[2,4,4096]{2,1,0:T(4,128)S(1)} %slice_select_fusion), channel_id=1, source_target_pairs={{0,64},{64,0},{128,192},{192,128},{1,65},{65,1},{129,193},{193,129... | collective-permute-start | bytes 393224 | tf_op jit(solution)/shard_map/ppermute | solution.py:279
  98.0 2.0 %copy-start.4 = (bf16[32,192]{1,0:T(8,128)(2,1)S(1)}, bf16[32,192]{1,0:T(8,128)(2,1)}, u32[]{:S(2)}) copy-start(bf16[32,192]{1,0:T(8,128)(2,1)} %constant.58.clone.small_ref) | copy-start | bytes 36868
  98.1 6.5 %collective-permute-start.8 = (f32[2,2,4096]{2,1,0:T(2,128)S(1)}, f32[2,2,4096]{2,1,0:T(2,128)S(1)}, u32[]{:S(2)}, u32[]{:S(2)}) collective-permute-start(f32[2,2,4096]{2,1,0:T(2,128)S(1)} %broadcast_select_fusion.3), channel_id=1, source_target_pairs={{0,128},{64,192},{128,0},{192,64},{1,129},{65,193},{129,1},{193,65... | collective-permute-start | bytes 196616 | tf_op jit(solution)/shard_map/ppermute | solution.py:279
  104.7 11.4 %collective-permute-start.9 = (f32[2,4096]{1,0:T(2,128)S(1)}, f32[2,4096]{1,0:T(2,128)S(1)}, u32[]{:S(2)}, u32[]{:S(2)}) collective-permute-start(f32[2,4096]{1,0:T(2,128)S(1)} %select_bitcast_fusion), channel_id=1, source_target_pairs={{0,1},{1,0},{2,3},{3,2},{4,5},{5,4},{6,7},{7,6},{8,9},{9,8},{10,11... | collective-permute-start | bytes 98312 | tf_op jit(solution)/shard_map/ppermute | solution.py:363
  109.5 42.9 %all-to-all-start.1 = ((f32[32,1,4096]{2,1,0:T(1,128)}), f32[32,1,4096]{2,1,0:T(1,128)S(1)}, u32[]{:S(2)}, u32[]{:S(2)}) async-start(f32[32,1,4096]{2,1,0:T(1,128)} %back.1), calls=%async_computation.1 | async-start | bytes 1048576 | tf_op jit(solution)/shard_map/all_to_all | solution.py:381
  116.3 21.0 %collective-permute-start.10 = (f32[2,4096]{1,0:T(2,128)S(1)}, f32[2,4096]{1,0:T(2,128)S(1)}, u32[]{:S(2)}, u32[]{:S(2)}) collective-permute-start(f32[2,4096]{1,0:T(2,128)S(1)} %fusion.1), channel_id=1, source_target_pairs={{0,0},{256,1},{128,2},{384,3},{64,4},{320,5},{192,6},{448,7},{32,8... | collective-permute-start | bytes 98312 | tf_op jit(solution)/shard_map/ppermute | solution.py:386
  125.6 26.8 %copy-start = (bf16[1,64,1024]{2,1,0:T(8,128)(2,1)S(1)}, bf16[1,64,1024]{2,1,0:T(8,128)(2,1)}, u32[]{:S(2)}) copy-start(bf16[1,64,1024]{2,1,0:T(8,128)(2,1)} %out_ref.1) | copy-start | bytes 393220
  125.6 26.1 %collective-permute-start.11 = (f32[2,4096]{1,0:T(2,128)S(1)}, f32[2,4096]{1,0:T(2,128)S(1)}, u32[]{:S(2)}, u32[]{:S(2)}) collective-permute-start(f32[2,4096]{1,0:T(2,128)S(1)} %bitcast.39), channel_id=1, source_target_pairs={{256,0},{0,1},{384,2},{128,3},{320,4},{64,5},{448,6},{192,7},{288,... | collective-permute-start | bytes 98312 | tf_op jit(solution)/shard_map/ppermute | solution.py:386
